TPU v7x, 256 devices: a whole 4x4x8 slice. The times are simulated.
256 devices in a mesh: blk: 16 (over z, core), red: 16 (over x, y).
Axes of the slice: x: 4, y: 4, z: 8, core: 2. Of those that a mesh axis runs over, the one named last changes fastest.
Arguments:
- amplitudes: bfloat16 [8, 192, 128, 128], P(None, 'blk', 'red'), may hold values from -6 to 6
- ladder_ints: bfloat16 [16384, 16384], P('red', 'blk'), may hold values from -0.046875 to 0.046875
- cycle_ints: bfloat16 [24576, 24576], P('blk', 'red'), may hold values from -0.0390625 to 0.0390625
- occ_energy: float32 [192], replicated, may hold values from -2 to -0.3
- vir_energy: float32 [128], replicated, may hold values from 0.2 to 3
- slab_index: int32 [8], replicated, may hold values from 0 to 191
Outputs:
- update: float32 [8, 192, 128, 128], P(None, 'red', 'blk')
All inputs are finite; a program needn't handle non-finite values.
Results may differ from a plain program's by a relative error of at most 0.0003.
Values may be sent and summed in bfloat16 or wider, within the bound.
A program may use at most 64 MiB of HBM per device.

v0:
```python
import jax
import jax.numpy as jnp
from jax import lax
from jax.sharding import PartitionSpec as P


def shards(amplitudes, ladder_ints, cycle_ints, occ_energy, vir_energy, slab_index):
    slab_rows, occ_local, vir_local, virt_width = amplitudes.shape
    occ_all = occ_local * lax.axis_size("blk")
    occ_red = occ_all // lax.axis_size("red")
    shard_piece = lax.all_gather(amplitudes, "blk", axis=1, tiled=True)
    row_count = shard_piece.shape[1]
    flattened = shard_piece.reshape(slab_rows * row_count, vir_local * virt_width)
    product = jnp.dot(flattened, ladder_ints, preferred_element_type=jnp.float32)
    ladder = product.reshape(slab_rows, row_count, ladder_ints.shape[1])
    ladder_own = lax.psum_scatter(ladder, "red", scatter_dimension=1, tiled=True)
    ladder_own = ladder_own.reshape(slab_rows, occ_red, -1, virt_width)
    shard_piece = lax.all_gather(amplitudes, "red", axis=2, tiled=True)
    vir_count = shard_piece.shape[2]
    operand = jnp.transpose(shard_piece, (0, 2, 1, 3)).reshape(
        slab_rows * vir_count, occ_local * virt_width
    )
    product = jnp.dot(operand, cycle_ints, preferred_element_type=jnp.float32)
    cycle_term = product.reshape(slab_rows, vir_count, cycle_ints.shape[1])
    cycle_own = lax.psum_scatter(cycle_term, "blk", scatter_dimension=1, tiled=True)
    vir_block = cycle_own.shape[1]
    cycle_own = jnp.transpose(
        cycle_own.reshape(slab_rows, vir_block, occ_red, virt_width), (0, 2, 1, 3)
    )
    orbital_ids = jnp.arange(occ_energy.shape[0], dtype=jnp.int32)
    chosen = slab_index[:, None] == orbital_ids[None, :]
    slab_energy = jnp.sum(jnp.where(chosen, occ_energy[None, :], jnp.float32(0.0)), axis=1)
    pair_energy = lax.dynamic_slice_in_dim(occ_energy, lax.axis_index("red") * occ_red, occ_red)
    first_virtual = lax.dynamic_slice_in_dim(
        vir_energy, lax.axis_index("blk") * vir_block, vir_block
    )
    denominator = (
        first_virtual[None, None, :, None]
        + vir_energy[None, None, None, :]
        - slab_energy[:, None, None, None]
        - pair_energy[None, :, None, None]
    )
    return (ladder_own + cycle_own) / denominator


def solution(mesh):
    placed = (P(None, "blk", "red", None), P("red", "blk"), P("blk", "red"), P(), P(), P())
    return jax.shard_map(
        shards, mesh=mesh, in_specs=placed, out_specs=P(None, "red", "blk", None), check_vma=False
    )
```

profile of v0, /device:TPU:1, one launch (start us, length us, event | category | flops | bytes accessed | tf_op | source)
XLA Modules:
  0.0 272.5 jit_solution(8363558085387435878)
XLA Ops:
  6.5 0.0 copy-start
  6.5 0.0 all-gather.5.cloned.1.call-start
  6.5 1.8 copy.20
  8.4 0.0 all-gather.5.cloned.1.call-update
  8.4 0.0 all-gather.3.cloned.1.call-start
  8.4 0.7 all-gather.3.cloned.1.call-update
  9.1 0.0 reduce-scatter.5.cloned.1.call-start
  9.2 57.1 %all-gather.5.cloned.1.call-done = bf16[8,12,128,128]{3,0,1,2:T(8,128)(2,1)} async-done(((bf16[8,12,8,128]{3,0,1,2:T(8,128)(2,1)}), bf16[8,12,128,128]{3,0,1,2:T(8,128)(2,1)}) %all-gather.5.cloned.1.call-update) | async-done | bytes 3145744 | tf_op jit(solution)/shard_map/all_gather | solution.py:18
  66.3 5.0 %copy.21 = bf16[8,12,128,128]{2,3,1,0:T(8,128)(2,1)} copy(bf16[8,12,128,128]{3,0,1,2:T(8,128)(2,1)} %all-gather.5.cloned.1.call-done) | data formatting | bytes 6291456 | tf_op jit(solution)/shard_map/all_gather | solution.py:18
  71.3 9.8 %fusion = f32[8,128,1536]{2,1,0:T(8,128)} fusion(bf16[8,128,1536]{1,2,0:T(8,128)(2,1)} %bitcast.26, bf16[1536,1536]{1,0:T(8,128)(2,1)} %param.8), kind=kOutput, calls=%fused_computation | convolution fusion | flops 4831838208 | bytes 14155776 | tf_op jit(solution)/shard_map/dot_general | solution.py:23
  81.1 0.0 reduce-scatter.5.cloned.1.call-update
  81.1 0.0 reduce-scatter.3.cloned.1.call-start
  81.2 27.7 %all-gather.3.cloned.1.call-done = bf16[8,192,8,128]{3,2,1,0:T(8,128)(2,1)} async-done(((bf16[8,12,8,128]{3,2,1,0:T(8,128)(2,1)}), bf16[8,192,8,128]{3,2,1,0:T(8,128)(2,1)}) %all-gather.3.cloned.1.call-update) | async-done | bytes 3145744 | tf_op jit(solution)/shard_map/all_gather | solution.py:11
  108.9 5.8 %dot_general.10 = bf16[8,192,1024]{2,1,0:T(8,128)(2,1)} reshape(bf16[8,192,8,128]{3,2,1,0:T(8,128)(2,1)} %all-gather.3.cloned.1.call-done) | data formatting | bytes 6291456 | tf_op jit(solution)/shard_map/dot_general | solution.py:14
  114.7 0.0 copy-done
  114.7 7.9 %fusion.2 = f32[8,192,1024]{2,0,1:T(8,128)} fusion(bf16[8,192,1024]{2,1,0:T(8,128)(2,1)} %dot_general.10, bf16[1024,1024]{1,0:T(8,128)(2,1)S(1)} %copy-done), kind=kOutput, calls=%fused_computation.2 | convolution fusion | flops 3221225472 | bytes 11534336 | tf_op jit(solution)/shard_map/dot_general | solution.py:14
  122.6 0.0 copy-start.2
  122.6 0.0 copy-start.1
  122.6 0.0 copy-start.3
  122.6 0.0 reduce-scatter.3.cloned.1.call-update
  122.7 0.6 copy-done.2
  123.3 0.1 dynamic_slice.6
  123.4 0.0 copy-done.1
  123.4 0.1 dynamic_slice.7
  123.4 0.0 copy-done.3
  123.4 0.2 select_reduce_fusion
  123.6 0.1 broadcast_add_fusion
  123.7 0.1 broadcast_subtract_fusion
  123.8 49.4 %reduce-scatter.5.cloned.1.call-done = f32[8,8,1536]{2,1,0:T(8,128)} async-done(((f32[8,128,1536]{2,1,0:T(8,128)}), f32[8,8,1536]{2,1,0:T(8,128)}) %reduce-scatter.5.cloned.1.call-update) | async-done | bytes 393232 | tf_op jit(solution)/shard_map/reduce_scatter | solution.py:25
  173.2 90.8 %reduce-scatter.3.cloned.1.call-done = f32[8,12,1024]{2,0,1:T(8,128)} async-done(((f32[8,192,1024]{2,0,1:T(8,128)}), f32[8,12,1024]{2,0,1:T(8,128)}) %reduce-scatter.3.cloned.1.call-update) | async-done | bytes 393232 | tf_op jit(solution)/shard_map/reduce_scatter | solution.py:16
  264.0 1.3 fusion.5
  265.2 0.8 copy.24
Async XLA Ops:
  6.5 108.1 %copy-start = (bf16[1024,1024]{1,0:T(8,128)(2,1)S(1)}, bf16[1024,1024]{1,0:T(8,128)(2,1)}, u32[]{:S(2)}) copy-start(bf16[1024,1024]{1,0:T(8,128)(2,1)} %param.7) | copy-start | bytes 6291460
  6.5 59.8 %all-gather.5.cloned.1.call-start = ((), (), s32[]{:S(2)}) async-start(), calls=%async_computation.4 | async-start | bytes 3342336 | tf_op jit(solution)/shard_map/all_gather | solution.py:18
  8.4 100.5 %all-gather.3.cloned.1.call-start = ((), (), s32[]{:S(2)}) async-start(), calls=%async_computation.2 | async-start | bytes 3342336 | tf_op jit(solution)/shard_map/all_gather | solution.py:11
  9.1 164.1 %reduce-scatter.5.cloned.1.call-start = ((), (), s32[]{:S(2)}) async-start(), calls=%async_computation.5 | async-start | bytes 6684672 | tf_op jit(solution)/shard_map/reduce_scatter | solution.py:25
  81.1 182.9 %reduce-scatter.3.cloned.1.call-start = ((), (), s32[]{:S(2)}) async-start(), calls=%async_computation.3 | async-start | bytes 6684672 | tf_op jit(solution)/shard_map/reduce_scatter | solution.py:16
  122.6 0.7 copy-start.2
  122.6 0.7 copy-start.1
  122.6 0.8 copy-start.3
Sparse Core Ops, SparseCore 0:
  9.8 56.4 all-gather.4
  68.2 40.6 all-gather.2
  111.5 61.7 reduce-scatter.4
  176.8 87.1 reduce-scatter.2
where the time goes:
time: 273 us
  waiting for transfers between devices  226 us (83%)
  matrix products  17.7 us (6%)
  local copies, waits for them, and re-layouts  14.1 us (5%)
  between operations  13.1 us (5%)
    reduce_scatter x1, waiting for transfers between devices, shards(): lax.psum_scatter(ladder, 'red', scatter_dimension=1, tiled=True)  90.8 us
    all_gather x1, waiting for transfers between devices, shards(): shard_piece = lax.all_gather(amplitudes, 'red', axis=2, tiled=True)  57.1 us
    reduce_scatter x1, waiting for transfers between devices, shards(): lax.psum_scatter(cycle_term, 'blk', scatter_dimension=1, tiled=True)  49.4 us
    all_gather x1, waiting for transfers between devices, shards(): shard_piece = lax.all_gather(amplitudes, 'blk', axis=1, tiled=True)  27.7 us
    dot_general x1, matrix products, shards(): product = jnp.dot(operand, cycle_ints, preferred_element_type=jnp.float32)  9.79 us
    dot_general x1, matrix products, shards(): jnp.dot(flattened, ladder_ints, preferred_element_type=jnp.float32)  7.95 us
    dot_general x1, local copies, waits for them, and re-layouts, shards(): jnp.dot(flattened, ladder_ints, preferred_element_type=jnp.float32)  5.78 us
  transfers between devices with their start and end apart: 4, of which 4 were waited for; matrix products, arithmetic and copies ran while one was open for 11% of the time, Pallas kernels for 0%

commit v1 on v0

v1 whole, which is shorter than its diff:
```python
import functools

import jax
import jax.numpy as jnp
from jax import lax
from jax.experimental import pallas as pl
from jax.experimental.pallas import tpu as pltpu
from jax.sharding import PartitionSpec as P

MESH = pl.DeviceIdType.MESH


def _exchange_kernel(n, per_peer, src_ref, dst_ref, send_sem, recv_sem, local_sem):
    me = lax.axis_index("red")
    row = lax.axis_index("blk")

    def peer_of(o):
        return lax.rem(me + o, n)

    barrier = pltpu.get_barrier_semaphore()
    for o in range(1, n):
        pl.semaphore_signal(barrier, inc=1, device_id=(row, peer_of(o)), device_id_type=MESH)
    pl.semaphore_wait(barrier, n - 1)

    def src_for(g):
        return src_ref.at[g] if per_peer else src_ref

    for o in range(1, n):
        g = peer_of(o)
        pltpu.make_async_remote_copy(
            src_ref=src_for(g),
            dst_ref=dst_ref.at[me],
            send_sem=send_sem.at[g],
            recv_sem=recv_sem.at[me],
            device_id=(row, g),
            device_id_type=MESH,
        ).start()
    local = pltpu.make_async_copy(src_for(me), dst_ref.at[me], local_sem)
    local.start()
    local.wait()
    for o in range(1, n):
        g = peer_of(o)
        pltpu.make_async_remote_copy(
            src_ref=src_for(g),
            dst_ref=dst_ref.at[g],
            send_sem=send_sem.at[g],
            recv_sem=recv_sem.at[g],
            device_id=(row, g),
            device_id_type=MESH,
        ).wait()


def _exchange(x, n, per_peer, collective_id):
    out_shape = x.shape if per_peer else (n,) + x.shape
    nbytes = x.size * x.dtype.itemsize * (1 if per_peer else n)
    return pl.pallas_call(
        functools.partial(_exchange_kernel, n, per_peer),
        out_shape=jax.ShapeDtypeStruct(out_shape, x.dtype),
        in_specs=[pl.BlockSpec(memory_space=pl.ANY)],
        out_specs=pl.BlockSpec(memory_space=pl.ANY),
        scratch_shapes=[
            pltpu.SemaphoreType.DMA((n,)),
            pltpu.SemaphoreType.DMA((n,)),
            pltpu.SemaphoreType.DMA,
        ],
        compiler_params=pltpu.CompilerParams(collective_id=collective_id, has_side_effects=True),
        cost_estimate=pl.CostEstimate(flops=0, bytes_accessed=2 * nbytes, transcendentals=0),
    )(x)


def shards(amplitudes, ladder_ints, cycle_ints, occ_energy, vir_energy, slab_index):
    slab_rows, occ_local, vir_local, virt_width = amplitudes.shape
    n_red = lax.axis_size("red")
    n_blk = lax.axis_size("blk")
    occ_all = occ_local * n_blk
    occ_red = occ_all // n_red

    swapped = jnp.transpose(amplitudes, (0, 2, 1, 3))
    gathered = _exchange(swapped, n_red, False, 0)
    operand = gathered.reshape(n_red * slab_rows * vir_local, occ_local * virt_width)
    product = jnp.dot(operand, cycle_ints, preferred_element_type=jnp.float32)
    product = product.reshape(n_red, slab_rows, vir_local, cycle_ints.shape[1])
    cycle_own = lax.psum_scatter(product, "blk", scatter_dimension=0, tiled=True)[0]
    cycle_own = jnp.transpose(
        cycle_own.reshape(slab_rows, vir_local, occ_red, virt_width), (0, 2, 1, 3)
    )

    shard_piece = lax.all_gather(amplitudes, "blk", axis=0, tiled=False)
    flattened = shard_piece.reshape(n_blk * slab_rows * occ_local, vir_local * virt_width)
    product = jnp.dot(flattened, ladder_ints, preferred_element_type=jnp.float32)
    product = product.reshape(n_blk, slab_rows, occ_local, ladder_ints.shape[1])
    received = _exchange(product, n_red, True, 1)
    ladder_own = jnp.sum(received, axis=0).reshape(slab_rows, occ_red, -1, virt_width)

    vir_block = cycle_own.shape[2]
    orbital_ids = jnp.arange(occ_energy.shape[0], dtype=jnp.int32)
    chosen = slab_index[:, None] == orbital_ids[None, :]
    slab_energy = jnp.sum(jnp.where(chosen, occ_energy[None, :], jnp.float32(0.0)), axis=1)
    pair_energy = lax.dynamic_slice_in_dim(occ_energy, lax.axis_index("red") * occ_red, occ_red)
    first_virtual = lax.dynamic_slice_in_dim(
        vir_energy, lax.axis_index("blk") * vir_block, vir_block
    )
    denominator = (
        first_virtual[None, None, :, None]
        + vir_energy[None, None, None, :]
        - slab_energy[:, None, None, None]
        - pair_energy[None, :, None, None]
    )
    return (ladder_own + cycle_own) / denominator


def solution(mesh):
    placed = (P(None, "blk", "red", None), P("red", "blk"), P("blk", "red"), P(), P(), P())
    return jax.shard_map(
        shards, mesh=mesh, in_specs=placed, out_specs=P(None, "red", "blk", None), check_vma=False
    )
```

time: 273 us -> 338 us (1.24)
  the two profiles are of different devices: /device:TPU:1 before, /device:TPU:28 now
where the time goes in v1:
time: 338 us
  Pallas kernels  282 us (83%)
  matrix products  18.7 us (6%)
  local copies, waits for them, and re-layouts  17 us (5%)
  between operations  13.5 us (4%)
  other arithmetic  5.88 us (2%)
    pallas_call x2, Pallas kernels, _exchange(): pl.pallas_call(functools.partial(_exchange_kernel, n, per_peer), out_shap...  282 us
    dot_general x1, matrix products, shards(): product = jnp.dot(operand, cycle_ints, preferred_element_type=jnp.float32)  9.71 us
    dot_general x1, matrix products, shards(): jnp.dot(flattened, ladder_ints, preferred_element_type=jnp.float32)  8.97 us
    dot_general x1, local copies, waits for them, and re-layouts, shards(): jnp.dot(flattened, ladder_ints, preferred_element_type=jnp.float32)  6.86 us
    dot_general x1, local copies, waits for them, and re-layouts, shards(): product = jnp.dot(operand, cycle_ints, preferred_element_type=jnp.float32)  6.86 us
  transfers between devices with their start and end apart: 2, of which 0 were waited for; matrix products, arithmetic and copies ran while one was open for 12% of the time, Pallas kernels for 83%

profile of v1, /device:TPU:28, one launch (start us, length us, event | category | flops | bytes accessed | tf_op | source)
XLA Modules:
  0.0 337.7 jit_solution(13180546982815386203)
XLA Ops:
  6.5 0.0 copy-start
  6.5 0.0 all-gather.3.cloned.1.call-start
  6.5 0.7 all-gather.3.cloned.1.call-update
  7.3 0.0 reduce-scatter.2.cloned.1.call-start
  7.3 1.7 copy.39
  9.0 93.8 %shard_map.65 = bf16[16,8,8,12,128]{4,3,2,1,0:T(8,128)(2,1)} custom-call(bf16[8,8,12,128]{3,2,1,0:T(8,128)(2,1)} %bitcast.24), custom_call_target="tpu_custom_call" | custom-call | bytes 6291456 | tf_op jit(solution)/shard_map/pallas_call | solution.py:56
  102.8 6.9 %dot_general.12 = bf16[16,8,8,1536]{3,2,1,0:T(8,128)(2,1)} reshape(bf16[16,8,8,12,128]{4,3,2,1,0:T(8,128)(2,1)} %shard_map.65) | data formatting | bytes 6291456 | tf_op jit(solution)/shard_map/dot_general | solution.py:81
  109.6 9.7 %fusion = f32[16,8,8,1536]{3,2,1,0:T(8,128)} fusion(bf16[16,8,8,1536]{3,2,1,0:T(8,128)(2,1)} %dot_general.12, bf16[1536,1536]{1,0:T(8,128)(2,1)} %param.8), kind=kOutput, calls=%fused_computation | convolution fusion | flops 4831838208 | bytes 14155776 | tf_op jit(solution)/shard_map/dot_general | solution.py:81
  119.4 0.0 copy-start.1
  119.4 0.0 copy-start.2
  119.4 0.0 copy-start.3
  119.4 0.0 reduce-scatter.2.cloned.1.call-update
  119.4 0.6 copy-done.1
  120.0 0.1 dynamic_slice.7
  120.1 0.0 copy-done.2
  120.1 0.1 dynamic_slice.6
  120.2 0.0 copy-done.3
  120.2 0.2 select_reduce_fusion
  120.4 0.1 broadcast_add_fusion
  120.4 0.1 broadcast_subtract_fusion
  120.5 0.0 all-gather.3.cloned.1.call-done
  120.5 6.9 %reshape.58 = bf16[16,8,12,1024]{3,2,1,0:T(8,128)(2,1)} reshape(bf16[128,12,8,128]{3,2,1,0:T(8,128)(2,1)} %all-gather.3.cloned.1.call-done) | data formatting | bytes 6291456 | tf_op jit(solution)/shard_map/dot_general | solution.py:90
  127.4 0.0 copy-done
  127.4 9.0 %fusion.2.src_ref = f32[16,8,12,1024]{3,2,1,0:T(8,128)} fusion(bf16[16,8,12,1024]{3,2,1,0:T(8,128)(2,1)} %reshape.58, bf16[1024,1024]{1,0:T(8,128)(2,1)S(1)} %copy-done), kind=kOutput, calls=%fused_computation.2 | convolution fusion | flops 3221225472 | bytes 11534336 | tf_op jit(solution)/shard_map/dot_general | solution.py:90
  136.4 188.1 %shard_map.64 = f32[16,8,12,1024]{3,2,1,0:T(8,128)} custom-call(f32[16,8,12,1024]{3,2,1,0:T(8,128)} %fusion.2.src_ref), custom_call_target="tpu_custom_call" | custom-call | bytes 12582912 | tf_op jit(solution)/shard_map/pallas_call | solution.py:56
  324.4 4.4 %reduce_sum.18 = f32[8,12,1024]{2,1,0:T(8,128)S(1)} reduce(f32[16,8,12,1024]{3,2,1,0:T(8,128)} %shard_map.64, f32[]{:T(128)} %constant.3.clone.1), dimensions={0}, to_apply=%region_0.0 | reduce | flops 1474560 | bytes 6684676 | tf_op jit(solution)/shard_map/reduce_sum | solution.py:93
  328.9 0.1 reshape.59
  328.9 0.0 reduce-scatter.2.cloned.1.call-done
  329.0 1.1 fusion.4
  330.1 0.8 copy.28
Async XLA Ops:
  6.5 120.8 %copy-start = (bf16[1024,1024]{1,0:T(8,128)(2,1)S(1)}, bf16[1024,1024]{1,0:T(8,128)(2,1)}, u32[]{:S(2)}) copy-start(bf16[1024,1024]{1,0:T(8,128)(2,1)} %param.7) | copy-start | bytes 6291460
  6.5 114.0 %all-gather.3.cloned.1.call-start = ((), (), s32[]{:S(2)}) async-start(), calls=%async_computation.2 | async-start | bytes 3342336 | tf_op jit(solution)/shard_map/all_gather | solution.py:88
  7.3 321.7 %reduce-scatter.2.cloned.1.call-start = ((), (), s32[]{:S(2)}) async-start(), calls=%async_computation.1 | async-start | bytes 6684672 | tf_op jit(solution)/shard_map/reduce_scatter | solution.py:83
  119.4 0.7 copy-start.1
  119.4 0.8 copy-start.2
  119.4 0.8 copy-start.3
Sparse Core Ops, SparseCore 0:
  9.2 43.2 all-gather.2
  119.5 70.2 reduce-scatter.1

commit v2 on v0

v2 whole, which is shorter than its diff:
```python
import functools

import jax
import jax.numpy as jnp
from jax import lax
from jax.experimental import pallas as pl
from jax.experimental.pallas import tpu as pltpu
from jax.sharding import PartitionSpec as P

MESH = pl.DeviceIdType.MESH


NY = 4


def _group(kind, n_red):
    r = lax.axis_index("red")
    x, y = r // NY, lax.rem(r, NY)
    if kind == "y":
        return y, NY, lambda pos: x * NY + pos
    if kind == "x":
        return x, n_red // NY, lambda pos: pos * NY + y
    return r, n_red, lambda pos: pos


def _exchange_kernel(jobs, n_red, *refs):
    k = len(jobs)
    srcs, dsts = refs[:k], refs[k:2 * k]
    send_sem, recv_sem, local_sem = refs[2 * k:]
    row = lax.axis_index("blk")

    barrier = pltpu.get_barrier_semaphore()
    count = 0
    for kind in sorted(set(kind for kind, _ in jobs)):
        me, n, red_of = _group(kind, n_red)
        for o in range(1, n):
            pl.semaphore_signal(
                barrier, inc=1, device_id=(row, red_of(lax.rem(me + o, n))), device_id_type=MESH
            )
            count += 1
    pl.semaphore_wait(barrier, count)

    def remote(j, pos, slot):
        kind, src_view = jobs[j]
        _, _, red_of = _group(kind, n_red)
        return pltpu.make_async_remote_copy(
            src_ref=src_view(srcs[j], pos),
            dst_ref=dsts[j].at[slot],
            send_sem=send_sem.at[j, pos],
            recv_sem=recv_sem.at[j, slot],
            device_id=(row, red_of(pos)),
            device_id_type=MESH,
        )

    for j, (kind, src_view) in enumerate(jobs):
        me, n, _ = _group(kind, n_red)
        for o in range(1, n):
            remote(j, lax.rem(me + o, n), me).start()
    for j, (kind, src_view) in enumerate(jobs):
        me, n, _ = _group(kind, n_red)
        local = pltpu.make_async_copy(src_view(srcs[j], me), dsts[j].at[me], local_sem.at[j])
        local.start()
        local.wait()
    for j, (kind, src_view) in enumerate(jobs):
        me, n, _ = _group(kind, n_red)
        for o in range(1, n):
            g = lax.rem(me + o, n)
            remote(j, g, g).wait()


def _exchange(jobs, srcs, out_shapes, n_red, collective_id):
    nbytes = sum(s.size * s.dtype.itemsize for s in srcs)
    nmax = max(_group_size(kind, n_red) for kind, _ in jobs)
    return pl.pallas_call(
        functools.partial(_exchange_kernel, tuple(jobs), n_red),
        out_shape=tuple(jax.ShapeDtypeStruct(s, x.dtype) for s, x in zip(out_shapes, srcs)),
        in_specs=[pl.BlockSpec(memory_space=pl.ANY)] * len(srcs),
        out_specs=tuple(pl.BlockSpec(memory_space=pl.ANY) for _ in srcs),
        scratch_shapes=[
            pltpu.SemaphoreType.DMA((len(jobs), nmax)),
            pltpu.SemaphoreType.DMA((len(jobs), nmax)),
            pltpu.SemaphoreType.DMA((len(jobs),)),
        ],
        compiler_params=pltpu.CompilerParams(collective_id=collective_id, has_side_effects=True),
        cost_estimate=pl.CostEstimate(flops=0, bytes_accessed=4 * nbytes, transcendentals=0),
    )(*srcs)


def _group_size(kind, n_red):
    return {"y": NY, "x": n_red // NY}.get(kind, n_red)


def _whole(ref, pos):
    return ref


def _slot(ref, pos):
    return ref.at[pos]


def shards(amplitudes, ladder_ints, cycle_ints, occ_energy, vir_energy, slab_index):
    slab_rows, occ_local, vir_local, virt_width = amplitudes.shape
    n_red = lax.axis_size("red")
    n_blk = lax.axis_size("blk")
    occ_all = occ_local * n_blk
    occ_red = occ_all // n_red
    n_x = n_red // NY

    swapped = jnp.transpose(amplitudes, (0, 2, 1, 3)).reshape(
        slab_rows * vir_local, occ_local * virt_width
    )
    (gathered,) = _exchange(
        [("all", _whole)], [swapped], [(n_red,) + swapped.shape], n_red, 0
    )
    operand = gathered.reshape(n_red * slab_rows * vir_local, occ_local * virt_width)
    product = jnp.dot(operand, cycle_ints, preferred_element_type=jnp.float32)
    product = product.reshape(n_red, slab_rows * vir_local, cycle_ints.shape[1])
    cycle_own = lax.psum_scatter(product, "blk", scatter_dimension=0, tiled=True)[0]
    cycle_own = jnp.transpose(
        cycle_own.reshape(slab_rows, vir_local, occ_red, virt_width), (0, 2, 1, 3)
    )

    rows = slab_rows * occ_local
    flat = amplitudes.reshape(rows, vir_local * virt_width)
    shard_piece = lax.all_gather(flat, "blk", axis=0, tiled=False)
    product = jnp.dot(
        shard_piece.reshape(n_blk * rows, -1), ladder_ints, preferred_element_type=jnp.float32
    )
    cols = ladder_ints.shape[1]
    product = product.reshape(n_x, NY, rows, cols)
    half = rows // 2
    first_a, first_b = _exchange(
        [
            ("y", lambda ref, pos: ref.at[:, pos, pl.ds(0, half)]),
            ("x", lambda ref, pos: ref.at[pos, :, pl.ds(half, half)]),
        ],
        [product, product],
        [(NY, n_x, half, cols), (n_x, NY, half, cols)],
        n_red,
        1,
    )
    second_a, second_b = _exchange(
        [("x", _slot), ("y", _slot)],
        [jnp.sum(first_a, axis=0), jnp.sum(first_b, axis=0)],
        [(n_x, half, cols), (NY, half, cols)],
        n_red,
        2,
    )
    ladder_own = jnp.concatenate([jnp.sum(second_a, axis=0), jnp.sum(second_b, axis=0)], axis=0)
    ladder_own = ladder_own.reshape(slab_rows, occ_red, -1, virt_width)

    vir_block = cycle_own.shape[2]
    orbital_ids = jnp.arange(occ_energy.shape[0], dtype=jnp.int32)
    chosen = slab_index[:, None] == orbital_ids[None, :]
    slab_energy = jnp.sum(jnp.where(chosen, occ_energy[None, :], jnp.float32(0.0)), axis=1)
    pair_energy = lax.dynamic_slice_in_dim(occ_energy, lax.axis_index("red") * occ_red, occ_red)
    first_virtual = lax.dynamic_slice_in_dim(
        vir_energy, lax.axis_index("blk") * vir_block, vir_block
    )
    denominator = (
        first_virtual[None, None, :, None]
        + vir_energy[None, None, None, :]
        - slab_energy[:, None, None, None]
        - pair_energy[None, :, None, None]
    )
    return (ladder_own + cycle_own) / denominator


def solution(mesh):
    placed = (P(None, "blk", "red", None), P("red", "blk"), P("blk", "red"), P(), P(), P())
    return jax.shard_map(
        shards, mesh=mesh, in_specs=placed, out_specs=P(None, "red", "blk", None), check_vma=False
    )
```

time: 273 us -> 182 us (0.67)
  waiting for transfers between devices: 226 us -> 0.06 us
  Pallas kernels: 0 us -> 137 us
  local copies, waits for them, and re-layouts: 14.1 us -> 2.71 us
  other arithmetic: 1.58 us -> 11 us
    reduce_scatter x2 -> x1, waiting for transfers between devices: 140 us -> 0.02 us  [shards(): lax.psum_scatter(product, 'blk', scatter_dimension=0, tiled=True)[0]]
    pallas_call x0 -> x3, Pallas kernels: none -> 137 us  [_exchange(): pl.pallas_call(functools.partial(_exchange_kernel, tuple(jobs), n_red), o...]
    all_gather x2 -> x1, waiting for transfers between devices: 84.9 us -> 0.01 us  [shards(): shard_piece = lax.all_gather(flat, 'blk', axis=0, tiled=False)]
    reduce_sum x0 -> x4, other arithmetic: none -> 8.78 us  [the longest x1 3.22 us: shards(): jnp.sum(first_a, axis=0)]
    dot_general x1 -> x0, local copies, waits for them, and re-layouts: 5.78 us -> none  [shards(): jnp.dot(flattened, ladder_ints, preferred_element_type=jnp.float32)]
    all_gather x1 -> x0, local copies, waits for them, and re-layouts: 4.97 us -> none  [shards(): shard_piece = lax.all_gather(amplitudes, 'red', axis=2, tiled=True)]
  transfers between devices with their start and end apart: 4 -> 2, of which waited for: 4 -> 0; matrix products, arithmetic and copies ran while one was open for 11% -> 14% of each run, Pallas kernels for 0% -> 76%
where the time goes in v2:
time: 182 us
  Pallas kernels  137 us (75%)
  matrix products  16.9 us (9%)
  between operations  13.5 us (7%)
  other arithmetic  11 us (6%)
  local copies, waits for them, and re-layouts  2.71 us (1%)
    pallas_call x3, Pallas kernels, _exchange(): pl.pallas_call(functools.partial(_exchange_kernel, tuple(jobs), n_red), o...  137 us
    dot_general x1, matrix products, shards(): product = jnp.dot(operand, cycle_ints, preferred_element_type=jnp.float32)  9.73 us
    dot_general x1, matrix products, shards(): jnp.dot(shard_piece.reshape(n_blk * rows, -1), ladder_ints, preferred_ele...  7.22 us
  transfers between devices with their start and end apart: 2, of which 0 were waited for; matrix products, arithmetic and copies ran while one was open for 14% of the time, Pallas kernels for 76%

profile of v2, /device:TPU:1, one launch (start us, length us, event | category | flops | bytes accessed | tf_op | source)
XLA Modules:
  0.0 181.5 jit_solution(7745619105899166869)
XLA Ops:
  6.5 0.0 copy-start
  6.5 0.0 all-gather.2.cloned.1.call-start
  6.5 1.8 %all_gather_reshape.3 = bf16[1,96,1024]{2,1,0:T(8,128)(2,1)} reshape(bf16[8,12,8,128]{3,2,1,0:T(8,128)(2,1)} %param.6) | data formatting | bytes 393216 | tf_op jit(solution)/shard_map/all_gather;reshape | solution.py:125
  8.4 0.0 all-gather.2.cloned.1.call-update
  8.4 0.0 reduce-scatter.2.cloned.1.call-start
  8.5 58.9 %shard_map.66 = bf16[16,64,1536]{2,1,0:T(8,128)(2,1)} custom-call(bf16[64,1536]{1,0:T(8,128)(2,1)} %bitcast.27), custom_call_target="tpu_custom_call" | custom-call | bytes 786432 | tf_op jit(solution)/shard_map/pallas_call | solution.py:74
  67.4 9.7 %fusion = f32[16,64,1536]{2,1,0:T(8,128)} fusion(bf16[16,64,1536]{2,1,0:T(8,128)(2,1)} %shard_map.66, bf16[1536,1536]{1,0:T(8,128)(2,1)} %param.8), kind=kOutput, calls=%fused_computation | convolution fusion | flops 4831838208 | bytes 14155776 | tf_op jit(solution)/shard_map/dot_general | solution.py:116
  77.1 0.0 copy-start.1
  77.1 0.0 copy-start.2
  77.1 0.0 copy-start.3
  77.1 0.0 reduce-scatter.2.cloned.1.call-update
  77.1 0.6 copy-done.1
  77.8 0.1 dynamic_slice.7
  77.9 0.0 copy-done.2
  77.9 0.1 dynamic_slice.6
  77.9 0.0 copy-done.3
  77.9 0.2 select_reduce_fusion
  78.1 0.1 broadcast_add_fusion
  78.2 0.1 broadcast_subtract_fusion
  78.3 0.0 all-gather.2.cloned.1.call-done
  78.3 0.0 copy-done
  78.3 7.2 %fusion.2.refs_0_.refs_1_ = f32[4,4,96,1024]{3,2,1,0:T(8,128)} fusion(bf16[4,4,96,1024]{3,2,1,0:T(8,128)(2,1)} %bitcast.28, bf16[1024,1024]{1,0:T(8,128)(2,1)S(1)} %copy-done), kind=kOutput, calls=%fused_computation.2 | convolution fusion | flops 3221225472 | bytes 11534336 | tf_op jit(solution)/shard_map/dot_general | solution.py:126
  85.5 60.4 %shard_map.64 = (f32[4,4,48,1024]{3,2,1,0:T(8,128)}, f32[4,4,48,1024]{3,2,1,0:T(8,128)}) custom-call(f32[4,4,96,1024]{3,2,1,0:T(8,128)} %fusion.2.refs_0_.refs_1_, f32[4,4,96,1024]{3,2,1,0:T(8,128)} %fusion.2.refs_0_.refs_1_), custom_call_target="tpu_custom_call" | custom-call | bytes 50331648 | tf_op jit(solution)/shard_map/pallas_call | solution.py:74
  145.9 3.2 %reduce_sum.45.refs_0_ = f32[4,48,1024]{2,1,0:T(8,128)} reduce(f32[4,4,48,1024]{3,2,1,0:T(8,128)} %get-tuple-element.9, f32[]{:T(128)} %constant.3.clone.1), dimensions={0}, to_apply=%region_0.0 | reduce | flops 589824 | bytes 3932164 | tf_op jit(solution)/shard_map/reduce_sum | solution.py:144
  149.1 3.2 %reduce_sum.46.refs_1_ = f32[4,48,1024]{2,1,0:T(8,128)} reduce(f32[4,4,48,1024]{3,2,1,0:T(8,128)} %get-tuple-element.10, f32[]{:T(128)} %constant.3.clone.1), dimensions={0}, to_apply=%region_1.0 | reduce | flops 589824 | bytes 3932164 | tf_op jit(solution)/shard_map/reduce_sum | solution.py:144
  152.3 18.0 %shard_map.65 = (f32[4,48,1024]{2,1,0:T(8,128)}, f32[4,48,1024]{2,1,0:T(8,128)}) custom-call(f32[4,48,1024]{2,1,0:T(8,128)} %reduce_sum.45.refs_0_, f32[4,48,1024]{2,1,0:T(8,128)} %reduce_sum.46.refs_1_), custom_call_target="tpu_custom_call" | custom-call | bytes 6291456 | tf_op jit(solution)/shard_map/pallas_call | solution.py:74
  170.2 1.2 reduce_sum.48
  171.4 1.2 reduce_sum.47
  172.7 0.1 copy.8
  172.8 0.0 reduce-scatter.2.cloned.1.call-done
  172.8 1.9 %fusion.4 = f32[8,12,8,128]{3,2,1,0:T(8,128)} fusion(f32[8,12,8,128]{3,2,1,0:T(8,128)S(1)} %bitcast.26, f32[1,64,1536]{2,1,0:T(8,128)} %reduce-scatter.2.cloned.1.call-done, f32[12]{0:T(128)S(1)} %dynamic_slice.7, f32[8,8,128]{2,1,0:T(8,128)S(1)} %broadcast_subtract_fusion), kind=kLoop, calls=%fused_computation.6 | loop fusion | flops 294912 | bytes 1212464 | tf_op jit(solution)/shard_map/div | solution.py:166
  (1 shorter events, 0.0 us)
Async XLA Ops:
  6.5 71.7 %copy-start = (bf16[1024,1024]{1,0:T(8,128)(2,1)S(1)}, bf16[1024,1024]{1,0:T(8,128)(2,1)}, u32[]{:S(2)}) copy-start(bf16[1024,1024]{1,0:T(8,128)(2,1)} %param.7) | copy-start | bytes 6291460
  6.5 71.7 %all-gather.2.cloned.1.call-start = ((), (), s32[]{:S(2)}) async-start(), calls=%async_computation.1 | async-start | bytes 3342336 | tf_op jit(solution)/shard_map/all_gather | solution.py:125
  8.4 164.4 %reduce-scatter.2.cloned.1.call-start = ((), (), s32[]{:S(2)}) async-start(), calls=%async_computation.2 | async-start | bytes 6684672 | tf_op jit(solution)/shard_map/reduce_scatter | solution.py:118
  77.1 0.7 copy-start.1
  77.1 0.8 copy-start.2
  77.1 0.8 copy-start.3
Sparse Core Ops, SparseCore 0:
  9.2 44.9 all-gather.1
  77.3 77.0 reduce-scatter.1

commit v3 on v2

--- a/solution.py
+++ b/solution.py
@@ -23,15 +23,14 @@
     return r, n_red, lambda pos: pos
 
 
-def _exchange_kernel(jobs, n_red, *refs):
-    k = len(jobs)
-    srcs, dsts = refs[:k], refs[k:2 * k]
-    send_sem, recv_sem, local_sem = refs[2 * k:]
+def _exchange_kernel(jobs, n_in, n_out, n_red, *refs):
+    ins, outs = refs[:n_in], refs[n_in:n_in + n_out]
+    send_sem, recv_sem, local_sem = refs[n_in + n_out:]
     row = lax.axis_index("blk")
 
     barrier = pltpu.get_barrier_semaphore()
     count = 0
-    for kind in sorted(set(kind for kind, _ in jobs)):
+    for kind in sorted(set(job[0] for job in jobs)):
         me, n, red_of = _group(kind, n_red)
         for o in range(1, n):
             pl.semaphore_signal(
@@ -41,28 +40,30 @@
     pl.semaphore_wait(barrier, count)
 
     def remote(j, pos, slot):
-        kind, src_view = jobs[j]
+        kind, si, src_view, di, dst_view = jobs[j]
         _, _, red_of = _group(kind, n_red)
         return pltpu.make_async_remote_copy(
-            src_ref=src_view(srcs[j], pos),
-            dst_ref=dsts[j].at[slot],
+            src_ref=src_view(ins[si], pos),
+            dst_ref=dst_view(outs[di], slot),
             send_sem=send_sem.at[j, pos],
             recv_sem=recv_sem.at[j, slot],
             device_id=(row, red_of(pos)),
             device_id_type=MESH,
         )
 
-    for j, (kind, src_view) in enumerate(jobs):
-        me, n, _ = _group(kind, n_red)
+    for j, job in enumerate(jobs):
+        me, n, _ = _group(job[0], n_red)
         for o in range(1, n):
             remote(j, lax.rem(me + o, n), me).start()
-    for j, (kind, src_view) in enumerate(jobs):
+    for j, (kind, si, src_view, di, dst_view) in enumerate(jobs):
         me, n, _ = _group(kind, n_red)
-        local = pltpu.make_async_copy(src_view(srcs[j], me), dsts[j].at[me], local_sem.at[j])
+        local = pltpu.make_async_copy(
+            src_view(ins[si], me), dst_view(outs[di], me), local_sem.at[j]
+        )
         local.start()
         local.wait()
-    for j, (kind, src_view) in enumerate(jobs):
-        me, n, _ = _group(kind, n_red)
+    for j, job in enumerate(jobs):
+        me, n, _ = _group(job[0], n_red)
         for o in range(1, n):
             g = lax.rem(me + o, n)
             remote(j, g, g).wait()
@@ -70,12 +71,12 @@
 
 def _exchange(jobs, srcs, out_shapes, n_red, collective_id):
     nbytes = sum(s.size * s.dtype.itemsize for s in srcs)
-    nmax = max(_group_size(kind, n_red) for kind, _ in jobs)
+    nmax = max(_group_size(job[0], n_red) for job in jobs)
     return pl.pallas_call(
-        functools.partial(_exchange_kernel, tuple(jobs), n_red),
-        out_shape=tuple(jax.ShapeDtypeStruct(s, x.dtype) for s, x in zip(out_shapes, srcs)),
+        functools.partial(_exchange_kernel, tuple(jobs), len(srcs), len(out_shapes), n_red),
+        out_shape=tuple(jax.ShapeDtypeStruct(s, d) for s, d in out_shapes),
         in_specs=[pl.BlockSpec(memory_space=pl.ANY)] * len(srcs),
-        out_specs=tuple(pl.BlockSpec(memory_space=pl.ANY) for _ in srcs),
+        out_specs=tuple(pl.BlockSpec(memory_space=pl.ANY) for _ in out_shapes),
         scratch_shapes=[
             pltpu.SemaphoreType.DMA((len(jobs), nmax)),
             pltpu.SemaphoreType.DMA((len(jobs), nmax)),
@@ -109,8 +110,28 @@
     swapped = jnp.transpose(amplitudes, (0, 2, 1, 3)).reshape(
         slab_rows * vir_local, occ_local * virt_width
     )
+    width = swapped.shape[1]
+    part = swapped.shape[0] // 2
+    bf = swapped.dtype
+    near_a, near_b = _exchange(
+        [
+            ("y", 0, lambda ref, pos: ref.at[pl.ds(0, part)], 0, _slot),
+            ("x", 0, lambda ref, pos: ref.at[pl.ds(part, part)], 1, _slot),
+        ],
+        [swapped],
+        [((NY, part, width), bf), ((n_x, part, width), bf)],
+        n_red,
+        0,
+    )
     (gathered,) = _exchange(
-        [("all", _whole)], [swapped], [(n_red,) + swapped.shape], n_red, 0
+        [
+            ("x", 0, _whole, 0, lambda ref, slot: ref.at[slot, :, pl.ds(0, part)]),
+            ("y", 1, _whole, 0, lambda ref, slot: ref.at[:, slot, pl.ds(part, part)]),
+        ],
+        [near_a, near_b],
+        [((n_x, NY, 2 * part, width), bf)],
+        n_red,
+        3,
     )
     operand = gathered.reshape(n_red * slab_rows * vir_local, occ_local * virt_width)
     product = jnp.dot(operand, cycle_ints, preferred_element_type=jnp.float32)
@@ -131,18 +152,18 @@
     half = rows // 2
     first_a, first_b = _exchange(
         [
-            ("y", lambda ref, pos: ref.at[:, pos, pl.ds(0, half)]),
-            ("x", lambda ref, pos: ref.at[pos, :, pl.ds(half, half)]),
+            ("y", 0, lambda ref, pos: ref.at[:, pos, pl.ds(0, half)], 0, _slot),
+            ("x", 0, lambda ref, pos: ref.at[pos, :, pl.ds(half, half)], 1, _slot),
         ],
-        [product, product],
-        [(NY, n_x, half, cols), (n_x, NY, half, cols)],
+        [product],
+        [((NY, n_x, half, cols), jnp.float32), ((n_x, NY, half, cols), jnp.float32)],
         n_red,
         1,
     )
     second_a, second_b = _exchange(
-        [("x", _slot), ("y", _slot)],
+        [("x", 0, _slot, 0, _slot), ("y", 1, _slot, 1, _slot)],
         [jnp.sum(first_a, axis=0), jnp.sum(first_b, axis=0)],
-        [(n_x, half, cols), (NY, half, cols)],
+        [((n_x, half, cols), jnp.float32), ((NY, half, cols), jnp.float32)],
         n_red,
         2,
     )

time: 182 us -> 159 us (0.87)
  Pallas kernels: 137 us -> 114 us
    pallas_call x3 -> x4, Pallas kernels: 137 us -> 114 us  [_exchange(): pl.pallas_call(functools.partial(_exchange_kernel, tuple(jobs), len(srcs)...]
  transfers between devices with their start and end apart: 2 -> 2, of which waited for: 0 -> 0; matrix products, arithmetic and copies ran while one was open for 14% -> 17% of each run, Pallas kernels for 76% -> 72%
where the time goes in v3:
time: 159 us
  Pallas kernels  114 us (72%)
  matrix products  16.9 us (11%)
  between operations  13.5 us (8%)
  other arithmetic  11 us (7%)
  local copies, waits for them, and re-layouts  2.71 us (2%)
    pallas_call x4, Pallas kernels, _exchange(): pl.pallas_call(functools.partial(_exchange_kernel, tuple(jobs), len(srcs)...  114 us
    dot_general x1, matrix products, shards(): product = jnp.dot(operand, cycle_ints, preferred_element_type=jnp.float32)  9.73 us
    dot_general x1, matrix products, shards(): jnp.dot(shard_piece.reshape(n_blk * rows, -1), ladder_ints, preferred_ele...  7.21 us
    reduce_sum x1, other arithmetic, shards(): jnp.sum(first_a, axis=0)  3.18 us
    reduce_sum x1, other arithmetic, shards(): jnp.sum(first_b, axis=0)  3.18 us
  transfers between devices with their start and end apart: 2, of which 0 were waited for; matrix products, arithmetic and copies ran while one was open for 17% of the time, Pallas kernels for 72%

profile of v3, /device:TPU:1, one launch (start us, length us, event | category | flops | bytes accessed | tf_op | source)
XLA Modules:
  0.0 158.6 jit_solution(11163928151035767220)
XLA Ops:
  6.5 0.0 copy-start
  6.5 0.0 all-gather.2.cloned.1.call-start
  6.5 1.8 %all_gather_reshape.3 = bf16[1,96,1024]{2,1,0:T(8,128)(2,1)} reshape(bf16[8,12,8,128]{3,2,1,0:T(8,128)(2,1)} %param.6) | data formatting | bytes 393216 | tf_op jit(solution)/shard_map/all_gather;reshape | solution.py:146
  8.4 0.0 all-gather.2.cloned.1.call-update
  8.4 0.0 reduce-scatter.2.cloned.1.call-start
  8.5 12.3 %shard_map.66 = (bf16[4,32,1536]{2,1,0:T(8,128)(2,1)}, bf16[4,32,1536]{2,1,0:T(8,128)(2,1)}) custom-call(bf16[64,1536]{1,0:T(8,128)(2,1)} %bitcast.29), custom_call_target="tpu_custom_call" | custom-call | bytes 786432 | tf_op jit(solution)/shard_map/pallas_call | solution.py:75
  20.7 34.8 %shard_map.67 = bf16[4,4,64,1536]{3,2,1,0:T(8,128)(2,1)} custom-call(bf16[4,32,1536]{2,1,0:T(8,128)(2,1)} %get-tuple-element.15.refs_0_, bf16[4,32,1536]{2,1,0:T(8,128)(2,1)} %get-tuple-element.16.refs_1_), custom_call_target="tpu_custom_call" | custom-call | bytes 3145728 | tf_op jit(solution)/shard_map/pallas_call | solution.py:75
  55.5 9.7 %fusion = f32[16,64,1536]{2,1,0:T(8,128)} fusion(bf16[16,64,1536]{2,1,0:T(8,128)(2,1)} %bitcast.27, bf16[1536,1536]{1,0:T(8,128)(2,1)} %param.8), kind=kOutput, calls=%fused_computation | convolution fusion | flops 4831838208 | bytes 14155776 | tf_op jit(solution)/shard_map/dot_general | solution.py:137
  65.3 0.0 copy-start.1
  65.3 0.0 copy-start.2
  65.3 0.0 copy-start.3
  65.3 0.0 reduce-scatter.2.cloned.1.call-update
  65.3 0.6 copy-done.1
  66.0 0.1 dynamic_slice.7
  66.0 0.0 copy-done.2
  66.0 0.1 dynamic_slice.6
  66.1 0.0 copy-done.3
  66.1 0.2 select_reduce_fusion
  66.3 0.1 broadcast_add_fusion
  66.4 0.1 broadcast_subtract_fusion
  66.4 0.0 all-gather.2.cloned.1.call-done
  66.4 0.0 copy-done
  66.5 7.2 %fusion.2.refs_0_ = f32[4,4,96,1024]{3,2,1,0:T(8,128)} fusion(bf16[4,4,96,1024]{3,2,1,0:T(8,128)(2,1)} %bitcast.30, bf16[1024,1024]{1,0:T(8,128)(2,1)S(1)} %copy-done), kind=kOutput, calls=%fused_computation.2 | convolution fusion | flops 3221225472 | bytes 11534336 | tf_op jit(solution)/shard_map/dot_general | solution.py:147
  73.7 50.3 %shard_map.64 = (f32[4,4,48,1024]{3,2,1,0:T(8,128)}, f32[4,4,48,1024]{3,2,1,0:T(8,128)}) custom-call(f32[4,4,96,1024]{3,2,1,0:T(8,128)} %fusion.2.refs_0_), custom_call_target="tpu_custom_call" | custom-call | bytes 25165824 | tf_op jit(solution)/shard_map/pallas_call | solution.py:75
  123.9 3.2 %reduce_sum.45.refs_0_ = f32[4,48,1024]{2,1,0:T(8,128)} reduce(f32[4,4,48,1024]{3,2,1,0:T(8,128)} %get-tuple-element.11, f32[]{:T(128)} %constant.3.clone.1), dimensions={0}, to_apply=%region_0.0 | reduce | flops 589824 | bytes 3932164 | tf_op jit(solution)/shard_map/reduce_sum | solution.py:165
  127.1 3.2 %reduce_sum.46.refs_1_ = f32[4,48,1024]{2,1,0:T(8,128)} reduce(f32[4,4,48,1024]{3,2,1,0:T(8,128)} %get-tuple-element.12, f32[]{:T(128)} %constant.3.clone.1), dimensions={0}, to_apply=%region_1.0 | reduce | flops 589824 | bytes 3932164 | tf_op jit(solution)/shard_map/reduce_sum | solution.py:165
  130.3 17.0 %shard_map.65 = (f32[4,48,1024]{2,1,0:T(8,128)}, f32[4,48,1024]{2,1,0:T(8,128)}) custom-call(f32[4,48,1024]{2,1,0:T(8,128)} %reduce_sum.45.refs_0_, f32[4,48,1024]{2,1,0:T(8,128)} %reduce_sum.46.refs_1_), custom_call_target="tpu_custom_call" | custom-call | bytes 6291456 | tf_op jit(solution)/shard_map/pallas_call | solution.py:75
  147.3 1.2 reduce_sum.48
  148.5 1.2 reduce_sum.47
  149.8 0.1 copy.8
  149.9 0.0 reduce-scatter.2.cloned.1.call-done
  149.9 1.9 %fusion.4 = f32[8,12,8,128]{3,2,1,0:T(8,128)} fusion(f32[8,12,8,128]{3,2,1,0:T(8,128)S(1)} %bitcast.28, f32[1,64,1536]{2,1,0:T(8,128)} %reduce-scatter.2.cloned.1.call-done, f32[12]{0:T(128)S(1)} %dynamic_slice.7, f32[8,8,128]{2,1,0:T(8,128)S(1)} %broadcast_subtract_fusion), kind=kLoop, calls=%fused_computation.6 | loop fusion | flops 294912 | bytes 1212464 | tf_op jit(solution)/shard_map/div | solution.py:187
  (1 shorter events, 0.0 us)
Async XLA Ops:
  6.5 59.9 %copy-start = (bf16[1024,1024]{1,0:T(8,128)(2,1)S(1)}, bf16[1024,1024]{1,0:T(8,128)(2,1)}, u32[]{:S(2)}) copy-start(bf16[1024,1024]{1,0:T(8,128)(2,1)} %param.7) | copy-start | bytes 6291460
  6.5 59.9 %all-gather.2.cloned.1.call-start = ((), (), s32[]{:S(2)}) async-start(), calls=%async_computation.1 | async-start | bytes 3342336 | tf_op jit(solution)/shard_map/all_gather | solution.py:146
  8.4 141.5 %reduce-scatter.2.cloned.1.call-start = ((), (), s32[]{:S(2)}) async-start(), calls=%async_computation.2 | async-start | bytes 6684672 | tf_op jit(solution)/shard_map/reduce_scatter | solution.py:139
  65.3 0.7 copy-start.1
  65.3 0.8 copy-start.2
  65.3 0.8 copy-start.3
Sparse Core Ops, SparseCore 0:
  9.2 45.1 all-gather.1
  65.4 65.9 reduce-scatter.1

commit v4 on v3

--- a/solution.py
+++ b/solution.py
@@ -23,9 +23,15 @@
     return r, n_red, lambda pos: pos
 
 
+def _half(ref, which):
+    size = ref.shape[0] // 2
+    return ref.at[pl.ds(which * size, size)]
+
+
 def _exchange_kernel(jobs, n_in, n_out, n_red, *refs):
     ins, outs = refs[:n_in], refs[n_in:n_in + n_out]
-    send_sem, recv_sem, local_sem = refs[n_in + n_out:]
+    relays = refs[n_in + n_out:n_in + n_out + len(jobs)]
+    send_sem, recv_sem, local_sem = refs[n_in + n_out + len(jobs):]
     row = lax.axis_index("blk")
 
     barrier = pltpu.get_barrier_semaphore()
@@ -39,22 +45,30 @@
             count += 1
     pl.semaphore_wait(barrier, count)
 
-    def remote(j, pos, slot):
-        kind, si, src_view, di, dst_view = jobs[j]
-        _, _, red_of = _group(kind, n_red)
+    def copy(j, role, src, dst, pos):
+        _, _, red_of = _group(jobs[j][0], n_red)
         return pltpu.make_async_remote_copy(
-            src_ref=src_view(ins[si], pos),
-            dst_ref=dst_view(outs[di], slot),
-            send_sem=send_sem.at[j, pos],
-            recv_sem=recv_sem.at[j, slot],
+            src_ref=src,
+            dst_ref=dst,
+            send_sem=send_sem.at[j, role],
+            recv_sem=recv_sem.at[j, role],
             device_id=(row, red_of(pos)),
             device_id_type=MESH,
         )
 
-    for j, job in enumerate(jobs):
-        me, n, _ = _group(job[0], n_red)
-        for o in range(1, n):
-            remote(j, lax.rem(me + o, n), me).start()
+    started = []
+    for j, (kind, si, src_view, di, dst_view) in enumerate(jobs):
+        me, n, _ = _group(kind, n_red)
+        right, left, far = lax.rem(me + 1, n), lax.rem(me + n - 1, n), lax.rem(me + 2, n)
+        sends = [
+            copy(j, 0, src_view(ins[si], right), dst_view(outs[di], me), right),
+            copy(j, 1, src_view(ins[si], left), dst_view(outs[di], me), left),
+            copy(j, 2, _half(src_view(ins[si], far), 0), relays[j].at[0], right),
+            copy(j, 3, _half(src_view(ins[si], far), 1), relays[j].at[1], left),
+        ]
+        for c in sends:
+            c.start()
+        started.append(sends)
     for j, (kind, si, src_view, di, dst_view) in enumerate(jobs):
         me, n, _ = _group(kind, n_red)
         local = pltpu.make_async_copy(
@@ -62,24 +76,41 @@
         )
         local.start()
         local.wait()
-    for j, job in enumerate(jobs):
-        me, n, _ = _group(job[0], n_red)
-        for o in range(1, n):
-            g = lax.rem(me + o, n)
-            remote(j, g, g).wait()
-
-
-def _exchange(jobs, srcs, out_shapes, n_red, collective_id):
+    for j, (kind, si, src_view, di, dst_view) in enumerate(jobs):
+        me, n, _ = _group(kind, n_red)
+        right, left = lax.rem(me + 1, n), lax.rem(me + n - 1, n)
+        to_right = copy(j, 4, relays[j].at[0], _half(dst_view(outs[di], left), 0), right)
+        to_left = copy(j, 5, relays[j].at[1], _half(dst_view(outs[di], right), 1), left)
+        copy(j, 2, relays[j].at[0], relays[j].at[0], right).wait_recv()
+        to_right.start()
+        copy(j, 3, relays[j].at[1], relays[j].at[1], left).wait_recv()
+        to_left.start()
+        started[j] += [to_right, to_left]
+    for j, (kind, si, src_view, di, dst_view) in enumerate(jobs):
+        me, n, _ = _group(kind, n_red)
+        right, left, far = lax.rem(me + 1, n), lax.rem(me + n - 1, n), lax.rem(me + 2, n)
+        for c in started[j]:
+            c.wait_send()
+        copy(j, 0, src_view(ins[si], me), dst_view(outs[di], left), left).wait_recv()
+        copy(j, 1, src_view(ins[si], me), dst_view(outs[di], right), right).wait_recv()
+        copy(j, 4, relays[j].at[0], _half(dst_view(outs[di], far), 0), left).wait_recv()
+        copy(j, 5, relays[j].at[1], _half(dst_view(outs[di], far), 1), right).wait_recv()
+
+
+def _exchange(jobs, srcs, out_shapes, units, n_red, collective_id):
     nbytes = sum(s.size * s.dtype.itemsize for s in srcs)
-    nmax = max(_group_size(job[0], n_red) for job in jobs)
+    relay_shapes = [
+        pltpu.VMEM((2, unit[0] // 2) + tuple(unit[1:]), srcs[job[1]].dtype)
+        for job, unit in zip(jobs, units)
+    ]
     return pl.pallas_call(
         functools.partial(_exchange_kernel, tuple(jobs), len(srcs), len(out_shapes), n_red),
         out_shape=tuple(jax.ShapeDtypeStruct(s, d) for s, d in out_shapes),
         in_specs=[pl.BlockSpec(memory_space=pl.ANY)] * len(srcs),
         out_specs=tuple(pl.BlockSpec(memory_space=pl.ANY) for _ in out_shapes),
-        scratch_shapes=[
-            pltpu.SemaphoreType.DMA((len(jobs), nmax)),
-            pltpu.SemaphoreType.DMA((len(jobs), nmax)),
+        scratch_shapes=relay_shapes + [
+            pltpu.SemaphoreType.DMA((len(jobs), 6)),
+            pltpu.SemaphoreType.DMA((len(jobs), 6)),
             pltpu.SemaphoreType.DMA((len(jobs),)),
         ],
         compiler_params=pltpu.CompilerParams(collective_id=collective_id, has_side_effects=True),
@@ -120,6 +151,7 @@
         ],
         [swapped],
         [((NY, part, width), bf), ((n_x, part, width), bf)],
+        [(part, width), (part, width)],
         n_red,
         0,
     )
@@ -130,6 +162,7 @@
         ],
         [near_a, near_b],
         [((n_x, NY, 2 * part, width), bf)],
+        [(NY, part, width), (n_x, part, width)],
         n_red,
         3,
     )
@@ -157,6 +190,7 @@
         ],
         [product],
         [((NY, n_x, half, cols), jnp.float32), ((n_x, NY, half, cols), jnp.float32)],
+        [(n_x, half, cols), (NY, half, cols)],
         n_red,
         1,
     )
@@ -164,6 +198,7 @@
         [("x", 0, _slot, 0, _slot), ("y", 1, _slot, 1, _slot)],
         [jnp.sum(first_a, axis=0), jnp.sum(first_b, axis=0)],
         [((n_x, half, cols), jnp.float32), ((NY, half, cols), jnp.float32)],
+        [(half, cols), (half, cols)],
         n_red,
         2,
     )

time: 159 us -> 182 us (1.14)
  Pallas kernels: 114 us -> 137 us
    pallas_call x4, Pallas kernels: 114 us -> 137 us  [_exchange(): pl.pallas_call(functools.partial(_exchange_kernel, tuple(jobs), len(srcs)...]
  transfers between devices with their start and end apart: 2 -> 2, of which waited for: 0 -> 0; matrix products, arithmetic and copies ran while one was open for 17% -> 15% of each run, Pallas kernels for 72% -> 76%
where the time goes in v4:
time: 182 us; the launch traced here: 181 us
  Pallas kernels  137 us (75%)
  matrix products  16.9 us (9%)
  between operations  13.5 us (7%)
  other arithmetic  10.9 us (6%)
  local copies, waits for them, and re-layouts  2.71 us (1%)
    pallas_call x4, Pallas kernels, _exchange(): pl.pallas_call(functools.partial(_exchange_kernel, tuple(jobs), len(srcs)...  137 us
    dot_general x1, matrix products, shards(): product = jnp.dot(operand, cycle_ints, preferred_element_type=jnp.float32)  9.73 us
    dot_general x1, matrix products, shards(): jnp.dot(shard_piece.reshape(n_blk * rows, -1), ladder_ints, preferred_ele...  7.21 us
  transfers between devices with their start and end apart: 2, of which 0 were waited for; matrix products, arithmetic and copies ran while one was open for 15% of the time, Pallas kernels for 76%

profile of v4, /device:TPU:1, one launch (start us, length us, event | category | flops | bytes accessed | tf_op | source)
XLA Modules:
  0.0 180.7 jit_solution(5325563883444067231)
XLA Ops:
  6.5 0.0 copy-start
  6.5 0.0 all-gather.2.cloned.1.call-start
  6.5 1.8 %all_gather_reshape.3 = bf16[1,96,1024]{2,1,0:T(8,128)(2,1)} reshape(bf16[8,12,8,128]{3,2,1,0:T(8,128)(2,1)} %param.6) | data formatting | bytes 393216 | tf_op jit(solution)/shard_map/all_gather;reshape | solution.py:179
  8.4 0.0 all-gather.2.cloned.1.call-update
  8.4 0.0 reduce-scatter.2.cloned.1.call-start
  8.5 16.5 %shard_map.66 = (bf16[4,32,1536]{2,1,0:T(8,128)(2,1)}, bf16[4,32,1536]{2,1,0:T(8,128)(2,1)}) custom-call(bf16[64,1536]{1,0:T(8,128)(2,1)} %bitcast.29), custom_call_target="tpu_custom_call" | custom-call | bytes 786432 | tf_op jit(solution)/shard_map/pallas_call | solution.py:106
  24.9 38.5 %shard_map.67 = bf16[4,4,64,1536]{3,2,1,0:T(8,128)(2,1)} custom-call(bf16[4,32,1536]{2,1,0:T(8,128)(2,1)} %get-tuple-element.15.refs_0_, bf16[4,32,1536]{2,1,0:T(8,128)(2,1)} %get-tuple-element.16.refs_1_), custom_call_target="tpu_custom_call" | custom-call | bytes 3145728 | tf_op jit(solution)/shard_map/pallas_call | solution.py:106
  63.4 9.7 %fusion = f32[16,64,1536]{2,1,0:T(8,128)} fusion(bf16[16,64,1536]{2,1,0:T(8,128)(2,1)} %bitcast.27, bf16[1536,1536]{1,0:T(8,128)(2,1)} %param.8), kind=kOutput, calls=%fused_computation | convolution fusion | flops 4831838208 | bytes 14155776 | tf_op jit(solution)/shard_map/dot_general | solution.py:170
  73.2 0.0 copy-start.1
  73.2 0.0 copy-start.2
  73.2 0.0 copy-start.3
  73.2 0.0 reduce-scatter.2.cloned.1.call-update
  73.2 0.6 copy-done.1
  73.9 0.1 dynamic_slice.7
  73.9 0.0 copy-done.2
  73.9 0.1 dynamic_slice.6
  74.0 0.0 copy-done.3
  74.0 0.2 select_reduce_fusion
  74.2 0.1 broadcast_add_fusion
  74.3 0.1 broadcast_subtract_fusion
  74.3 0.0 all-gather.2.cloned.1.call-done
  74.3 0.0 copy-done
  74.3 7.2 %fusion.2.refs_0_ = f32[4,4,96,1024]{3,2,1,0:T(8,128)} fusion(bf16[4,4,96,1024]{3,2,1,0:T(8,128)(2,1)} %bitcast.30, bf16[1024,1024]{1,0:T(8,128)(2,1)S(1)} %copy-done), kind=kOutput, calls=%fused_computation.2 | convolution fusion | flops 3221225472 | bytes 11534336 | tf_op jit(solution)/shard_map/dot_general | solution.py:180
  81.6 62.1 %shard_map.64 = (f32[4,4,48,1024]{3,2,1,0:T(8,128)}, f32[4,4,48,1024]{3,2,1,0:T(8,128)}) custom-call(f32[4,4,96,1024]{3,2,1,0:T(8,128)} %fusion.2.refs_0_), custom_call_target="tpu_custom_call" | custom-call | bytes 25165824 | tf_op jit(solution)/shard_map/pallas_call | solution.py:106
  143.7 3.2 %reduce_sum.45.refs_0_ = f32[4,48,1024]{2,1,0:T(8,128)} reduce(f32[4,4,48,1024]{3,2,1,0:T(8,128)} %get-tuple-element.11, f32[]{:T(128)} %constant.3.clone.1), dimensions={0}, to_apply=%region_0.0 | reduce | flops 589824 | bytes 3932164 | tf_op jit(solution)/shard_map/reduce_sum | solution.py:199
  146.9 3.1 %reduce_sum.46.refs_1_ = f32[4,48,1024]{2,1,0:T(8,128)} reduce(f32[4,4,48,1024]{3,2,1,0:T(8,128)} %get-tuple-element.12, f32[]{:T(128)} %constant.3.clone.1), dimensions={0}, to_apply=%region_1.0 | reduce | flops 589824 | bytes 3932164 | tf_op jit(solution)/shard_map/reduce_sum | solution.py:199
  150.0 19.4 %shard_map.65 = (f32[4,48,1024]{2,1,0:T(8,128)}, f32[4,48,1024]{2,1,0:T(8,128)}) custom-call(f32[4,48,1024]{2,1,0:T(8,128)} %reduce_sum.45.refs_0_, f32[4,48,1024]{2,1,0:T(8,128)} %reduce_sum.46.refs_1_), custom_call_target="tpu_custom_call" | custom-call | bytes 6291456 | tf_op jit(solution)/shard_map/pallas_call | solution.py:106
  169.4 1.2 reduce_sum.48
  170.6 1.2 reduce_sum.47
  171.9 0.1 copy.8
  171.9 0.0 reduce-scatter.2.cloned.1.call-done
  172.0 1.9 %fusion.4 = f32[8,12,8,128]{3,2,1,0:T(8,128)} fusion(f32[8,12,8,128]{3,2,1,0:T(8,128)S(1)} %bitcast.28, f32[1,64,1536]{2,1,0:T(8,128)} %reduce-scatter.2.cloned.1.call-done, f32[12]{0:T(128)S(1)} %dynamic_slice.7, f32[8,8,128]{2,1,0:T(8,128)S(1)} %broadcast_subtract_fusion), kind=kLoop, calls=%fused_computation.6 | loop fusion | flops 294912 | bytes 1212464 | tf_op jit(solution)/shard_map/div | solution.py:222
  (1 shorter events, 0.0 us)
Async XLA Ops:
  6.5 67.8 %copy-start = (bf16[1024,1024]{1,0:T(8,128)(2,1)S(1)}, bf16[1024,1024]{1,0:T(8,128)(2,1)}, u32[]{:S(2)}) copy-start(bf16[1024,1024]{1,0:T(8,128)(2,1)} %param.7) | copy-start | bytes 6291460
  6.5 67.8 %all-gather.2.cloned.1.call-start = ((), (), s32[]{:S(2)}) async-start(), calls=%async_computation.1 | async-start | bytes 3342336 | tf_op jit(solution)/shard_map/all_gather | solution.py:179
  8.4 163.6 %reduce-scatter.2.cloned.1.call-start = ((), (), s32[]{:S(2)}) async-start(), calls=%async_computation.2 | async-start | bytes 6684672 | tf_op jit(solution)/shard_map/reduce_scatter | solution.py:172
  73.2 0.7 copy-start.1
  73.2 0.8 copy-start.2
  73.2 0.8 copy-start.3
Sparse Core Ops, SparseCore 0:
  9.2 45.1 all-gather.1
  73.3 64.4 reduce-scatter.1

commit v5 on v3

--- a/solution.py
+++ b/solution.py
@@ -8,6 +8,7 @@
 from jax.sharding import PartitionSpec as P
 
 MESH = pl.DeviceIdType.MESH
+PIECES = 2
 
 
 NY = 4
@@ -39,22 +40,27 @@
             count += 1
     pl.semaphore_wait(barrier, count)
 
-    def remote(j, pos, slot):
+    def remote(j, pos, slot, piece=None):
         kind, si, src_view, di, dst_view = jobs[j]
         _, _, red_of = _group(kind, n_red)
+        src, dst = src_view(ins[si], pos), dst_view(outs[di], slot)
+        if piece is not None:
+            size = src.shape[0] // PIECES
+            src, dst = src.at[pl.ds(piece * size, size)], dst.at[pl.ds(piece * size, size)]
         return pltpu.make_async_remote_copy(
-            src_ref=src_view(ins[si], pos),
-            dst_ref=dst_view(outs[di], slot),
+            src_ref=src,
+            dst_ref=dst,
             send_sem=send_sem.at[j, pos],
             recv_sem=recv_sem.at[j, slot],
             device_id=(row, red_of(pos)),
             device_id_type=MESH,
         )
 
-    for j, job in enumerate(jobs):
-        me, n, _ = _group(job[0], n_red)
-        for o in range(1, n):
-            remote(j, lax.rem(me + o, n), me).start()
+    for piece in range(PIECES):
+        for j, job in enumerate(jobs):
+            me, n, _ = _group(job[0], n_red)
+            for o in range(1, n):
+                remote(j, lax.rem(me + o, n), me, piece).start()
     for j, (kind, si, src_view, di, dst_view) in enumerate(jobs):
         me, n, _ = _group(kind, n_red)
         local = pltpu.make_async_copy(

time: 159 us -> 159 us (level)
  no operation moved by 1% of the time
where the time goes in v5:
time: 159 us
  Pallas kernels  114 us (72%)
  matrix products  16.9 us (11%)
  between operations  13.5 us (8%)
  other arithmetic  11 us (7%)
  local copies, waits for them, and re-layouts  2.71 us (2%)
    pallas_call x4, Pallas kernels, _exchange(): pl.pallas_call(functools.partial(_exchange_kernel, tuple(jobs), len(srcs)...  114 us
    dot_general x1, matrix products, shards(): product = jnp.dot(operand, cycle_ints, preferred_element_type=jnp.float32)  9.73 us
    dot_general x1, matrix products, shards(): jnp.dot(shard_piece.reshape(n_blk * rows, -1), ladder_ints, preferred_ele...  7.21 us
    reduce_sum x1, other arithmetic, shards(): jnp.sum(first_b, axis=0)  3.19 us
    reduce_sum x1, other arithmetic, shards(): jnp.sum(first_a, axis=0)  3.18 us
  transfers between devices with their start and end apart: 2, of which 0 were waited for; matrix products, arithmetic and copies ran while one was open for 17% of the time, Pallas kernels for 72%

profile of v5, /device:TPU:1, one launch (start us, length us, event | category | flops | bytes accessed | tf_op | source)
XLA Modules:
  0.0 158.6 jit_solution(4779983231320305099)
XLA Ops:
  6.5 0.0 copy-start
  6.5 0.0 all-gather.2.cloned.1.call-start
  6.5 1.8 %all_gather_reshape.3 = bf16[1,96,1024]{2,1,0:T(8,128)(2,1)} reshape(bf16[8,12,8,128]{3,2,1,0:T(8,128)(2,1)} %param.6) | data formatting | bytes 393216 | tf_op jit(solution)/shard_map/all_gather;reshape | solution.py:152
  8.4 0.0 all-gather.2.cloned.1.call-update
  8.4 0.0 reduce-scatter.2.cloned.1.call-start
  8.5 12.3 %shard_map.66 = (bf16[4,32,1536]{2,1,0:T(8,128)(2,1)}, bf16[4,32,1536]{2,1,0:T(8,128)(2,1)}) custom-call(bf16[64,1536]{1,0:T(8,128)(2,1)} %bitcast.29), custom_call_target="tpu_custom_call" | custom-call | bytes 786432 | tf_op jit(solution)/shard_map/pallas_call | solution.py:81
  20.7 34.8 %shard_map.67 = bf16[4,4,64,1536]{3,2,1,0:T(8,128)(2,1)} custom-call(bf16[4,32,1536]{2,1,0:T(8,128)(2,1)} %get-tuple-element.15.refs_0_, bf16[4,32,1536]{2,1,0:T(8,128)(2,1)} %get-tuple-element.16.refs_1_), custom_call_target="tpu_custom_call" | custom-call | bytes 3145728 | tf_op jit(solution)/shard_map/pallas_call | solution.py:81
  55.5 9.7 %fusion = f32[16,64,1536]{2,1,0:T(8,128)} fusion(bf16[16,64,1536]{2,1,0:T(8,128)(2,1)} %bitcast.27, bf16[1536,1536]{1,0:T(8,128)(2,1)} %param.8), kind=kOutput, calls=%fused_computation | convolution fusion | flops 4831838208 | bytes 14155776 | tf_op jit(solution)/shard_map/dot_general | solution.py:143
  65.3 0.0 copy-start.1
  65.3 0.0 copy-start.2
  65.3 0.0 copy-start.3
  65.3 0.0 reduce-scatter.2.cloned.1.call-update
  65.3 0.6 copy-done.1
  66.0 0.1 dynamic_slice.7
  66.0 0.0 copy-done.2
  66.0 0.1 dynamic_slice.6
  66.1 0.0 copy-done.3
  66.1 0.2 select_reduce_fusion
  66.3 0.1 broadcast_add_fusion
  66.4 0.1 broadcast_subtract_fusion
  66.4 0.0 all-gather.2.cloned.1.call-done
  66.4 0.0 copy-done
  66.5 7.2 %fusion.2.refs_0_ = f32[4,4,96,1024]{3,2,1,0:T(8,128)} fusion(bf16[4,4,96,1024]{3,2,1,0:T(8,128)(2,1)} %bitcast.30, bf16[1024,1024]{1,0:T(8,128)(2,1)S(1)} %copy-done), kind=kOutput, calls=%fused_computation.2 | convolution fusion | flops 3221225472 | bytes 11534336 | tf_op jit(solution)/shard_map/dot_general | solution.py:153
  73.7 50.3 %shard_map.64 = (f32[4,4,48,1024]{3,2,1,0:T(8,128)}, f32[4,4,48,1024]{3,2,1,0:T(8,128)}) custom-call(f32[4,4,96,1024]{3,2,1,0:T(8,128)} %fusion.2.refs_0_), custom_call_target="tpu_custom_call" | custom-call | bytes 25165824 | tf_op jit(solution)/shard_map/pallas_call | solution.py:81
  123.9 3.2 %reduce_sum.45.refs_0_ = f32[4,48,1024]{2,1,0:T(8,128)} reduce(f32[4,4,48,1024]{3,2,1,0:T(8,128)} %get-tuple-element.11, f32[]{:T(128)} %constant.3.clone.1), dimensions={0}, to_apply=%region_0.0 | reduce | flops 589824 | bytes 3932164 | tf_op jit(solution)/shard_map/reduce_sum | solution.py:171
  127.1 3.2 %reduce_sum.46.refs_1_ = f32[4,48,1024]{2,1,0:T(8,128)} reduce(f32[4,4,48,1024]{3,2,1,0:T(8,128)} %get-tuple-element.12, f32[]{:T(128)} %constant.3.clone.1), dimensions={0}, to_apply=%region_1.0 | reduce | flops 589824 | bytes 3932164 | tf_op jit(solution)/shard_map/reduce_sum | solution.py:171
  130.3 17.0 %shard_map.65 = (f32[4,48,1024]{2,1,0:T(8,128)}, f32[4,48,1024]{2,1,0:T(8,128)}) custom-call(f32[4,48,1024]{2,1,0:T(8,128)} %reduce_sum.45.refs_0_, f32[4,48,1024]{2,1,0:T(8,128)} %reduce_sum.46.refs_1_), custom_call_target="tpu_custom_call" | custom-call | bytes 6291456 | tf_op jit(solution)/shard_map/pallas_call | solution.py:81
  147.4 1.2 reduce_sum.48
  148.6 1.2 reduce_sum.47
  149.8 0.1 copy.8
  149.9 0.0 reduce-scatter.2.cloned.1.call-done
  149.9 1.9 %fusion.4 = f32[8,12,8,128]{3,2,1,0:T(8,128)} fusion(f32[8,12,8,128]{3,2,1,0:T(8,128)S(1)} %bitcast.28, f32[1,64,1536]{2,1,0:T(8,128)} %reduce-scatter.2.cloned.1.call-done, f32[12]{0:T(128)S(1)} %dynamic_slice.7, f32[8,8,128]{2,1,0:T(8,128)S(1)} %broadcast_subtract_fusion), kind=kLoop, calls=%fused_computation.6 | loop fusion | flops 294912 | bytes 1212464 | tf_op jit(solution)/shard_map/div | solution.py:193
  (1 shorter events, 0.0 us)
Async XLA Ops:
  6.5 59.9 %copy-start = (bf16[1024,1024]{1,0:T(8,128)(2,1)S(1)}, bf16[1024,1024]{1,0:T(8,128)(2,1)}, u32[]{:S(2)}) copy-start(bf16[1024,1024]{1,0:T(8,128)(2,1)} %param.7) | copy-start | bytes 6291460
  6.5 59.9 %all-gather.2.cloned.1.call-start = ((), (), s32[]{:S(2)}) async-start(), calls=%async_computation.1 | async-start | bytes 3342336 | tf_op jit(solution)/shard_map/all_gather | solution.py:152
  8.4 141.5 %reduce-scatter.2.cloned.1.call-start = ((), (), s32[]{:S(2)}) async-start(), calls=%async_computation.2 | async-start | bytes 6684672 | tf_op jit(solution)/shard_map/reduce_scatter | solution.py:145
  65.3 0.7 copy-start.1
  65.3 0.8 copy-start.2
  65.3 0.8 copy-start.3
Sparse Core Ops, SparseCore 0:
  9.2 45.1 all-gather.1
  65.4 65.9 reduce-scatter.1

commit v6 on v5

--- a/solution.py
+++ b/solution.py
@@ -8,7 +8,7 @@
 from jax.sharding import PartitionSpec as P
 
 MESH = pl.DeviceIdType.MESH
-PIECES = 2
+PIECES = 1
 
 
 NY = 4
@@ -73,6 +73,111 @@
         for o in range(1, n):
             g = lax.rem(me + o, n)
             remote(j, g, g).wait()
+
+
+def _gather_kernel(n_red, src_ref, out_ref, send_sem, recv_sem, local_sem):
+    row = lax.axis_index("blk")
+    ym, ny, red_y = _group("y", n_red)
+    xm, nx, red_x = _group("x", n_red)
+    part = src_ref.shape[0] // 2
+    first, second = pl.ds(0, part), pl.ds(part, part)
+
+    barrier = pltpu.get_barrier_semaphore()
+    for o in range(1, ny):
+        pl.semaphore_signal(barrier, inc=1, device_id=(row, red_y(lax.rem(ym + o, ny))), device_id_type=MESH)
+    for o in range(1, nx):
+        pl.semaphore_signal(barrier, inc=1, device_id=(row, red_x(lax.rem(xm + o, nx))), device_id_type=MESH)
+    pl.semaphore_wait(barrier, ny - 1 + nx - 1)
+
+    def copy(src, dst, stage, pos, dev):
+        return pltpu.make_async_remote_copy(
+            src_ref=src,
+            dst_ref=dst,
+            send_sem=send_sem.at[stage, pos],
+            recv_sem=recv_sem.at[stage, pos],
+            device_id=(row, dev),
+            device_id_type=MESH,
+        )
+
+    sent = []
+    for o in range(1, ny):
+        g = lax.rem(ym + o, ny)
+        c = pltpu.make_async_remote_copy(
+            src_ref=src_ref.at[first], dst_ref=out_ref.at[xm, ym, first],
+            send_sem=send_sem.at[0, g], recv_sem=recv_sem.at[0, ym],
+            device_id=(row, red_y(g)), device_id_type=MESH,
+        )
+        c.start()
+        sent.append(c)
+    for o in range(1, nx):
+        g = lax.rem(xm + o, nx)
+        c = pltpu.make_async_remote_copy(
+            src_ref=src_ref.at[second], dst_ref=out_ref.at[xm, ym, second],
+            send_sem=send_sem.at[1, g], recv_sem=recv_sem.at[1, xm],
+            device_id=(row, red_x(g)), device_id_type=MESH,
+        )
+        c.start()
+        sent.append(c)
+    own = [
+        pltpu.make_async_copy(src_ref.at[first], out_ref.at[xm, ym, first], local_sem.at[0]),
+        pltpu.make_async_copy(src_ref.at[second], out_ref.at[xm, ym, second], local_sem.at[1]),
+    ]
+    for c in own:
+        c.start()
+    for c in own:
+        c.wait()
+
+    for o in range(1, ny):
+        g = lax.rem(ym + o, ny)
+        copy(src_ref.at[first], out_ref.at[xm, g, first], 0, g, red_y(g)).wait_recv()
+    for o in range(1, nx):
+        g = lax.rem(xm + o, nx)
+        c = pltpu.make_async_remote_copy(
+            src_ref=out_ref.at[xm, :, first], dst_ref=out_ref.at[xm, :, first],
+            send_sem=send_sem.at[2, g], recv_sem=recv_sem.at[2, xm],
+            device_id=(row, red_x(g)), device_id_type=MESH,
+        )
+        c.start()
+        sent.append(c)
+    for o in range(1, nx):
+        g = lax.rem(xm + o, nx)
+        copy(src_ref.at[second], out_ref.at[g, ym, second], 1, g, red_x(g)).wait_recv()
+    for o in range(1, ny):
+        g = lax.rem(ym + o, ny)
+        c = pltpu.make_async_remote_copy(
+            src_ref=out_ref.at[:, ym, second], dst_ref=out_ref.at[:, ym, second],
+            send_sem=send_sem.at[3, g], recv_sem=recv_sem.at[3, ym],
+            device_id=(row, red_y(g)), device_id_type=MESH,
+        )
+        c.start()
+        sent.append(c)
+
+    for c in sent:
+        c.wait_send()
+    for o in range(1, nx):
+        g = lax.rem(xm + o, nx)
+        copy(out_ref.at[g, :, first], out_ref.at[g, :, first], 2, g, red_x(g)).wait_recv()
+    for o in range(1, ny):
+        g = lax.rem(ym + o, ny)
+        copy(out_ref.at[:, g, second], out_ref.at[:, g, second], 3, g, red_y(g)).wait_recv()
+
+
+def _gather(block, n_red, collective_id):
+    n_x = n_red // NY
+    nbytes = block.size * block.dtype.itemsize
+    return pl.pallas_call(
+        functools.partial(_gather_kernel, n_red),
+        out_shape=jax.ShapeDtypeStruct((n_x, NY) + block.shape, block.dtype),
+        in_specs=[pl.BlockSpec(memory_space=pl.ANY)],
+        out_specs=pl.BlockSpec(memory_space=pl.ANY),
+        scratch_shapes=[
+            pltpu.SemaphoreType.DMA((4, max(n_x, NY))),
+            pltpu.SemaphoreType.DMA((4, max(n_x, NY))),
+            pltpu.SemaphoreType.DMA((2,)),
+        ],
+        compiler_params=pltpu.CompilerParams(collective_id=collective_id, has_side_effects=True),
+        cost_estimate=pl.CostEstimate(flops=0, bytes_accessed=2 * n_red * nbytes, transcendentals=0),
+    )(block)
 
 
 def _exchange(jobs, srcs, out_shapes, n_red, collective_id):
@@ -116,29 +221,7 @@
     swapped = jnp.transpose(amplitudes, (0, 2, 1, 3)).reshape(
         slab_rows * vir_local, occ_local * virt_width
     )
-    width = swapped.shape[1]
-    part = swapped.shape[0] // 2
-    bf = swapped.dtype
-    near_a, near_b = _exchange(
-        [
-            ("y", 0, lambda ref, pos: ref.at[pl.ds(0, part)], 0, _slot),
-            ("x", 0, lambda ref, pos: ref.at[pl.ds(part, part)], 1, _slot),
-        ],
-        [swapped],
-        [((NY, part, width), bf), ((n_x, part, width), bf)],
-        n_red,
-        0,
-    )
-    (gathered,) = _exchange(
-        [
-            ("x", 0, _whole, 0, lambda ref, slot: ref.at[slot, :, pl.ds(0, part)]),
-            ("y", 1, _whole, 0, lambda ref, slot: ref.at[:, slot, pl.ds(part, part)]),
-        ],
-        [near_a, near_b],
-        [((n_x, NY, 2 * part, width), bf)],
-        n_red,
-        3,
-    )
+    gathered = _gather(swapped, n_red, 0)
     operand = gathered.reshape(n_red * slab_rows * vir_local, occ_local * virt_width)
     product = jnp.dot(operand, cycle_ints, preferred_element_type=jnp.float32)
     product = product.reshape(n_red, slab_rows * vir_local, cycle_ints.shape[1])

time: 159 us -> 149 us (0.937)
  Pallas kernels: 114 us -> 102 us
  waiting for transfers between devices: 0.06 us -> 3.33 us
    pallas_call x4 -> x2, Pallas kernels: 114 us -> 70.3 us  [_exchange(): pl.pallas_call(functools.partial(_exchange_kernel, tuple(jobs), len(srcs)...]
    pallas_call x0 -> x1, Pallas kernels: none -> 31.3 us  [_gather(): pl.pallas_call(functools.partial(_gather_kernel, n_red), out_shape=jax.Sh...]
    all_gather x1, waiting for transfers between devices: 0.01 us -> 3.28 us  [shards(): shard_piece = lax.all_gather(flat, 'blk', axis=0, tiled=False)]
  transfers between devices with their start and end apart: 2 -> 2, of which waited for: 0 -> 1; matrix products, arithmetic and copies ran while one was open for 17% -> 18% of each run, Pallas kernels for 72% -> 68%
where the time goes in v6:
time: 149 us
  Pallas kernels  102 us (68%)
  matrix products  17 us (11%)
  between operations  13.5 us (9%)
  other arithmetic  11 us (7%)
  waiting for transfers between devices  3.33 us (2%)
  local copies, waits for them, and re-layouts  2.71 us (2%)
    pallas_call x2, Pallas kernels, _exchange(): pl.pallas_call(functools.partial(_exchange_kernel, tuple(jobs), len(srcs)...  70.3 us
    pallas_call x1, Pallas kernels, _gather(): pl.pallas_call(functools.partial(_gather_kernel, n_red), out_shape=jax.Sh...  31.3 us
    dot_general x1, matrix products, shards(): product = jnp.dot(operand, cycle_ints, preferred_element_type=jnp.float32)  9.79 us
    dot_general x1, matrix products, shards(): jnp.dot(shard_piece.reshape(n_blk * rows, -1), ladder_ints, preferred_ele...  7.19 us
    all_gather x1, waiting for transfers between devices, shards(): shard_piece = lax.all_gather(flat, 'blk', axis=0, tiled=False)  3.28 us
    reduce_sum x1, other arithmetic, shards(): jnp.sum(first_b, axis=0)  3.17 us
    reduce_sum x1, other arithmetic, shards(): jnp.sum(first_a, axis=0)  3.15 us
  transfers between devices with their start and end apart: 2, of which 1 were waited for; matrix products, arithmetic and copies ran while one was open for 18% of the time, Pallas kernels for 68%

profile of v6, /device:TPU:1, one launch (start us, length us, event | category | flops | bytes accessed | tf_op | source)
XLA Modules:
  0.0 149.1 jit_solution(2489601145627715295)
XLA Ops:
  6.5 0.0 copy-start
  6.5 0.0 all-gather.2.cloned.1.call-start
  6.5 1.8 %all_gather_reshape.3 = bf16[1,96,1024]{2,1,0:T(8,128)(2,1)} reshape(bf16[8,12,8,128]{3,2,1,0:T(8,128)(2,1)} %param.6) | data formatting | bytes 393216 | tf_op jit(solution)/shard_map/all_gather;reshape | solution.py:235
  8.4 0.0 all-gather.2.cloned.1.call-update
  8.4 0.0 reduce-scatter.2.cloned.1.call-start
  8.5 31.3 %shard_map.66 = bf16[4,4,64,1536]{3,2,1,0:T(8,128)(2,1)} custom-call(bf16[64,1536]{1,0:T(8,128)(2,1)} %bitcast.29), custom_call_target="tpu_custom_call" | custom-call | bytes 6291456 | tf_op jit(solution)/shard_map/pallas_call | solution.py:168
  39.8 9.8 %fusion = f32[16,64,1536]{2,1,0:T(8,128)} fusion(bf16[16,64,1536]{2,1,0:T(8,128)(2,1)} %bitcast.27, bf16[1536,1536]{1,0:T(8,128)(2,1)} %param.8), kind=kOutput, calls=%fused_computation | convolution fusion | flops 4831838208 | bytes 14155776 | tf_op jit(solution)/shard_map/dot_general | solution.py:226
  49.6 0.0 copy-start.1
  49.6 0.0 copy-start.2
  49.6 0.0 copy-start.3
  49.6 0.0 reduce-scatter.2.cloned.1.call-update
  49.6 0.6 copy-done.1
  50.2 0.1 dynamic_slice.7
  50.3 0.0 copy-done.2
  50.3 0.1 dynamic_slice.6
  50.4 0.0 copy-done.3
  50.4 0.2 select_reduce_fusion
  50.6 0.1 broadcast_add_fusion
  50.7 0.1 broadcast_subtract_fusion
  50.7 3.3 %all-gather.2.cloned.1.call-done = bf16[16,96,1024]{2,1,0:T(8,128)(2,1)} async-done(((bf16[1,96,1024]{2,1,0:T(8,128)(2,1)}), bf16[16,96,1024]{2,1,0:T(8,128)(2,1)}) %all-gather.2.cloned.1.call-update) | async-done | bytes 3145744 | tf_op jit(solution)/shard_map/all_gather | solution.py:235
  54.0 0.0 copy-done
  54.0 7.2 %fusion.2.refs_0_ = f32[4,4,96,1024]{3,2,1,0:T(8,128)} fusion(bf16[4,4,96,1024]{3,2,1,0:T(8,128)(2,1)} %bitcast.30, bf16[1024,1024]{1,0:T(8,128)(2,1)S(1)} %copy-done), kind=kOutput, calls=%fused_computation.2 | convolution fusion | flops 3221225472 | bytes 11534336 | tf_op jit(solution)/shard_map/dot_general | solution.py:236
  61.2 52.7 %shard_map.64 = (f32[4,4,48,1024]{3,2,1,0:T(8,128)}, f32[4,4,48,1024]{3,2,1,0:T(8,128)}) custom-call(f32[4,4,96,1024]{3,2,1,0:T(8,128)} %fusion.2.refs_0_), custom_call_target="tpu_custom_call" | custom-call | bytes 25165824 | tf_op jit(solution)/shard_map/pallas_call | solution.py:186
  113.9 3.2 %reduce_sum.45.refs_0_ = f32[4,48,1024]{2,1,0:T(8,128)} reduce(f32[4,4,48,1024]{3,2,1,0:T(8,128)} %get-tuple-element.9, f32[]{:T(128)} %constant.3.clone.1), dimensions={0}, to_apply=%region_0.0 | reduce | flops 589824 | bytes 3932164 | tf_op jit(solution)/shard_map/reduce_sum | solution.py:254
  117.1 3.2 %reduce_sum.46.refs_1_ = f32[4,48,1024]{2,1,0:T(8,128)} reduce(f32[4,4,48,1024]{3,2,1,0:T(8,128)} %get-tuple-element.10, f32[]{:T(128)} %constant.3.clone.1), dimensions={0}, to_apply=%region_1.0 | reduce | flops 589824 | bytes 3932164 | tf_op jit(solution)/shard_map/reduce_sum | solution.py:254
  120.2 17.6 %shard_map.65 = (f32[4,48,1024]{2,1,0:T(8,128)}, f32[4,48,1024]{2,1,0:T(8,128)}) custom-call(f32[4,48,1024]{2,1,0:T(8,128)} %reduce_sum.45.refs_0_, f32[4,48,1024]{2,1,0:T(8,128)} %reduce_sum.46.refs_1_), custom_call_target="tpu_custom_call" | custom-call | bytes 6291456 | tf_op jit(solution)/shard_map/pallas_call | solution.py:186
  137.8 1.2 reduce_sum.48
  139.0 1.2 reduce_sum.47
  140.3 0.1 copy.8
  140.3 0.0 reduce-scatter.2.cloned.1.call-done
  140.4 1.9 %fusion.4 = f32[8,12,8,128]{3,2,1,0:T(8,128)} fusion(f32[8,12,8,128]{3,2,1,0:T(8,128)S(1)} %bitcast.28, f32[1,64,1536]{2,1,0:T(8,128)} %reduce-scatter.2.cloned.1.call-done, f32[12]{0:T(128)S(1)} %dynamic_slice.7, f32[8,8,128]{2,1,0:T(8,128)S(1)} %broadcast_subtract_fusion), kind=kLoop, calls=%fused_computation.6 | loop fusion | flops 294912 | bytes 1212464 | tf_op jit(solution)/shard_map/div | solution.py:276
  (1 shorter events, 0.0 us)
Async XLA Ops:
  6.5 47.5 %copy-start = (bf16[1024,1024]{1,0:T(8,128)(2,1)S(1)}, bf16[1024,1024]{1,0:T(8,128)(2,1)}, u32[]{:S(2)}) copy-start(bf16[1024,1024]{1,0:T(8,128)(2,1)} %param.7) | copy-start | bytes 6291460
  6.5 47.5 %all-gather.2.cloned.1.call-start = ((), (), s32[]{:S(2)}) async-start(), calls=%async_computation.1 | async-start | bytes 3342336 | tf_op jit(solution)/shard_map/all_gather | solution.py:235
  8.4 132.0 %reduce-scatter.2.cloned.1.call-start = ((), (), s32[]{:S(2)}) async-start(), calls=%async_computation.2 | async-start | bytes 6684672 | tf_op jit(solution)/shard_map/reduce_scatter | solution.py:228
  49.6 0.7 copy-start.1
  49.6 0.8 copy-start.2
  49.6 0.8 copy-start.3
Sparse Core Ops, SparseCore 0:
  9.2 44.7 all-gather.1
  56.6 63.6 reduce-scatter.1

commit v7 on v6

--- a/solution.py
+++ b/solution.py
@@ -180,6 +180,111 @@
     )(block)
 
 
+def _reduce_kernel(n_red, prod_ref, out_ref, ra, rb, sa, sb, qa, qb, send1, recv1, send2, recv2, local_sem):
+    row = lax.axis_index("blk")
+    ym, ny, red_y = _group("y", n_red)
+    xm, nx, red_x = _group("x", n_red)
+    half = ra.shape[2]
+    first, second = pl.ds(0, half), pl.ds(half, half)
+
+    barrier = pltpu.get_barrier_semaphore()
+    for o in range(1, ny):
+        pl.semaphore_signal(barrier, inc=1, device_id=(row, red_y(lax.rem(ym + o, ny))), device_id_type=MESH)
+    for o in range(1, nx):
+        pl.semaphore_signal(barrier, inc=1, device_id=(row, red_x(lax.rem(xm + o, nx))), device_id_type=MESH)
+    pl.semaphore_wait(barrier, ny - 1 + nx - 1)
+
+    def copy(src, dst, send, recv, dev):
+        return pltpu.make_async_remote_copy(
+            src_ref=src, dst_ref=dst, send_sem=send, recv_sem=recv,
+            device_id=(row, dev), device_id_type=MESH,
+        )
+
+    sent = []
+    for o in range(1, ny):
+        g = lax.rem(ym + o, ny)
+        c = copy(prod_ref.at[:, g, first], ra.at[ym], send1.at[0, g], recv1.at[0, ym], red_y(g))
+        c.start()
+        sent.append(c)
+    for o in range(1, nx):
+        g = lax.rem(xm + o, nx)
+        c = copy(prod_ref.at[g, :, second], rb.at[xm], send1.at[1, g], recv1.at[1, xm], red_x(g))
+        c.start()
+        sent.append(c)
+    own_a = pltpu.make_async_copy(prod_ref.at[:, ym, first], ra.at[ym], local_sem.at[0])
+    own_b = pltpu.make_async_copy(prod_ref.at[xm, :, second], rb.at[xm], local_sem.at[1])
+    own_a.start()
+    own_b.start()
+
+    own_a.wait()
+    for o in range(1, ny):
+        g = lax.rem(ym + o, ny)
+        copy(prod_ref.at[:, g, first], ra.at[g], send1.at[0, g], recv1.at[0, g], red_y(g)).wait_recv()
+    for k in range(nx):
+        sa[k] = ra[0, k] + ra[1, k] + ra[2, k] + ra[3, k]
+    for o in range(1, nx):
+        g = lax.rem(xm + o, nx)
+        c = copy(sa.at[g], qa.at[xm], send2.at[0, g], recv2.at[0, xm], red_x(g))
+        c.start()
+        sent.append(c)
+
+    own_b.wait()
+    for o in range(1, nx):
+        g = lax.rem(xm + o, nx)
+        copy(prod_ref.at[g, :, second], rb.at[g], send1.at[1, g], recv1.at[1, g], red_x(g)).wait_recv()
+    for k in range(ny):
+        sb[k] = rb[0, k] + rb[1, k] + rb[2, k] + rb[3, k]
+    for o in range(1, ny):
+        g = lax.rem(ym + o, ny)
+        c = copy(sb.at[g], qb.at[ym], send2.at[1, g], recv2.at[1, ym], red_y(g))
+        c.start()
+        sent.append(c)
+
+    for c in sent:
+        c.wait_send()
+    total_a = sa[xm]
+    for o in range(1, nx):
+        g = lax.rem(xm + o, nx)
+        copy(sa.at[g], qa.at[g], send2.at[0, g], recv2.at[0, g], red_x(g)).wait_recv()
+        total_a = total_a + qa[g]
+    total_b = sb[ym]
+    for o in range(1, ny):
+        g = lax.rem(ym + o, ny)
+        copy(sb.at[g], qb.at[g], send2.at[1, g], recv2.at[1, g], red_y(g)).wait_recv()
+        total_b = total_b + qb[g]
+    out_ref[first] = total_a
+    out_ref[second] = total_b
+
+
+def _reduce(prod, n_red, collective_id):
+    n_x, n_y, rows, cols = prod.shape
+    half = rows // 2
+    f32 = jnp.float32
+    return pl.pallas_call(
+        functools.partial(_reduce_kernel, n_red),
+        out_shape=jax.ShapeDtypeStruct((rows, cols), f32),
+        in_specs=[pl.BlockSpec(memory_space=pl.ANY)],
+        out_specs=pl.BlockSpec(memory_space=pltpu.VMEM),
+        scratch_shapes=[
+            pltpu.VMEM((n_y, n_x, half, cols), f32),
+            pltpu.VMEM((n_x, n_y, half, cols), f32),
+            pltpu.VMEM((n_x, half, cols), f32),
+            pltpu.VMEM((n_y, half, cols), f32),
+            pltpu.VMEM((n_x, half, cols), f32),
+            pltpu.VMEM((n_y, half, cols), f32),
+            pltpu.SemaphoreType.DMA((2, max(n_x, n_y))),
+            pltpu.SemaphoreType.DMA((2, max(n_x, n_y))),
+            pltpu.SemaphoreType.DMA((2, max(n_x, n_y))),
+            pltpu.SemaphoreType.DMA((2, max(n_x, n_y))),
+            pltpu.SemaphoreType.DMA((2,)),
+        ],
+        compiler_params=pltpu.CompilerParams(collective_id=collective_id, has_side_effects=True),
+        cost_estimate=pl.CostEstimate(
+            flops=prod.size, bytes_accessed=2 * prod.size * 4, transcendentals=0
+        ),
+    )(prod)
+
+
 def _exchange(jobs, srcs, out_shapes, n_red, collective_id):
     nbytes = sum(s.size * s.dtype.itemsize for s in srcs)
     nmax = max(_group_size(job[0], n_red) for job in jobs)
@@ -238,25 +343,7 @@
     )
     cols = ladder_ints.shape[1]
     product = product.reshape(n_x, NY, rows, cols)
-    half = rows // 2
-    first_a, first_b = _exchange(
-        [
-            ("y", 0, lambda ref, pos: ref.at[:, pos, pl.ds(0, half)], 0, _slot),
-            ("x", 0, lambda ref, pos: ref.at[pos, :, pl.ds(half, half)], 1, _slot),
-        ],
-        [product],
-        [((NY, n_x, half, cols), jnp.float32), ((n_x, NY, half, cols), jnp.float32)],
-        n_red,
-        1,
-    )
-    second_a, second_b = _exchange(
-        [("x", 0, _slot, 0, _slot), ("y", 1, _slot, 1, _slot)],
-        [jnp.sum(first_a, axis=0), jnp.sum(first_b, axis=0)],
-        [((n_x, half, cols), jnp.float32), ((NY, half, cols), jnp.float32)],
-        n_red,
-        2,
-    )
-    ladder_own = jnp.concatenate([jnp.sum(second_a, axis=0), jnp.sum(second_b, axis=0)], axis=0)
+    ladder_own = _reduce(product, n_red, 1)
     ladder_own = ladder_own.reshape(slab_rows, occ_red, -1, virt_width)
 
     vir_block = cycle_own.shape[2]

time: 149 us -> 131 us (0.88); the launches traced: 149 us -> 129 us
  Pallas kernels: 102 us -> 82.3 us
  other arithmetic: 11 us -> 2.2 us
  waiting for transfers between devices: 3.33 us -> 10.1 us
    pallas_call x2 -> x1, Pallas kernels: 70.3 us -> 50.9 us  [_reduce(): pl.pallas_call(functools.partial(_reduce_kernel, n_red), out_shape=jax.Sh...]
    reduce_sum x4 -> x0, other arithmetic: 8.73 us -> none  [the longest x1 3.17 us: shards(): jnp.sum(first_b, axis=0)]
    reduce_scatter x1, waiting for transfers between devices: 0.02 us -> 6.75 us  [shards(): lax.psum_scatter(product, 'blk', scatter_dimension=0, tiled=True)[0]]
  transfers between devices with their start and end apart: 2 -> 2, of which waited for: 1 -> 2; matrix products, arithmetic and copies ran while one was open for 18% -> 14% of each run, Pallas kernels for 68% -> 64%
where the time goes in v7:
time: 131 us; the launch traced here: 129 us
  Pallas kernels  82.3 us (63%)
  matrix products  17 us (13%)
  between operations  13.4 us (10%)
  waiting for transfers between devices  10.1 us (8%)
  local copies, waits for them, and re-layouts  3.72 us (3%)
  other arithmetic  2.2 us (2%)
    pallas_call x1, Pallas kernels, _reduce(): pl.pallas_call(functools.partial(_reduce_kernel, n_red), out_shape=jax.Sh...  50.9 us
    pallas_call x1, Pallas kernels, _gather(): pl.pallas_call(functools.partial(_gather_kernel, n_red), out_shape=jax.Sh...  31.3 us
    dot_general x1, matrix products, shards(): product = jnp.dot(operand, cycle_ints, preferred_element_type=jnp.float32)  9.8 us
    dot_general x1, matrix products, shards(): jnp.dot(shard_piece.reshape(n_blk * rows, -1), ladder_ints, preferred_ele...  7.23 us
    reduce_scatter x1, waiting for transfers between devices, shards(): lax.psum_scatter(product, 'blk', scatter_dimension=0, tiled=True)[0]  6.75 us
    all_gather x1, waiting for transfers between devices, shards(): shard_piece = lax.all_gather(flat, 'blk', axis=0, tiled=False)  3.27 us
  transfers between devices with their start and end apart: 2, of which 2 were waited for; matrix products, arithmetic and copies ran while one was open for 14% of the time, Pallas kernels for 64%

profile of v7, /device:TPU:1, one launch (start us, length us, event | category | flops | bytes accessed | tf_op | source)
XLA Modules:
  0.0 128.7 jit_solution(17706013121002805627)
XLA Ops:
  6.5 0.0 copy-start
  6.5 0.0 all-gather.2.cloned.1.call-start
  6.5 1.8 %all_gather_reshape.3 = bf16[1,96,1024]{2,1,0:T(8,128)(2,1)} reshape(bf16[8,12,8,128]{3,2,1,0:T(8,128)(2,1)} %param.6) | data formatting | bytes 393216 | tf_op jit(solution)/shard_map/all_gather;reshape | solution.py:340
  8.4 0.0 all-gather.2.cloned.1.call-update
  8.4 0.0 reduce-scatter.2.cloned.1.call-start
  8.5 31.3 %shard_map.65 = bf16[4,4,64,1536]{3,2,1,0:T(8,128)(2,1)} custom-call(bf16[64,1536]{1,0:T(8,128)(2,1)} %bitcast.29), custom_call_target="tpu_custom_call" | custom-call | bytes 6291456 | tf_op jit(solution)/shard_map/pallas_call | solution.py:168
  39.8 9.8 %fusion = f32[16,64,1536]{2,1,0:T(8,128)} fusion(bf16[16,64,1536]{2,1,0:T(8,128)(2,1)} %bitcast.26, bf16[1536,1536]{1,0:T(8,128)(2,1)} %param.8), kind=kOutput, calls=%fused_computation | convolution fusion | flops 4831838208 | bytes 14155776 | tf_op jit(solution)/shard_map/dot_general | solution.py:331
  49.6 0.0 copy-start.1
  49.6 0.0 copy-start.2
  49.6 0.0 copy-start.3
  49.6 0.0 reduce-scatter.2.cloned.1.call-update
  49.6 0.6 copy-done.1
  50.3 0.1 dynamic_slice.7
  50.3 0.0 copy-done.2
  50.3 0.1 dynamic_slice.6
  50.4 0.0 copy-done.3
  50.4 0.2 select_reduce_fusion
  50.6 0.1 broadcast_add_fusion
  50.7 0.1 broadcast_subtract_fusion
  50.7 3.3 %all-gather.2.cloned.1.call-done = bf16[16,96,1024]{2,1,0:T(8,128)(2,1)} async-done(((bf16[1,96,1024]{2,1,0:T(8,128)(2,1)}), bf16[16,96,1024]{2,1,0:T(8,128)(2,1)}) %all-gather.2.cloned.1.call-update) | async-done | bytes 3145744 | tf_op jit(solution)/shard_map/all_gather | solution.py:340
  54.0 0.0 copy-done
  54.0 7.2 %fusion.2.prod_ref = f32[4,4,96,1024]{3,2,1,0:T(8,128)} fusion(bf16[4,4,96,1024]{3,2,1,0:T(8,128)(2,1)} %bitcast.30, bf16[1024,1024]{1,0:T(8,128)(2,1)S(1)} %copy-done), kind=kOutput, calls=%fused_computation.2 | convolution fusion | flops 3221225472 | bytes 11534336 | tf_op jit(solution)/shard_map/dot_general | solution.py:341
  61.2 50.9 %shard_map.64 = f32[96,1024]{1,0:T(8,128)} custom-call(f32[4,4,96,1024]{3,2,1,0:T(8,128)} %fusion.2.prod_ref), custom_call_target="tpu_custom_call" | custom-call | flops 1572864 | bytes 12582912 | tf_op jit(solution)/shard_map/pallas_call | solution.py:263
  112.2 1.1 copy.8
  113.3 6.8 %reduce-scatter.2.cloned.1.call-done = f32[1,64,1536]{2,1,0:T(8,128)} async-done(((f32[16,64,1536]{2,1,0:T(8,128)}), f32[1,64,1536]{2,1,0:T(8,128)}) %reduce-scatter.2.cloned.1.call-update) | async-done | bytes 393232 | tf_op jit(solution)/shard_map/reduce_scatter | solution.py:333
  120.0 1.9 %fusion.4 = f32[8,12,8,128]{3,2,1,0:T(8,128)} fusion(f32[8,12,8,128]{3,2,1,0:T(8,128)S(1)} %bitcast.28, f32[1,64,1536]{2,1,0:T(8,128)} %reduce-scatter.2.cloned.1.call-done, f32[12]{0:T(128)S(1)} %dynamic_slice.7, f32[8,8,128]{2,1,0:T(8,128)S(1)} %broadcast_subtract_fusion), kind=kLoop, calls=%fused_computation.5 | loop fusion | flops 294912 | bytes 1212464 | tf_op jit(solution)/shard_map/div | solution.py:363
Async XLA Ops:
  6.5 47.5 %copy-start = (bf16[1024,1024]{1,0:T(8,128)(2,1)S(1)}, bf16[1024,1024]{1,0:T(8,128)(2,1)}, u32[]{:S(2)}) copy-start(bf16[1024,1024]{1,0:T(8,128)(2,1)} %param.7) | copy-start | bytes 6291460
  6.5 47.5 %all-gather.2.cloned.1.call-start = ((), (), s32[]{:S(2)}) async-start(), calls=%async_computation.1 | async-start | bytes 3342336 | tf_op jit(solution)/shard_map/all_gather | solution.py:340
  8.4 111.6 %reduce-scatter.2.cloned.1.call-start = ((), (), s32[]{:S(2)}) async-start(), calls=%async_computation.2 | async-start | bytes 6684672 | tf_op jit(solution)/shard_map/reduce_scatter | solution.py:333
  49.6 0.7 copy-start.1
  49.6 0.8 copy-start.2
  49.6 0.8 copy-start.3
Sparse Core Ops, SparseCore 0:
  9.2 44.7 all-gather.1
  56.6 63.4 reduce-scatter.1

commit v8 on v7

--- a/solution.py
+++ b/solution.py
@@ -5,13 +5,18 @@
 from jax import lax
 from jax.experimental import pallas as pl
 from jax.experimental.pallas import tpu as pltpu
-from jax.sharding import PartitionSpec as P
+from jax.sharding import Mesh, PartitionSpec as P
 
 MESH = pl.DeviceIdType.MESH
 PIECES = 1
 
 
 NY = 4
+CORES = 2
+
+
+def _row():
+    return lax.axis_index("z"), lax.axis_index("core")
 
 
 def _group(kind, n_red):
@@ -27,7 +32,7 @@
 def _exchange_kernel(jobs, n_in, n_out, n_red, *refs):
     ins, outs = refs[:n_in], refs[n_in:n_in + n_out]
     send_sem, recv_sem, local_sem = refs[n_in + n_out:]
-    row = lax.axis_index("blk")
+    row = _row()
 
     barrier = pltpu.get_barrier_semaphore()
     count = 0
@@ -35,7 +40,7 @@
         me, n, red_of = _group(kind, n_red)
         for o in range(1, n):
             pl.semaphore_signal(
-                barrier, inc=1, device_id=(row, red_of(lax.rem(me + o, n))), device_id_type=MESH
+                barrier, inc=1, device_id=(*row, red_of(lax.rem(me + o, n))), device_id_type=MESH
             )
             count += 1
     pl.semaphore_wait(barrier, count)
@@ -52,7 +57,7 @@
             dst_ref=dst,
             send_sem=send_sem.at[j, pos],
             recv_sem=recv_sem.at[j, slot],
-            device_id=(row, red_of(pos)),
+            device_id=(*row, red_of(pos)),
             device_id_type=MESH,
         )
 
@@ -76,7 +81,7 @@
 
 
 def _gather_kernel(n_red, src_ref, out_ref, send_sem, recv_sem, local_sem):
-    row = lax.axis_index("blk")
+    row = _row()
     ym, ny, red_y = _group("y", n_red)
     xm, nx, red_x = _group("x", n_red)
     part = src_ref.shape[0] // 2
@@ -84,9 +89,9 @@
 
     barrier = pltpu.get_barrier_semaphore()
     for o in range(1, ny):
-        pl.semaphore_signal(barrier, inc=1, device_id=(row, red_y(lax.rem(ym + o, ny))), device_id_type=MESH)
-    for o in range(1, nx):
-        pl.semaphore_signal(barrier, inc=1, device_id=(row, red_x(lax.rem(xm + o, nx))), device_id_type=MESH)
+        pl.semaphore_signal(barrier, inc=1, device_id=(*row, red_y(lax.rem(ym + o, ny))), device_id_type=MESH)
+    for o in range(1, nx):
+        pl.semaphore_signal(barrier, inc=1, device_id=(*row, red_x(lax.rem(xm + o, nx))), device_id_type=MESH)
     pl.semaphore_wait(barrier, ny - 1 + nx - 1)
 
     def copy(src, dst, stage, pos, dev):
@@ -95,7 +100,7 @@
             dst_ref=dst,
             send_sem=send_sem.at[stage, pos],
             recv_sem=recv_sem.at[stage, pos],
-            device_id=(row, dev),
+            device_id=(*row, dev),
             device_id_type=MESH,
         )
 
@@ -105,7 +110,7 @@
         c = pltpu.make_async_remote_copy(
             src_ref=src_ref.at[first], dst_ref=out_ref.at[xm, ym, first],
             send_sem=send_sem.at[0, g], recv_sem=recv_sem.at[0, ym],
-            device_id=(row, red_y(g)), device_id_type=MESH,
+            device_id=(*row, red_y(g)), device_id_type=MESH,
         )
         c.start()
         sent.append(c)
@@ -114,7 +119,7 @@
         c = pltpu.make_async_remote_copy(
             src_ref=src_ref.at[second], dst_ref=out_ref.at[xm, ym, second],
             send_sem=send_sem.at[1, g], recv_sem=recv_sem.at[1, xm],
-            device_id=(row, red_x(g)), device_id_type=MESH,
+            device_id=(*row, red_x(g)), device_id_type=MESH,
         )
         c.start()
         sent.append(c)
@@ -135,7 +140,7 @@
         c = pltpu.make_async_remote_copy(
             src_ref=out_ref.at[xm, :, first], dst_ref=out_ref.at[xm, :, first],
             send_sem=send_sem.at[2, g], recv_sem=recv_sem.at[2, xm],
-            device_id=(row, red_x(g)), device_id_type=MESH,
+            device_id=(*row, red_x(g)), device_id_type=MESH,
         )
         c.start()
         sent.append(c)
@@ -147,7 +152,7 @@
         c = pltpu.make_async_remote_copy(
             src_ref=out_ref.at[:, ym, second], dst_ref=out_ref.at[:, ym, second],
             send_sem=send_sem.at[3, g], recv_sem=recv_sem.at[3, ym],
-            device_id=(row, red_y(g)), device_id_type=MESH,
+            device_id=(*row, red_y(g)), device_id_type=MESH,
         )
         c.start()
         sent.append(c)
@@ -181,7 +186,7 @@
 
 
 def _reduce_kernel(n_red, prod_ref, out_ref, ra, rb, sa, sb, qa, qb, send1, recv1, send2, recv2, local_sem):
-    row = lax.axis_index("blk")
+    row = _row()
     ym, ny, red_y = _group("y", n_red)
     xm, nx, red_x = _group("x", n_red)
     half = ra.shape[2]
@@ -189,15 +194,15 @@
 
     barrier = pltpu.get_barrier_semaphore()
     for o in range(1, ny):
-        pl.semaphore_signal(barrier, inc=1, device_id=(row, red_y(lax.rem(ym + o, ny))), device_id_type=MESH)
-    for o in range(1, nx):
-        pl.semaphore_signal(barrier, inc=1, device_id=(row, red_x(lax.rem(xm + o, nx))), device_id_type=MESH)
+        pl.semaphore_signal(barrier, inc=1, device_id=(*row, red_y(lax.rem(ym + o, ny))), device_id_type=MESH)
+    for o in range(1, nx):
+        pl.semaphore_signal(barrier, inc=1, device_id=(*row, red_x(lax.rem(xm + o, nx))), device_id_type=MESH)
     pl.semaphore_wait(barrier, ny - 1 + nx - 1)
 
     def copy(src, dst, send, recv, dev):
         return pltpu.make_async_remote_copy(
             src_ref=src, dst_ref=dst, send_sem=send, recv_sem=recv,
-            device_id=(row, dev), device_id_type=MESH,
+            device_id=(*row, dev), device_id_type=MESH,
         )
 
     sent = []
@@ -318,7 +323,7 @@
 def shards(amplitudes, ladder_ints, cycle_ints, occ_energy, vir_energy, slab_index):
     slab_rows, occ_local, vir_local, virt_width = amplitudes.shape
     n_red = lax.axis_size("red")
-    n_blk = lax.axis_size("blk")
+    n_blk = lax.axis_size("z") * lax.axis_size("core")
     occ_all = occ_local * n_blk
     occ_red = occ_all // n_red
     n_x = n_red // NY
@@ -329,15 +334,20 @@
     gathered = _gather(swapped, n_red, 0)
     operand = gathered.reshape(n_red * slab_rows * vir_local, occ_local * virt_width)
     product = jnp.dot(operand, cycle_ints, preferred_element_type=jnp.float32)
-    product = product.reshape(n_red, slab_rows * vir_local, cycle_ints.shape[1])
-    cycle_own = lax.psum_scatter(product, "blk", scatter_dimension=0, tiled=True)[0]
+    product = product.reshape(n_blk // CORES, CORES, slab_rows * vir_local, cycle_ints.shape[1])
+    core = lax.axis_index("core")
+    theirs = lax.dynamic_index_in_dim(product, CORES - 1 - core, axis=1, keepdims=False)
+    mine = lax.dynamic_index_in_dim(product, core, axis=1, keepdims=False)
+    product = mine + lax.ppermute(theirs, "core", [(0, 1), (1, 0)])
+    cycle_own = lax.psum_scatter(product, "z", scatter_dimension=0, tiled=True)[0]
     cycle_own = jnp.transpose(
         cycle_own.reshape(slab_rows, vir_local, occ_red, virt_width), (0, 2, 1, 3)
     )
 
     rows = slab_rows * occ_local
     flat = amplitudes.reshape(rows, vir_local * virt_width)
-    shard_piece = lax.all_gather(flat, "blk", axis=0, tiled=False)
+    shard_piece = lax.all_gather(flat, "z", axis=0, tiled=False)
+    shard_piece = lax.all_gather(shard_piece, "core", axis=1, tiled=False)
     product = jnp.dot(
         shard_piece.reshape(n_blk * rows, -1), ladder_ints, preferred_element_type=jnp.float32
     )
@@ -352,7 +362,7 @@
     slab_energy = jnp.sum(jnp.where(chosen, occ_energy[None, :], jnp.float32(0.0)), axis=1)
     pair_energy = lax.dynamic_slice_in_dim(occ_energy, lax.axis_index("red") * occ_red, occ_red)
     first_virtual = lax.dynamic_slice_in_dim(
-        vir_energy, lax.axis_index("blk") * vir_block, vir_block
+        vir_energy, (lax.axis_index("z") * CORES + lax.axis_index("core")) * vir_block, vir_block
     )
     denominator = (
         first_virtual[None, None, :, None]
@@ -364,7 +374,12 @@
 
 
 def solution(mesh):
-    placed = (P(None, "blk", "red", None), P("red", "blk"), P("blk", "red"), P(), P(), P())
+    blk = ("z", "core")
+    split = Mesh(
+        mesh.devices.reshape(mesh.shape["blk"] // CORES, CORES, mesh.shape["red"]),
+        ("z", "core", "red"),
+    )
+    placed = (P(None, blk, "red", None), P("red", blk), P(blk, "red"), P(), P(), P())
     return jax.shard_map(
-        shards, mesh=mesh, in_specs=placed, out_specs=P(None, "red", "blk", None), check_vma=False
-    )
+        shards, mesh=split, in_specs=placed, out_specs=P(None, "red", blk, None), check_vma=False
+    )

time: 131 us -> 139 us (1.061); the launches traced: 129 us -> 139 us
  other arithmetic: 2.2 us -> 7.32 us
  local copies, waits for them, and re-layouts: 3.72 us -> 7.38 us
  waiting for transfers between devices: 10.1 us -> 12.4 us
  matrix products: 17 us -> 15.1 us
  starting transfers between devices: 0.04 us -> 1.65 us
    reduce_scatter x1, waiting for transfers between devices: 6.75 us -> 0.02 us  [shards(): lax.psum_scatter(product, 'z', scatter_dimension=0, tiled=True)[0]]
    ppermute x0 -> x1, waiting for transfers between devices: none -> 5.55 us  [shards(): product = mine + lax.ppermute(theirs, 'core', [(0, 1), (1, 0)])]
    add x0 -> x1, other arithmetic: none -> 5.12 us  [shards(): product = mine + lax.ppermute(theirs, 'core', [(0, 1), (1, 0)])]
    all_gather x1 -> x2, waiting for transfers between devices: 3.27 us -> 6.75 us  [the longest x1 6.75 us: shards(): shard_piece = lax.all_gather(shard_piece, 'core', axis=1, tiled=False)]
    squeeze x0 -> x1, local copies, waits for them, and re-layouts: none -> 2.15 us  [shards(): lax.dynamic_index_in_dim(product, CORES - 1 - core, axis=1, keepdims=False)]
    dot_general x1, matrix products: 9.8 us -> 7.88 us  [shards(): product = jnp.dot(operand, cycle_ints, preferred_element_type=jnp.float32)]
    ppermute x0 -> x1, starting transfers between devices: none -> 1.57 us  [shards(): product = mine + lax.ppermute(theirs, 'core', [(0, 1), (1, 0)])]
    unnamed x9 -> x11, local copies, waits for them, and re-layouts: 1.73 us -> 3.24 us
  transfers between devices with their start and end apart: 2 -> 4, of which waited for: 2 -> 2; matrix products, arithmetic and copies ran while one was open for 14% -> 17% of each run, Pallas kernels for 64% -> 59%
where the time goes in v8:
time: 139 us
  Pallas kernels  82 us (59%)
  matrix products  15.1 us (11%)
  between operations  13.2 us (9%)
  waiting for transfers between devices  12.4 us (9%)
  local copies, waits for them, and re-layouts  7.38 us (5%)
  other arithmetic  7.32 us (5%)
  starting transfers between devices  1.65 us (1%)
    pallas_call x1, Pallas kernels, _reduce(): pl.pallas_call(functools.partial(_reduce_kernel, n_red), out_shape=jax.Sh...  50.7 us
    pallas_call x1, Pallas kernels, _gather(): pl.pallas_call(functools.partial(_gather_kernel, n_red), out_shape=jax.Sh...  31.3 us
    dot_general x1, matrix products, shards(): product = jnp.dot(operand, cycle_ints, preferred_element_type=jnp.float32)  7.88 us
    dot_general x1, matrix products, shards(): jnp.dot(shard_piece.reshape(n_blk * rows, -1), ladder_ints, preferred_ele...  7.27 us
    all_gather x1, waiting for transfers between devices, shards(): shard_piece = lax.all_gather(shard_piece, 'core', axis=1, tiled=False)  6.75 us
    ppermute x1, waiting for transfers between devices, shards(): product = mine + lax.ppermute(theirs, 'core', [(0, 1), (1, 0)])  5.55 us
    add x1, other arithmetic, shards(): product = mine + lax.ppermute(theirs, 'core', [(0, 1), (1, 0)])  5.12 us
    unnamed x11, local copies, waits for them, and re-layouts  3.24 us
  transfers between devices with their start and end apart: 4, of which 2 were waited for; matrix products, arithmetic and copies ran while one was open for 17% of the time, Pallas kernels for 59%

profile of v8, /device:TPU:1, one launch (start us, length us, event | category | flops | bytes accessed | tf_op | source)
XLA Modules:
  0.0 139.1 jit_solution(16142541078655076982)
XLA Ops:
  6.5 0.0 copy-start
  6.5 0.0 all-gather.4.cloned.1.call-start
  6.5 1.8 %all_gather_reshape.3 = bf16[1,96,1024]{2,1,0:T(8,128)(2,1)} reshape(bf16[8,12,8,128]{3,2,1,0:T(8,128)(2,1)} %param.6) | data formatting | bytes 393216 | tf_op jit(solution)/shard_map/all_gather;reshape | solution.py:349
  8.4 0.0 all-gather.4.cloned.1.call-update
  8.4 0.0 all-gather.6.cloned.1.call-start
  8.5 31.3 %shard_map.65 = bf16[4,4,64,1536]{3,2,1,0:T(8,128)(2,1)} custom-call(bf16[64,1536]{1,0:T(8,128)(2,1)} %bitcast.35), custom_call_target="tpu_custom_call" | custom-call | bytes 6291456 | tf_op jit(solution)/shard_map/pallas_call | solution.py:173
  39.8 7.9 %fusion = f32[8,2,64,1536]{3,2,1,0:T(8,128)S(1)} fusion(bf16[8,2,64,1536]{3,2,1,0:T(8,128)(2,1)} %bitcast.32, bf16[1536,1536]{1,0:T(8,128)(2,1)} %param.8), kind=kOutput, calls=%fused_computation | convolution fusion | flops 4831838208 | bytes 14155776 | tf_op jit(solution)/shard_map/dot_general | solution.py:336
  47.7 0.0 copy-start.1
  47.7 2.2 %dynamic-slice_bitcast_fusion = f32[8,64,1536]{2,1,0:T(8,128)} fusion(f32[8,2,64,1536]{3,2,1,0:T(8,128)S(1)} %fusion, s32[]{:T(128)S(6)} %select_n.18), kind=kLoop, calls=%fused_computation.3 | loop fusion | bytes 6291460 | tf_op jit(solution)/shard_map/jit(dynamic_index_in_dim)/squeeze | solution.py:339
  49.8 1.5 %copy-done.1 = f32[8,2,64,1536]{3,2,1,0:T(8,128)} copy-done((f32[8,2,64,1536]{3,2,1,0:T(8,128)}, f32[8,2,64,1536]{3,2,1,0:T(8,128)S(1)}, u32[]{:S(2)}) %copy-start.1) | copy-done | bytes 6291480
  51.4 1.6 %collective-permute-start = (f32[8,64,1536]{2,1,0:T(8,128)}, f32[8,64,1536]{2,1,0:T(8,128)}, u32[]{:S(2)}, u32[]{:S(2)}) collective-permute-start(f32[8,64,1536]{2,1,0:T(8,128)} %dynamic-slice_bitcast_fusion), channel_id=1, source_target_pairs={{0,16},{16,0},{1,17},{17,1},{2,18},{18,2},{3,19},{19,3},{4,20},{20... | collective-permute-start | bytes 9437192 | tf_op jit(solution)/shard_map/ppermute | solution.py:341
  53.0 0.0 all-gather.4.cloned.1.call-done
  53.0 0.0 all-gather.6.cloned.1.call-update
  53.0 0.0 reduce-scatter.2.cloned.1.call-start
  53.0 5.6 %collective-permute-done = f32[8,64,1536]{2,1,0:T(8,128)} collective-permute-done((f32[8,64,1536]{2,1,0:T(8,128)}, f32[8,64,1536]{2,1,0:T(8,128)}, u32[]{:S(2)}, u32[]{:S(2)}) %collective-permute-start) | collective-permute-done | bytes 3145760 | tf_op jit(solution)/shard_map/ppermute | solution.py:341
  58.6 5.1 %bitcast_add_fusion = f32[8,64,1536]{2,1,0:T(8,128)} fusion(f32[8,64,1536]{2,1,0:T(8,128)} %collective-permute-done, f32[8,2,64,1536]{3,2,1,0:T(8,128)} %copy-done.1, s32[]{:T(128)S(6)} %select_n.17), kind=kLoop, calls=%fused_computation.2 | loop fusion | flops 786432 | bytes 9437188 | tf_op jit(solution)/shard_map/add | solution.py:341
  63.7 0.0 copy-start.3
  63.7 0.0 copy-start.2
  63.7 0.0 copy-start.4
  63.7 0.0 reduce-scatter.2.cloned.1.call-update
  63.7 0.6 copy-done.3
  64.4 0.1 dynamic_slice.15
  64.4 0.0 copy-done.2
  64.4 0.1 dynamic_slice.16
  64.5 0.0 copy-done.4
  64.5 0.2 select_reduce_fusion
  64.7 0.1 broadcast_add_fusion
  64.8 0.1 broadcast_subtract_fusion
  64.8 6.7 %all-gather.6.cloned.1.call-done = bf16[8,192,1024]{2,1,0:T(8,128)(2,1)} async-done(((bf16[8,96,1024]{2,1,0:T(8,128)(2,1)}), bf16[8,192,1024]{2,1,0:T(8,128)(2,1)}) %all-gather.6.cloned.1.call-update) | async-done | bytes 3145744 | tf_op jit(solution)/shard_map/all_gather | solution.py:350
  71.6 0.0 copy-done
  71.6 7.3 %fusion.2.prod_ref = f32[4,4,96,1024]{3,2,1,0:T(8,128)} fusion(bf16[4,4,96,1024]{3,2,1,0:T(8,128)(2,1)} %bitcast.36, bf16[1024,1024]{1,0:T(8,128)(2,1)S(1)} %copy-done), kind=kOutput, calls=%fused_computation.4 | convolution fusion | flops 3221225472 | bytes 11534336 | tf_op jit(solution)/shard_map/dot_general | solution.py:351
  78.9 50.7 %shard_map.64 = f32[96,1024]{1,0:T(8,128)} custom-call(f32[4,4,96,1024]{3,2,1,0:T(8,128)} %fusion.2.prod_ref), custom_call_target="tpu_custom_call" | custom-call | flops 1572864 | bytes 12582912 | tf_op jit(solution)/shard_map/pallas_call | solution.py:268
  129.6 1.1 copy.9
  130.6 0.0 reduce-scatter.2.cloned.1.call-done
  130.7 1.9 %fusion.4 = f32[8,12,8,128]{3,2,1,0:T(8,128)} fusion(f32[8,12,8,128]{3,2,1,0:T(8,128)S(1)} %bitcast.34, f32[1,64,1536]{2,1,0:T(8,128)} %reduce-scatter.2.cloned.1.call-done, f32[12]{0:T(128)S(1)} %dynamic_slice.16, f32[8,8,128]{2,1,0:T(8,128)S(1)} %broadcast_subtract_fusion), kind=kLoop, calls=%fused_computation.7 | loop fusion | flops 294912 | bytes 1212464 | tf_op jit(solution)/shard_map/div | solution.py:373
Async XLA Ops:
  6.5 65.1 %copy-start = (bf16[1024,1024]{1,0:T(8,128)(2,1)S(1)}, bf16[1024,1024]{1,0:T(8,128)(2,1)}, u32[]{:S(2)}) copy-start(bf16[1024,1024]{1,0:T(8,128)(2,1)} %param.7) | copy-start | bytes 6291460
  6.5 46.4 %all-gather.4.cloned.1.call-start = ((), (), s32[]{:S(2)}) async-start(), calls=%async_computation.1 | async-start | bytes 1769472 | tf_op jit(solution)/shard_map/all_gather | solution.py:349
  8.4 63.2 %all-gather.6.cloned.1.call-start = ((), (), s32[]{:S(2)}) async-start(), calls=%async_computation.3 | async-start | bytes 4718592 | tf_op jit(solution)/shard_map/all_gather | solution.py:350
  47.7 3.7 %copy-start.1 = (f32[8,2,64,1536]{3,2,1,0:T(8,128)}, f32[8,2,64,1536]{3,2,1,0:T(8,128)S(1)}, u32[]{:S(2)}) copy-start(f32[8,2,64,1536]{3,2,1,0:T(8,128)S(1)} %fusion) | copy-start | bytes 18874372
  51.4 7.2 %collective-permute-start = (f32[8,64,1536]{2,1,0:T(8,128)}, f32[8,64,1536]{2,1,0:T(8,128)}, u32[]{:S(2)}, u32[]{:S(2)}) collective-permute-start(f32[8,64,1536]{2,1,0:T(8,128)} %dynamic-slice_bitcast_fusion), channel_id=1, source_target_pairs={{0,16},{16,0},{1,17},{17,1},{2,18},{18,2},{3,19},{19,3},{4,20},{20... | collective-permute-start | bytes 9437192 | tf_op jit(solution)/shard_map/ppermute | solution.py:341
  53.0 77.7 %reduce-scatter.2.cloned.1.call-start = ((), (), s32[]{:S(2)}) async-start(), calls=%async_computation.2 | async-start | bytes 3538944 | tf_op jit(solution)/shard_map/reduce_scatter | solution.py:342
  63.7 0.7 copy-start.3
  63.7 0.7 copy-start.2
  63.7 0.8 copy-start.4
Sparse Core Ops, SparseCore 0:
  9.1 40.2 all-gather.3
  53.1 18.4 all-gather.5
  74.2 44.6 reduce-scatter.1

commit v9 on v8

--- a/solution.py
+++ b/solution.py
@@ -290,6 +290,48 @@
     )(prod)
 
 
+def _core_reduce_kernel(prod_ref, out_ref, theirs, mine, send_sem, recv_sem, local_sem):
+    z, core = _row()
+    red = lax.axis_index("red")
+    other = CORES - 1 - core
+    barrier = pltpu.get_barrier_semaphore()
+    pl.semaphore_signal(barrier, inc=1, device_id=(z, other, red), device_id_type=MESH)
+    pl.semaphore_wait(barrier, 1)
+    send = pltpu.make_async_remote_copy(
+        src_ref=prod_ref.at[:, other], dst_ref=theirs, send_sem=send_sem, recv_sem=recv_sem,
+        device_id=(z, other, red), device_id_type=MESH,
+    )
+    send.start()
+    own = pltpu.make_async_copy(prod_ref.at[:, core], mine, local_sem)
+    own.start()
+    own.wait()
+    send.wait()
+    for k in range(out_ref.shape[0]):
+        out_ref[k] = mine[k] + theirs[k]
+
+
+def _core_reduce(prod, collective_id):
+    n_z, _, rows, cols = prod.shape
+    f32 = jnp.float32
+    return pl.pallas_call(
+        _core_reduce_kernel,
+        out_shape=jax.ShapeDtypeStruct((n_z, rows, cols), f32),
+        in_specs=[pl.BlockSpec(memory_space=pl.ANY)],
+        out_specs=pl.BlockSpec(memory_space=pltpu.VMEM),
+        scratch_shapes=[
+            pltpu.VMEM((n_z, rows, cols), f32),
+            pltpu.VMEM((n_z, rows, cols), f32),
+            pltpu.SemaphoreType.DMA,
+            pltpu.SemaphoreType.DMA,
+            pltpu.SemaphoreType.DMA,
+        ],
+        compiler_params=pltpu.CompilerParams(collective_id=collective_id, has_side_effects=True),
+        cost_estimate=pl.CostEstimate(
+            flops=prod.size // 2, bytes_accessed=prod.size * 4, transcendentals=0
+        ),
+    )(prod)
+
+
 def _exchange(jobs, srcs, out_shapes, n_red, collective_id):
     nbytes = sum(s.size * s.dtype.itemsize for s in srcs)
     nmax = max(_group_size(job[0], n_red) for job in jobs)
@@ -335,10 +377,7 @@
     operand = gathered.reshape(n_red * slab_rows * vir_local, occ_local * virt_width)
     product = jnp.dot(operand, cycle_ints, preferred_element_type=jnp.float32)
     product = product.reshape(n_blk // CORES, CORES, slab_rows * vir_local, cycle_ints.shape[1])
-    core = lax.axis_index("core")
-    theirs = lax.dynamic_index_in_dim(product, CORES - 1 - core, axis=1, keepdims=False)
-    mine = lax.dynamic_index_in_dim(product, core, axis=1, keepdims=False)
-    product = mine + lax.ppermute(theirs, "core", [(0, 1), (1, 0)])
+    product = _core_reduce(product, 4)
     cycle_own = lax.psum_scatter(product, "z", scatter_dimension=0, tiled=True)[0]
     cycle_own = jnp.transpose(
         cycle_own.reshape(slab_rows, vir_local, occ_red, virt_width), (0, 2, 1, 3)
@@ -346,8 +385,7 @@
 
     rows = slab_rows * occ_local
     flat = amplitudes.reshape(rows, vir_local * virt_width)
-    shard_piece = lax.all_gather(flat, "z", axis=0, tiled=False)
-    shard_piece = lax.all_gather(shard_piece, "core", axis=1, tiled=False)
+    shard_piece = lax.all_gather(flat, ("z", "core"), axis=0, tiled=False)
     product = jnp.dot(
         shard_piece.reshape(n_blk * rows, -1), ladder_ints, preferred_element_type=jnp.float32
     )

time: 139 us -> 127 us (0.914)
  waiting for transfers between devices: 12.4 us -> 0.06 us
  Pallas kernels: 82 us -> 89.2 us
  other arithmetic: 7.32 us -> 2.2 us
  local copies, waits for them, and re-layouts: 7.38 us -> 3.69 us
  matrix products: 15.1 us -> 17.1 us
  between operations: 13.2 us -> 14.9 us
  starting transfers between devices: 1.65 us -> 0.05 us
    pallas_call x0 -> x1, Pallas kernels: none -> 9.13 us  [_core_reduce(): pl.pallas_call(_core_reduce_kernel, out_shape=jax.ShapeDtypeStruct((n_z,...]
    all_gather x2 -> x1, waiting for transfers between devices: 6.75 us -> 0.01 us  [shards(): shard_piece = lax.all_gather(flat, ('z', 'core'), axis=0, tiled=False)]
    ppermute x1 -> x0, waiting for transfers between devices: 5.55 us -> none  [shards(): product = mine + lax.ppermute(theirs, 'core', [(0, 1), (1, 0)])]
    add x1 -> x0, other arithmetic: 5.12 us -> none  [shards(): product = mine + lax.ppermute(theirs, 'core', [(0, 1), (1, 0)])]
    squeeze x1 -> x0, local copies, waits for them, and re-layouts: 2.15 us -> none  [shards(): lax.dynamic_index_in_dim(product, CORES - 1 - core, axis=1, keepdims=False)]
    pallas_call x1, Pallas kernels: 50.7 us -> 48.8 us  [_reduce(): pl.pallas_call(functools.partial(_reduce_kernel, n_red), out_shape=jax.Sh...]
    dot_general x1, matrix products: 7.88 us -> 9.79 us  [shards(): product = jnp.dot(operand, cycle_ints, preferred_element_type=jnp.float32)]
    ppermute x1 -> x0, starting transfers between devices: 1.57 us -> none  [shards(): product = mine + lax.ppermute(theirs, 'core', [(0, 1), (1, 0)])]
  transfers between devices with their start and end apart: 4 -> 2, of which waited for: 2 -> 0; matrix products, arithmetic and copies ran while one was open for 17% -> 15% of each run, Pallas kernels for 59% -> 70%
where the time goes in v9:
time: 127 us
  Pallas kernels  89.2 us (70%)
  matrix products  17.1 us (13%)
  between operations  14.9 us (12%)
  local copies, waits for them, and re-layouts  3.69 us (3%)
  other arithmetic  2.2 us (2%)
    pallas_call x1, Pallas kernels, _reduce(): pl.pallas_call(functools.partial(_reduce_kernel, n_red), out_shape=jax.Sh...  48.8 us
    pallas_call x1, Pallas kernels, _gather(): pl.pallas_call(functools.partial(_gather_kernel, n_red), out_shape=jax.Sh...  31.3 us
    dot_general x1, matrix products, shards(): product = jnp.dot(operand, cycle_ints, preferred_element_type=jnp.float32)  9.79 us
    pallas_call x1, Pallas kernels, _core_reduce(): pl.pallas_call(_core_reduce_kernel, out_shape=jax.ShapeDtypeStruct((n_z,...  9.13 us
    dot_general x1, matrix products, shards(): jnp.dot(shard_piece.reshape(n_blk * rows, -1), ladder_ints, preferred_ele...  7.27 us
  transfers between devices with their start and end apart: 2, of which 0 were waited for; matrix products, arithmetic and copies ran while one was open for 15% of the time, Pallas kernels for 70%

profile of v9, /device:TPU:1, one launch (start us, length us, event | category | flops | bytes accessed | tf_op | source)
XLA Modules:
  0.0 127.2 jit_solution(2246725707543492149)
XLA Ops:
  7.4 0.0 copy-start
  7.4 0.0 all-gather.2.cloned.1.call-start
  7.4 1.8 %all_gather_reshape.3 = bf16[1,96,1024]{2,1,0:T(8,128)(2,1)} reshape(bf16[8,12,8,128]{3,2,1,0:T(8,128)(2,1)} %param.6) | data formatting | bytes 393216 | tf_op jit(solution)/shard_map/all_gather;reshape | solution.py:388
  9.2 0.0 all-gather.2.cloned.1.call-update
  9.2 0.0 reduce-scatter.2.cloned.1.call-start
  9.3 31.3 %shard_map.65 = bf16[4,4,64,1536]{3,2,1,0:T(8,128)(2,1)} custom-call(bf16[64,1536]{1,0:T(8,128)(2,1)} %bitcast.31), custom_call_target="tpu_custom_call" | custom-call | bytes 6291456 | tf_op jit(solution)/shard_map/pallas_call | solution.py:173
  40.6 9.8 %fusion.prod_ref = f32[8,2,64,1536]{3,2,1,0:T(8,128)} fusion(bf16[8,2,64,1536]{3,2,1,0:T(8,128)(2,1)} %bitcast.28, bf16[1536,1536]{1,0:T(8,128)(2,1)} %param.8), kind=kOutput, calls=%fused_computation | convolution fusion | flops 4831838208 | bytes 14155776 | tf_op jit(solution)/shard_map/dot_general | solution.py:378
  50.4 9.1 %shard_map.66 = f32[8,64,1536]{2,1,0:T(8,128)} custom-call(f32[8,2,64,1536]{3,2,1,0:T(8,128)} %fusion.prod_ref), custom_call_target="tpu_custom_call" | custom-call | flops 786432 | bytes 6291456 | tf_op jit(solution)/shard_map/pallas_call | solution.py:316
  59.6 0.0 copy-start.1
  59.6 0.0 copy-start.2
  59.6 0.0 copy-start.3
  59.6 0.0 reduce-scatter.2.cloned.1.call-update
  59.6 0.6 copy-done.1
  60.2 0.1 dynamic_slice.7
  60.3 0.0 copy-done.2
  60.3 0.1 dynamic_slice.6
  60.4 0.0 copy-done.3
  60.4 0.2 select_reduce_fusion
  60.6 0.1 broadcast_add_fusion
  60.6 0.1 broadcast_subtract_fusion
  60.7 0.0 all-gather.2.cloned.1.call-done
  60.7 0.0 copy-done
  60.7 7.3 %fusion.2.prod_ref = f32[4,4,96,1024]{3,2,1,0:T(8,128)} fusion(bf16[4,4,96,1024]{3,2,1,0:T(8,128)(2,1)} %bitcast.32, bf16[1024,1024]{1,0:T(8,128)(2,1)S(1)} %copy-done), kind=kOutput, calls=%fused_computation.2 | convolution fusion | flops 3221225472 | bytes 11534336 | tf_op jit(solution)/shard_map/dot_general | solution.py:389
  68.0 48.8 %shard_map.64 = f32[96,1024]{1,0:T(8,128)} custom-call(f32[4,4,96,1024]{3,2,1,0:T(8,128)} %fusion.2.prod_ref), custom_call_target="tpu_custom_call" | custom-call | flops 1572864 | bytes 12582912 | tf_op jit(solution)/shard_map/pallas_call | solution.py:268
  116.8 1.1 copy.9
  117.8 0.0 reduce-scatter.2.cloned.1.call-done
  117.9 1.9 %fusion.4 = f32[8,12,8,128]{3,2,1,0:T(8,128)} fusion(f32[8,12,8,128]{3,2,1,0:T(8,128)S(1)} %bitcast.30, f32[1,64,1536]{2,1,0:T(8,128)} %reduce-scatter.2.cloned.1.call-done, f32[12]{0:T(128)S(1)} %dynamic_slice.7, f32[8,8,128]{2,1,0:T(8,128)S(1)} %broadcast_subtract_fusion), kind=kLoop, calls=%fused_computation.5 | loop fusion | flops 294912 | bytes 1212464 | tf_op jit(solution)/shard_map/div | solution.py:411
Async XLA Ops:
  7.4 53.4 %copy-start = (bf16[1024,1024]{1,0:T(8,128)(2,1)S(1)}, bf16[1024,1024]{1,0:T(8,128)(2,1)}, u32[]{:S(2)}) copy-start(bf16[1024,1024]{1,0:T(8,128)(2,1)} %param.7) | copy-start | bytes 6291460
  7.4 53.3 %all-gather.2.cloned.1.call-start = ((), (), s32[]{:S(2)}) async-start(), calls=%async_computation.1 | async-start | bytes 3342336 | tf_op jit(solution)/shard_map/all_gather | solution.py:388
  9.2 108.6 %reduce-scatter.2.cloned.1.call-start = ((), (), s32[]{:S(2)}) async-start(), calls=%async_computation.2 | async-start | bytes 3538944 | tf_op jit(solution)/shard_map/reduce_scatter | solution.py:381
  59.6 0.7 copy-start.1
  59.6 0.7 copy-start.2
  59.6 0.8 copy-start.3
Sparse Core Ops, SparseCore 0:
  10.0 46.3 all-gather.1
Sparse Core Ops, SparseCore 1:
  59.7 44.0 reduce-scatter.1

commit v10 on v9

--- a/solution.py
+++ b/solution.py
@@ -185,7 +185,7 @@
     )(block)
 
 
-def _reduce_kernel(n_red, prod_ref, out_ref, ra, rb, sa, sb, qa, qb, send1, recv1, send2, recv2, local_sem):
+def _reduce_kernel(n_red, amp_ref, ints_ref, out_ref, ra, rb, pa, pb, sa, sb, qa, qb, send1, recv1, send2, recv2):
     row = _row()
     ym, ny, red_y = _group("y", n_red)
     xm, nx, red_x = _group("x", n_red)
@@ -205,26 +205,34 @@
             device_id=(*row, dev), device_id_type=MESH,
         )
 
+    width = ints_ref.shape[1]
+
+    def block(lhs):
+        slots = lhs.shape[0]
+        flat = lhs.reshape(slots * half, lhs.shape[2])
+        product = jnp.dot(flat, ints_ref[...], preferred_element_type=jnp.float32)
+        return product.reshape(slots, half, width)
+
     sent = []
-    for o in range(1, ny):
-        g = lax.rem(ym + o, ny)
-        c = copy(prod_ref.at[:, g, first], ra.at[ym], send1.at[0, g], recv1.at[0, ym], red_y(g))
-        c.start()
-        sent.append(c)
-    for o in range(1, nx):
-        g = lax.rem(xm + o, nx)
-        c = copy(prod_ref.at[g, :, second], rb.at[xm], send1.at[1, g], recv1.at[1, xm], red_x(g))
-        c.start()
-        sent.append(c)
-    own_a = pltpu.make_async_copy(prod_ref.at[:, ym, first], ra.at[ym], local_sem.at[0])
-    own_b = pltpu.make_async_copy(prod_ref.at[xm, :, second], rb.at[xm], local_sem.at[1])
-    own_a.start()
-    own_b.start()
-
-    own_a.wait()
-    for o in range(1, ny):
-        g = lax.rem(ym + o, ny)
-        copy(prod_ref.at[:, g, first], ra.at[g], send1.at[0, g], recv1.at[0, g], red_y(g)).wait_recv()
+    for o in range(1, max(nx, ny)):
+        if o < ny:
+            g = lax.rem(ym + o, ny)
+            pa[g] = block(amp_ref[:, g, first])
+            c = copy(pa.at[g], ra.at[ym], send1.at[0, g], recv1.at[0, ym], red_y(g))
+            c.start()
+            sent.append(c)
+        if o < nx:
+            g = lax.rem(xm + o, nx)
+            pb[g] = block(amp_ref[g, :, second])
+            c = copy(pb.at[g], rb.at[xm], send1.at[1, g], recv1.at[1, xm], red_x(g))
+            c.start()
+            sent.append(c)
+    ra[ym] = block(amp_ref[:, ym, first])
+    rb[xm] = block(amp_ref[xm, :, second])
+
+    for o in range(1, ny):
+        g = lax.rem(ym + o, ny)
+        copy(pa.at[g], ra.at[g], send1.at[0, g], recv1.at[0, g], red_y(g)).wait_recv()
     for k in range(nx):
         sa[k] = ra[0, k] + ra[1, k] + ra[2, k] + ra[3, k]
     for o in range(1, nx):
@@ -233,10 +241,9 @@
         c.start()
         sent.append(c)
 
-    own_b.wait()
-    for o in range(1, nx):
-        g = lax.rem(xm + o, nx)
-        copy(prod_ref.at[g, :, second], rb.at[g], send1.at[1, g], recv1.at[1, g], red_x(g)).wait_recv()
+    for o in range(1, nx):
+        g = lax.rem(xm + o, nx)
+        copy(pb.at[g], rb.at[g], send1.at[1, g], recv1.at[1, g], red_x(g)).wait_recv()
     for k in range(ny):
         sb[k] = rb[0, k] + rb[1, k] + rb[2, k] + rb[3, k]
     for o in range(1, ny):
@@ -261,16 +268,19 @@
     out_ref[second] = total_b
 
 
-def _reduce(prod, n_red, collective_id):
-    n_x, n_y, rows, cols = prod.shape
+def _reduce(amp, ints, n_red, collective_id):
+    n_x, n_y, rows, _ = amp.shape
+    cols = ints.shape[1]
     half = rows // 2
     f32 = jnp.float32
     return pl.pallas_call(
         functools.partial(_reduce_kernel, n_red),
         out_shape=jax.ShapeDtypeStruct((rows, cols), f32),
-        in_specs=[pl.BlockSpec(memory_space=pl.ANY)],
+        in_specs=[pl.BlockSpec(memory_space=pltpu.VMEM)] * 2,
         out_specs=pl.BlockSpec(memory_space=pltpu.VMEM),
         scratch_shapes=[
+            pltpu.VMEM((n_y, n_x, half, cols), f32),
+            pltpu.VMEM((n_x, n_y, half, cols), f32),
             pltpu.VMEM((n_y, n_x, half, cols), f32),
             pltpu.VMEM((n_x, n_y, half, cols), f32),
             pltpu.VMEM((n_x, half, cols), f32),
@@ -281,13 +291,15 @@
             pltpu.SemaphoreType.DMA((2, max(n_x, n_y))),
             pltpu.SemaphoreType.DMA((2, max(n_x, n_y))),
             pltpu.SemaphoreType.DMA((2, max(n_x, n_y))),
-            pltpu.SemaphoreType.DMA((2,)),
         ],
-        compiler_params=pltpu.CompilerParams(collective_id=collective_id, has_side_effects=True),
+        compiler_params=pltpu.CompilerParams(
+            collective_id=collective_id, has_side_effects=True, vmem_limit_bytes=60 * 1024 * 1024
+        ),
         cost_estimate=pl.CostEstimate(
-            flops=prod.size, bytes_accessed=2 * prod.size * 4, transcendentals=0
+            flops=2 * amp.size * cols, bytes_accessed=amp.size * 2 + ints.size * 2 + rows * cols * 4,
+            transcendentals=0,
         ),
-    )(prod)
+    )(amp, ints)
 
 
 def _core_reduce_kernel(prod_ref, out_ref, theirs, mine, send_sem, recv_sem, local_sem):
@@ -386,12 +398,7 @@
     rows = slab_rows * occ_local
     flat = amplitudes.reshape(rows, vir_local * virt_width)
     shard_piece = lax.all_gather(flat, ("z", "core"), axis=0, tiled=False)
-    product = jnp.dot(
-        shard_piece.reshape(n_blk * rows, -1), ladder_ints, preferred_element_type=jnp.float32
-    )
-    cols = ladder_ints.shape[1]
-    product = product.reshape(n_x, NY, rows, cols)
-    ladder_own = _reduce(product, n_red, 1)
+    ladder_own = _reduce(shard_piece.reshape(n_x, NY, rows, -1), ladder_ints, n_red, 1)
     ladder_own = ladder_own.reshape(slab_rows, occ_red, -1, virt_width)
 
     vir_block = cycle_own.shape[2]

time: 127 us -> 125 us (0.984)
  matrix products: 17.1 us -> 9.78 us
  Pallas kernels: 89.2 us -> 94.6 us
    dot_general x1 -> x0, matrix products: 7.27 us -> none  [shards(): jnp.dot(shard_piece.reshape(n_blk * rows, -1), ladder_ints, preferred_ele...]
    pallas_call x1, Pallas kernels: 48.8 us -> 54.2 us  [_reduce(): pl.pallas_call(functools.partial(_reduce_kernel, n_red), out_shape=jax.Sh...]
  transfers between devices with their start and end apart: 2 -> 2, of which waited for: 0 -> 0; matrix products, arithmetic and copies ran while one was open for 15% -> 9% of each run, Pallas kernels for 70% -> 76%
where the time goes in v10:
time: 125 us
  Pallas kernels  94.6 us (76%)
  between operations  14.9 us (12%)
  matrix products  9.78 us (8%)
  local copies, waits for them, and re-layouts  3.51 us (3%)
  other arithmetic  2.2 us (2%)
    pallas_call x1, Pallas kernels, _reduce(): pl.pallas_call(functools.partial(_reduce_kernel, n_red), out_shape=jax.Sh...  54.2 us
    pallas_call x1, Pallas kernels, _gather(): pl.pallas_call(functools.partial(_gather_kernel, n_red), out_shape=jax.Sh...  31.3 us
    dot_general x1, matrix products, shards(): product = jnp.dot(operand, cycle_ints, preferred_element_type=jnp.float32)  9.78 us
    pallas_call x1, Pallas kernels, _core_reduce(): pl.pallas_call(_core_reduce_kernel, out_shape=jax.ShapeDtypeStruct((n_z,...  9.06 us
  transfers between devices with their start and end apart: 2, of which 0 were waited for; matrix products, arithmetic and copies ran while one was open for 9% of the time, Pallas kernels for 76%

profile of v10, /device:TPU:1, one launch (start us, length us, event | category | flops | bytes accessed | tf_op | source)
XLA Modules:
  0.0 125.1 jit_solution(2202502361548566729)
XLA Ops:
  7.4 0.0 all-gather.2.cloned.1.call-start
  7.4 1.7 %all_gather_reshape.3 = bf16[1,96,1024]{2,1,0:T(8,128)(2,1)} reshape(bf16[8,12,8,128]{3,2,1,0:T(8,128)(2,1)} %param.6) | data formatting | bytes 393216 | tf_op jit(solution)/shard_map/all_gather;reshape | solution.py:400
  9.1 0.0 all-gather.2.cloned.1.call-update
  9.1 0.0 reduce-scatter.2.cloned.1.call-start
  9.1 31.3 %shard_map.65 = bf16[4,4,64,1536]{3,2,1,0:T(8,128)(2,1)} custom-call(bf16[64,1536]{1,0:T(8,128)(2,1)} %bitcast.24), custom_call_target="tpu_custom_call" | custom-call | bytes 6291456 | tf_op jit(solution)/shard_map/pallas_call | solution.py:173
  40.5 9.8 %fusion.prod_ref = f32[8,2,64,1536]{3,2,1,0:T(8,128)} fusion(bf16[8,2,64,1536]{3,2,1,0:T(8,128)(2,1)} %bitcast.22, bf16[1536,1536]{1,0:T(8,128)(2,1)} %param.8), kind=kOutput, calls=%fused_computation | convolution fusion | flops 4831838208 | bytes 14155776 | tf_op jit(solution)/shard_map/dot_general | solution.py:390
  50.3 9.1 %shard_map.66 = f32[8,64,1536]{2,1,0:T(8,128)} custom-call(f32[8,2,64,1536]{3,2,1,0:T(8,128)} %fusion.prod_ref), custom_call_target="tpu_custom_call" | custom-call | flops 786432 | bytes 6291456 | tf_op jit(solution)/shard_map/pallas_call | solution.py:328
  59.3 0.0 copy-start.1
  59.3 0.0 copy-start
  59.3 0.0 copy-start.2
  59.4 0.0 reduce-scatter.2.cloned.1.call-update
  59.4 0.6 copy-done.1
  60.0 0.1 dynamic_slice.6
  60.1 0.0 copy-done
  60.1 0.1 dynamic_slice.7
  60.1 0.0 copy-done.2
  60.1 0.2 select_reduce_fusion
  60.3 0.1 broadcast_add_fusion
  60.4 0.1 broadcast_subtract_fusion
  60.5 0.0 all-gather.2.cloned.1.call-done
  60.5 54.2 %shard_map.64 = f32[96,1024]{1,0:T(8,128)} custom-call(bf16[4,4,96,1024]{3,2,1,0:T(8,128)(2,1)} %bitcast.26, bf16[1024,1024]{1,0:T(8,128)(2,1)} %ints_ref.1), custom_call_target="tpu_custom_call" | custom-call | flops 3221225472 | bytes 5636096 | tf_op jit(solution)/shard_map/pallas_call | solution.py:276
  114.6 1.1 copy.8
  115.7 0.0 reduce-scatter.2.cloned.1.call-done
  115.7 1.9 %fusion.2 = f32[8,12,8,128]{3,2,1,0:T(8,128)} fusion(f32[8,12,8,128]{3,2,1,0:T(8,128)S(1)} %bitcast.23, f32[1,64,1536]{2,1,0:T(8,128)} %reduce-scatter.2.cloned.1.call-done, f32[12]{0:T(128)S(1)} %dynamic_slice.7, f32[8,8,128]{2,1,0:T(8,128)S(1)} %broadcast_subtract_fusion), kind=kLoop, calls=%fused_computation.3 | loop fusion | flops 294912 | bytes 1212464 | tf_op jit(solution)/shard_map/div | solution.py:418
Async XLA Ops:
  7.4 53.1 %all-gather.2.cloned.1.call-start = ((), (), s32[]{:S(2)}) async-start(), calls=%async_computation.1 | async-start | bytes 3342336 | tf_op jit(solution)/shard_map/all_gather | solution.py:400
  9.1 106.7 %reduce-scatter.2.cloned.1.call-start = ((), (), s32[]{:S(2)}) async-start(), calls=%async_computation.2 | async-start | bytes 3538944 | tf_op jit(solution)/shard_map/reduce_scatter | solution.py:393
  59.3 0.7 copy-start.1
  59.3 0.7 copy-start
  59.3 0.8 copy-start.2
Sparse Core Ops, SparseCore 0:
  10.0 47.3 all-gather.1
Sparse Core Ops, SparseCore 1:
  59.5 44.1 reduce-scatter.1

commit v11 on v10

--- a/solution.py
+++ b/solution.py
@@ -302,46 +302,65 @@
     )(amp, ints)
 
 
-def _core_reduce_kernel(prod_ref, out_ref, theirs, mine, send_sem, recv_sem, local_sem):
+def _core_reduce_kernel(amp_ref, ints_ref, out_ref, mine_sent, theirs, send_sem, recv_sem):
     z, core = _row()
     red = lax.axis_index("red")
     other = CORES - 1 - core
+    n_z, _, rows, _ = amp_ref.shape
+    width = ints_ref.shape[1]
+    step = n_z // 2
     barrier = pltpu.get_barrier_semaphore()
     pl.semaphore_signal(barrier, inc=1, device_id=(z, other, red), device_id_type=MESH)
     pl.semaphore_wait(barrier, 1)
-    send = pltpu.make_async_remote_copy(
-        src_ref=prod_ref.at[:, other], dst_ref=theirs, send_sem=send_sem, recv_sem=recv_sem,
-        device_id=(z, other, red), device_id_type=MESH,
-    )
-    send.start()
-    own = pltpu.make_async_copy(prod_ref.at[:, core], mine, local_sem)
-    own.start()
-    own.wait()
-    send.wait()
-    for k in range(out_ref.shape[0]):
-        out_ref[k] = mine[k] + theirs[k]
-
-
-def _core_reduce(prod, collective_id):
-    n_z, _, rows, cols = prod.shape
+
+    def block(k, which):
+        lhs = amp_ref[pl.ds(k * step, step), which]
+        product = jnp.dot(
+            lhs.reshape(step * rows, lhs.shape[2]), ints_ref[...], preferred_element_type=jnp.float32
+        )
+        return product.reshape(step, rows, width)
+
+    sends = []
+    for k in range(2):
+        mine_sent[pl.ds(k * step, step)] = block(k, other)
+        c = pltpu.make_async_remote_copy(
+            src_ref=mine_sent.at[pl.ds(k * step, step)], dst_ref=theirs.at[pl.ds(k * step, step)],
+            send_sem=send_sem.at[k], recv_sem=recv_sem.at[k],
+            device_id=(z, other, red), device_id_type=MESH,
+        )
+        c.start()
+        sends.append(c)
+    for k in range(2):
+        out_ref[pl.ds(k * step, step)] = block(k, core)
+    for k, c in enumerate(sends):
+        c.wait()
+        for i in range(k * step, (k + 1) * step):
+            out_ref[i] = out_ref[i] + theirs[i]
+
+
+def _core_reduce(amp, ints, collective_id):
+    n_z, _, rows, _ = amp.shape
+    cols = ints.shape[1]
     f32 = jnp.float32
     return pl.pallas_call(
         _core_reduce_kernel,
         out_shape=jax.ShapeDtypeStruct((n_z, rows, cols), f32),
-        in_specs=[pl.BlockSpec(memory_space=pl.ANY)],
+        in_specs=[pl.BlockSpec(memory_space=pltpu.VMEM)] * 2,
         out_specs=pl.BlockSpec(memory_space=pltpu.VMEM),
         scratch_shapes=[
             pltpu.VMEM((n_z, rows, cols), f32),
             pltpu.VMEM((n_z, rows, cols), f32),
-            pltpu.SemaphoreType.DMA,
-            pltpu.SemaphoreType.DMA,
-            pltpu.SemaphoreType.DMA,
+            pltpu.SemaphoreType.DMA((2,)),
+            pltpu.SemaphoreType.DMA((2,)),
         ],
-        compiler_params=pltpu.CompilerParams(collective_id=collective_id, has_side_effects=True),
+        compiler_params=pltpu.CompilerParams(
+            collective_id=collective_id, has_side_effects=True, vmem_limit_bytes=60 * 1024 * 1024
+        ),
         cost_estimate=pl.CostEstimate(
-            flops=prod.size // 2, bytes_accessed=prod.size * 4, transcendentals=0
+            flops=2 * amp.size * cols, bytes_accessed=amp.size * 2 + ints.size * 2 + n_z * rows * cols * 4,
+            transcendentals=0,
         ),
-    )(prod)
+    )(amp, ints)
 
 
 def _exchange(jobs, srcs, out_shapes, n_red, collective_id):
@@ -386,10 +405,8 @@
         slab_rows * vir_local, occ_local * virt_width
     )
     gathered = _gather(swapped, n_red, 0)
-    operand = gathered.reshape(n_red * slab_rows * vir_local, occ_local * virt_width)
-    product = jnp.dot(operand, cycle_ints, preferred_element_type=jnp.float32)
-    product = product.reshape(n_blk // CORES, CORES, slab_rows * vir_local, cycle_ints.shape[1])
-    product = _core_reduce(product, 4)
+    operand = gathered.reshape(n_blk // CORES, CORES, slab_rows * vir_local, occ_local * virt_width)
+    product = _core_reduce(operand, cycle_ints, 4)
     cycle_own = lax.psum_scatter(product, "z", scatter_dimension=0, tiled=True)[0]
     cycle_own = jnp.transpose(
         cycle_own.reshape(slab_rows, vir_local, occ_red, virt_width), (0, 2, 1, 3)

time: 125 us -> 121 us (0.968)
  matrix products: 9.78 us -> 0 us
  Pallas kernels: 94.6 us -> 100 us
    dot_general x1 -> x0, matrix products: 9.78 us -> none  [shards(): product = jnp.dot(operand, cycle_ints, preferred_element_type=jnp.float32)]
    pallas_call x1, Pallas kernels: 9.06 us -> 13.8 us  [_core_reduce(): pl.pallas_call(_core_reduce_kernel, out_shape=jax.ShapeDtypeStruct((n_z,...]
  transfers between devices with their start and end apart: 2 -> 2, of which waited for: 0 -> 0; matrix products, arithmetic and copies ran while one was open for 9% -> 1% of each run, Pallas kernels for 76% -> 83%
where the time goes in v11:
time: 121 us
  Pallas kernels  100 us (83%)
  between operations  14.9 us (12%)
  local copies, waits for them, and re-layouts  3.51 us (3%)
  other arithmetic  2.2 us (2%)
    pallas_call x1, Pallas kernels, _reduce(): pl.pallas_call(functools.partial(_reduce_kernel, n_red), out_shape=jax.Sh...  55.1 us
    pallas_call x1, Pallas kernels, _gather(): pl.pallas_call(functools.partial(_gather_kernel, n_red), out_shape=jax.Sh...  31.3 us
    pallas_call x1, Pallas kernels, _core_reduce(): pl.pallas_call(_core_reduce_kernel, out_shape=jax.ShapeDtypeStruct((n_z,...  13.8 us
  transfers between devices with their start and end apart: 2, of which 0 were waited for; matrix products, arithmetic and copies ran while one was open for 1% of the time, Pallas kernels for 83%

profile of v11, /device:TPU:1, one launch (start us, length us, event | category | flops | bytes accessed | tf_op | source)
XLA Modules:
  0.0 120.9 jit_solution(8811180372163666507)
XLA Ops:
  7.4 0.0 all-gather.2.cloned.1.call-start
  7.4 1.7 %all_gather_reshape.3 = bf16[1,96,1024]{2,1,0:T(8,128)(2,1)} reshape(bf16[8,12,8,128]{3,2,1,0:T(8,128)(2,1)} %param.6) | data formatting | bytes 393216 | tf_op jit(solution)/shard_map/all_gather;reshape | solution.py:417
  9.1 0.0 all-gather.2.cloned.1.call-update
  9.1 0.0 reduce-scatter.2.cloned.1.call-start
  9.1 31.3 %shard_map.65 = bf16[4,4,64,1536]{3,2,1,0:T(8,128)(2,1)} custom-call(bf16[64,1536]{1,0:T(8,128)(2,1)} %bitcast.18), custom_call_target="tpu_custom_call" | custom-call | bytes 6291456 | tf_op jit(solution)/shard_map/pallas_call | solution.py:173
  40.5 13.8 %shard_map.66 = f32[8,64,1536]{2,1,0:T(8,128)} custom-call(bf16[8,2,64,1536]{3,2,1,0:T(8,128)(2,1)} %bitcast.16, bf16[1536,1536]{1,0:T(8,128)(2,1)} %ints_ref.3), custom_call_target="tpu_custom_call" | custom-call | flops 4831838208 | bytes 11010048 | tf_op jit(solution)/shard_map/pallas_call | solution.py:345
  54.3 0.0 copy-start.1
  54.3 0.0 copy-start
  54.3 0.0 copy-start.2
  54.3 0.0 reduce-scatter.2.cloned.1.call-update
  54.3 0.6 copy-done.1
  54.9 0.1 dynamic_slice.6
  55.0 0.0 copy-done
  55.0 0.1 dynamic_slice.7
  55.1 0.0 copy-done.2
  55.1 0.2 select_reduce_fusion
  55.2 0.1 broadcast_add_fusion
  55.3 0.1 broadcast_subtract_fusion
  55.4 0.0 all-gather.2.cloned.1.call-done
  55.4 55.1 %shard_map.64 = f32[96,1024]{1,0:T(8,128)} custom-call(bf16[4,4,96,1024]{3,2,1,0:T(8,128)(2,1)} %bitcast.20, bf16[1024,1024]{1,0:T(8,128)(2,1)} %ints_ref.2), custom_call_target="tpu_custom_call" | custom-call | flops 3221225472 | bytes 5636096 | tf_op jit(solution)/shard_map/pallas_call | solution.py:276
  110.5 1.1 copy.7
  111.6 0.0 reduce-scatter.2.cloned.1.call-done
  111.6 1.9 %fusion = f32[8,12,8,128]{3,2,1,0:T(8,128)} fusion(f32[8,12,8,128]{3,2,1,0:T(8,128)S(1)} %bitcast.17, f32[1,64,1536]{2,1,0:T(8,128)} %reduce-scatter.2.cloned.1.call-done, f32[12]{0:T(128)S(1)} %dynamic_slice.7, f32[8,8,128]{2,1,0:T(8,128)S(1)} %broadcast_subtract_fusion), kind=kLoop, calls=%fused_computation.1 | loop fusion | flops 294912 | bytes 1212464 | tf_op jit(solution)/shard_map/div | solution.py:435
Async XLA Ops:
  7.4 48.0 %all-gather.2.cloned.1.call-start = ((), (), s32[]{:S(2)}) async-start(), calls=%async_computation.1 | async-start | bytes 3342336 | tf_op jit(solution)/shard_map/all_gather | solution.py:417
  9.1 102.5 %reduce-scatter.2.cloned.1.call-start = ((), (), s32[]{:S(2)}) async-start(), calls=%async_computation.2 | async-start | bytes 3538944 | tf_op jit(solution)/shard_map/reduce_scatter | solution.py:410
  54.3 0.7 copy-start.1
  54.3 0.7 copy-start
  54.3 0.8 copy-start.2
Sparse Core Ops, SparseCore 0:
  10.0 44.7 all-gather.1
Sparse Core Ops, SparseCore 1:
  54.4 44.0 reduce-scatter.1

commit v12 on v11

--- a/solution.py
+++ b/solution.py
@@ -233,24 +233,24 @@
     for o in range(1, ny):
         g = lax.rem(ym + o, ny)
         copy(pa.at[g], ra.at[g], send1.at[0, g], recv1.at[0, g], red_y(g)).wait_recv()
-    for k in range(nx):
-        sa[k] = ra[0, k] + ra[1, k] + ra[2, k] + ra[3, k]
-    for o in range(1, nx):
-        g = lax.rem(xm + o, nx)
+    for o in range(1, nx):
+        g = lax.rem(xm + o, nx)
+        sa[g] = ra[0, g] + ra[1, g] + ra[2, g] + ra[3, g]
         c = copy(sa.at[g], qa.at[xm], send2.at[0, g], recv2.at[0, xm], red_x(g))
         c.start()
         sent.append(c)
+    sa[xm] = ra[0, xm] + ra[1, xm] + ra[2, xm] + ra[3, xm]
 
     for o in range(1, nx):
         g = lax.rem(xm + o, nx)
         copy(pb.at[g], rb.at[g], send1.at[1, g], recv1.at[1, g], red_x(g)).wait_recv()
-    for k in range(ny):
-        sb[k] = rb[0, k] + rb[1, k] + rb[2, k] + rb[3, k]
-    for o in range(1, ny):
-        g = lax.rem(ym + o, ny)
+    for o in range(1, ny):
+        g = lax.rem(ym + o, ny)
+        sb[g] = rb[0, g] + rb[1, g] + rb[2, g] + rb[3, g]
         c = copy(sb.at[g], qb.at[ym], send2.at[1, g], recv2.at[1, ym], red_y(g))
         c.start()
         sent.append(c)
+    sb[ym] = rb[0, ym] + rb[1, ym] + rb[2, ym] + rb[3, ym]
 
     for c in sent:
         c.wait_send()
@@ -405,6 +405,7 @@
         slab_rows * vir_local, occ_local * virt_width
     )
     gathered = _gather(swapped, n_red, 0)
+    gathered, amplitudes = lax.optimization_barrier((gathered, amplitudes))
     operand = gathered.reshape(n_blk // CORES, CORES, slab_rows * vir_local, occ_local * virt_width)
     product = _core_reduce(operand, cycle_ints, 4)
     cycle_own = lax.psum_scatter(product, "z", scatter_dimension=0, tiled=True)[0]

time: 121 us -> 159 us (1.31)
  waiting for transfers between devices: 0.06 us -> 38.7 us
    all_gather x1, waiting for transfers between devices: 0.01 us -> 38.6 us  [shards(): shard_piece = lax.all_gather(flat, ('z', 'core'), axis=0, tiled=False)]
  transfers between devices with their start and end apart: 2 -> 2, of which waited for: 0 -> 1; matrix products, arithmetic and copies ran while one was open for 1% -> 1% of each run, Pallas kernels for 83% -> 44%
where the time goes in v12:
time: 159 us
  Pallas kernels  100 us (63%)
  waiting for transfers between devices  38.7 us (24%)
  between operations  14.9 us (9%)
  local copies, waits for them, and re-layouts  2.61 us (2%)
  other arithmetic  2.2 us (1%)
    pallas_call x1, Pallas kernels, _reduce(): pl.pallas_call(functools.partial(_reduce_kernel, n_red), out_shape=jax.Sh...  55.8 us
    all_gather x1, waiting for transfers between devices, shards(): shard_piece = lax.all_gather(flat, ('z', 'core'), axis=0, tiled=False)  38.6 us
    pallas_call x1, Pallas kernels, _gather(): pl.pallas_call(functools.partial(_gather_kernel, n_red), out_shape=jax.Sh...  31.1 us
    pallas_call x1, Pallas kernels, _core_reduce(): pl.pallas_call(_core_reduce_kernel, out_shape=jax.ShapeDtypeStruct((n_z,...  13.5 us
  transfers between devices with their start and end apart: 2, of which 1 were waited for; matrix products, arithmetic and copies ran while one was open for 1% of the time, Pallas kernels for 44%

profile of v12, /device:TPU:1, one launch (start us, length us, event | category | flops | bytes accessed | tf_op | source)
XLA Modules:
  0.0 158.9 jit_solution(9957273872402246705)
XLA Ops:
  7.4 0.0 copy-start
  7.4 0.0 all-gather.2.cloned.1.call-start
  7.4 31.1 %shard_map.64 = bf16[4,4,64,1536]{3,2,1,0:T(8,128)(2,1)} custom-call(bf16[64,1536]{1,0:T(8,128)(2,1)} %bitcast.18), custom_call_target="tpu_custom_call" | custom-call | bytes 6291456 | tf_op jit(solution)/shard_map/pallas_call | solution.py:173
  38.5 0.0 copy-done
  38.5 0.8 all_gather_reshape.3
  39.3 0.0 all-gather.2.cloned.1.call-update
  39.3 0.0 reduce-scatter.2.cloned.1.call-start
  39.4 13.5 %shard_map.66 = f32[8,64,1536]{2,1,0:T(8,128)} custom-call(bf16[8,2,64,1536]{3,2,1,0:T(8,128)(2,1)} %bitcast.16, bf16[1536,1536]{1,0:T(8,128)(2,1)} %ints_ref.3), custom_call_target="tpu_custom_call" | custom-call | flops 4831838208 | bytes 11010048 | tf_op jit(solution)/shard_map/pallas_call | solution.py:345
  52.8 0.0 copy-start.1
  52.9 0.0 copy-start.2
  52.9 0.0 copy-start.3
  52.9 0.0 reduce-scatter.2.cloned.1.call-update
  52.9 0.6 copy-done.1
  53.5 0.1 dynamic_slice.7
  53.6 0.0 copy-done.2
  53.6 0.1 dynamic_slice.6
  53.7 0.0 copy-done.3
  53.7 0.2 select_reduce_fusion
  53.9 0.1 broadcast_add_fusion
  53.9 0.1 broadcast_subtract_fusion
  54.0 38.6 %all-gather.2.cloned.1.call-done = bf16[16,96,1024]{2,1,0:T(8,128)(2,1)} async-done(((bf16[1,96,1024]{2,1,0:T(8,128)(2,1)}), bf16[16,96,1024]{2,1,0:T(8,128)(2,1)}) %all-gather.2.cloned.1.call-update) | async-done | bytes 3145744 | tf_op jit(solution)/shard_map/all_gather | solution.py:418
  92.7 55.8 %shard_map.65 = f32[96,1024]{1,0:T(8,128)} custom-call(bf16[4,4,96,1024]{3,2,1,0:T(8,128)(2,1)} %bitcast.20, bf16[1024,1024]{1,0:T(8,128)(2,1)} %ints_ref.2), custom_call_target="tpu_custom_call" | custom-call | flops 3221225472 | bytes 5636096 | tf_op jit(solution)/shard_map/pallas_call | solution.py:276
  148.5 1.1 copy.7
  149.6 0.0 reduce-scatter.2.cloned.1.call-done
  149.6 1.9 %fusion = f32[8,12,8,128]{3,2,1,0:T(8,128)} fusion(f32[8,12,8,128]{3,2,1,0:T(8,128)S(1)} %bitcast.17, f32[1,64,1536]{2,1,0:T(8,128)} %reduce-scatter.2.cloned.1.call-done, f32[12]{0:T(128)S(1)} %dynamic_slice.7, f32[8,8,128]{2,1,0:T(8,128)S(1)} %broadcast_subtract_fusion), kind=kLoop, calls=%fused_computation.1 | loop fusion | flops 294912 | bytes 1212464 | tf_op jit(solution)/shard_map/div | solution.py:436
Async XLA Ops:
  7.4 31.1 %copy-start = (bf16[8,12,8,128]{3,2,1,0:T(8,128)(2,1)S(1)}, bf16[8,12,8,128]{3,2,1,0:T(8,128)(2,1)}, u32[]{:S(2)}) copy-start(bf16[8,12,8,128]{3,2,1,0:T(8,128)(2,1)} %param.6) | copy-start | bytes 589828
  7.4 85.3 %all-gather.2.cloned.1.call-start = ((), (), s32[]{:S(2)}) async-start(), calls=%async_computation.1 | async-start | bytes 3342336 | tf_op jit(solution)/shard_map/all_gather | solution.py:418
  39.3 110.3 %reduce-scatter.2.cloned.1.call-start = ((), (), s32[]{:S(2)}) async-start(), calls=%async_computation.2 | async-start | bytes 3538944 | tf_op jit(solution)/shard_map/reduce_scatter | solution.py:411
  52.8 0.7 copy-start.1
  52.9 0.7 copy-start.2
  52.9 0.8 copy-start.3
Sparse Core Ops, SparseCore 0:
  39.4 53.1 all-gather.1
Sparse Core Ops, SparseCore 1:
  53.0 50.9 reduce-scatter.1

commit v13 on v12

--- a/solution.py
+++ b/solution.py
@@ -405,7 +405,6 @@
         slab_rows * vir_local, occ_local * virt_width
     )
     gathered = _gather(swapped, n_red, 0)
-    gathered, amplitudes = lax.optimization_barrier((gathered, amplitudes))
     operand = gathered.reshape(n_blk // CORES, CORES, slab_rows * vir_local, occ_local * virt_width)
     product = _core_reduce(operand, cycle_ints, 4)
     cycle_own = lax.psum_scatter(product, "z", scatter_dimension=0, tiled=True)[0]

time: 159 us -> 121 us (0.76)
  waiting for transfers between devices: 38.7 us -> 0.06 us
    all_gather x1, waiting for transfers between devices: 38.6 us -> 0.01 us  [shards(): shard_piece = lax.all_gather(flat, ('z', 'core'), axis=0, tiled=False)]
  transfers between devices with their start and end apart: 2 -> 2, of which waited for: 1 -> 0; matrix products, arithmetic and copies ran while one was open for 1% -> 1% of each run, Pallas kernels for 44% -> 83%
where the time goes in v13:
time: 121 us
  Pallas kernels  100 us (83%)
  between operations  14.9 us (12%)
  local copies, waits for them, and re-layouts  3.51 us (3%)
  other arithmetic  2.2 us (2%)
    pallas_call x1, Pallas kernels, _reduce(): pl.pallas_call(functools.partial(_reduce_kernel, n_red), out_shape=jax.Sh...  55 us
    pallas_call x1, Pallas kernels, _gather(): pl.pallas_call(functools.partial(_gather_kernel, n_red), out_shape=jax.Sh...  31.3 us
    pallas_call x1, Pallas kernels, _core_reduce(): pl.pallas_call(_core_reduce_kernel, out_shape=jax.ShapeDtypeStruct((n_z,...  13.8 us
  transfers between devices with their start and end apart: 2, of which 0 were waited for; matrix products, arithmetic and copies ran while one was open for 1% of the time, Pallas kernels for 83%

profile of v13, /device:TPU:1, one launch (start us, length us, event | category | flops | bytes accessed | tf_op | source)
XLA Modules:
  0.0 120.9 jit_solution(10577528573325111086)
XLA Ops:
  7.4 0.0 all-gather.2.cloned.1.call-start
  7.4 1.7 %all_gather_reshape.3 = bf16[1,96,1024]{2,1,0:T(8,128)(2,1)} reshape(bf16[8,12,8,128]{3,2,1,0:T(8,128)(2,1)} %param.6) | data formatting | bytes 393216 | tf_op jit(solution)/shard_map/all_gather;reshape | solution.py:417
  9.1 0.0 all-gather.2.cloned.1.call-update
  9.1 0.0 reduce-scatter.2.cloned.1.call-start
  9.1 31.3 %shard_map.65 = bf16[4,4,64,1536]{3,2,1,0:T(8,128)(2,1)} custom-call(bf16[64,1536]{1,0:T(8,128)(2,1)} %bitcast.18), custom_call_target="tpu_custom_call" | custom-call | bytes 6291456 | tf_op jit(solution)/shard_map/pallas_call | solution.py:173
  40.5 13.8 %shard_map.66 = f32[8,64,1536]{2,1,0:T(8,128)} custom-call(bf16[8,2,64,1536]{3,2,1,0:T(8,128)(2,1)} %bitcast.16, bf16[1536,1536]{1,0:T(8,128)(2,1)} %ints_ref.3), custom_call_target="tpu_custom_call" | custom-call | flops 4831838208 | bytes 11010048 | tf_op jit(solution)/shard_map/pallas_call | solution.py:345
  54.3 0.0 copy-start.1
  54.3 0.0 copy-start
  54.3 0.0 copy-start.2
  54.3 0.0 reduce-scatter.2.cloned.1.call-update
  54.3 0.6 copy-done.1
  54.9 0.1 dynamic_slice.6
  55.0 0.0 copy-done
  55.0 0.1 dynamic_slice.7
  55.1 0.0 copy-done.2
  55.1 0.2 select_reduce_fusion
  55.2 0.1 broadcast_add_fusion
  55.3 0.1 broadcast_subtract_fusion
  55.4 0.0 all-gather.2.cloned.1.call-done
  55.4 55.0 %shard_map.64 = f32[96,1024]{1,0:T(8,128)} custom-call(bf16[4,4,96,1024]{3,2,1,0:T(8,128)(2,1)} %bitcast.20, bf16[1024,1024]{1,0:T(8,128)(2,1)} %ints_ref.2), custom_call_target="tpu_custom_call" | custom-call | flops 3221225472 | bytes 5636096 | tf_op jit(solution)/shard_map/pallas_call | solution.py:276
  110.4 1.1 copy.7
  111.5 0.0 reduce-scatter.2.cloned.1.call-done
  111.5 1.9 %fusion = f32[8,12,8,128]{3,2,1,0:T(8,128)} fusion(f32[8,12,8,128]{3,2,1,0:T(8,128)S(1)} %bitcast.17, f32[1,64,1536]{2,1,0:T(8,128)} %reduce-scatter.2.cloned.1.call-done, f32[12]{0:T(128)S(1)} %dynamic_slice.7, f32[8,8,128]{2,1,0:T(8,128)S(1)} %broadcast_subtract_fusion), kind=kLoop, calls=%fused_computation.1 | loop fusion | flops 294912 | bytes 1212464 | tf_op jit(solution)/shard_map/div | solution.py:435
Async XLA Ops:
  7.4 48.0 %all-gather.2.cloned.1.call-start = ((), (), s32[]{:S(2)}) async-start(), calls=%async_computation.1 | async-start | bytes 3342336 | tf_op jit(solution)/shard_map/all_gather | solution.py:417
  9.1 102.5 %reduce-scatter.2.cloned.1.call-start = ((), (), s32[]{:S(2)}) async-start(), calls=%async_computation.2 | async-start | bytes 3538944 | tf_op jit(solution)/shard_map/reduce_scatter | solution.py:410
  54.3 0.7 copy-start.1
  54.3 0.7 copy-start
  54.3 0.8 copy-start.2
Sparse Core Ops, SparseCore 0:
  10.0 44.7 all-gather.1
Sparse Core Ops, SparseCore 1:
  54.4 44.0 reduce-scatter.1

commit v14 on v13

--- a/solution.py
+++ b/solution.py
@@ -197,7 +197,6 @@
         pl.semaphore_signal(barrier, inc=1, device_id=(*row, red_y(lax.rem(ym + o, ny))), device_id_type=MESH)
     for o in range(1, nx):
         pl.semaphore_signal(barrier, inc=1, device_id=(*row, red_x(lax.rem(xm + o, nx))), device_id_type=MESH)
-    pl.semaphore_wait(barrier, ny - 1 + nx - 1)
 
     def copy(src, dst, send, recv, dev):
         return pltpu.make_async_remote_copy(
@@ -213,17 +212,22 @@
         product = jnp.dot(flat, ints_ref[...], preferred_element_type=jnp.float32)
         return product.reshape(slots, half, width)
 
+    pa[lax.rem(ym + 1, ny)] = block(amp_ref[:, lax.rem(ym + 1, ny), first])
+    pb[lax.rem(xm + 1, nx)] = block(amp_ref[lax.rem(xm + 1, nx), :, second])
+    pl.semaphore_wait(barrier, ny - 1 + nx - 1)
     sent = []
     for o in range(1, max(nx, ny)):
         if o < ny:
             g = lax.rem(ym + o, ny)
-            pa[g] = block(amp_ref[:, g, first])
+            if o > 1:
+                pa[g] = block(amp_ref[:, g, first])
             c = copy(pa.at[g], ra.at[ym], send1.at[0, g], recv1.at[0, ym], red_y(g))
             c.start()
             sent.append(c)
         if o < nx:
             g = lax.rem(xm + o, nx)
-            pb[g] = block(amp_ref[g, :, second])
+            if o > 1:
+                pb[g] = block(amp_ref[g, :, second])
             c = copy(pb.at[g], rb.at[xm], send1.at[1, g], recv1.at[1, xm], red_x(g))
             c.start()
             sent.append(c)
@@ -311,7 +315,6 @@
     step = n_z // 2
     barrier = pltpu.get_barrier_semaphore()
     pl.semaphore_signal(barrier, inc=1, device_id=(z, other, red), device_id_type=MESH)
-    pl.semaphore_wait(barrier, 1)
 
     def block(k, which):
         lhs = amp_ref[pl.ds(k * step, step), which]
@@ -323,6 +326,8 @@
     sends = []
     for k in range(2):
         mine_sent[pl.ds(k * step, step)] = block(k, other)
+        if k == 0:
+            pl.semaphore_wait(barrier, 1)
         c = pltpu.make_async_remote_copy(
             src_ref=mine_sent.at[pl.ds(k * step, step)], dst_ref=theirs.at[pl.ds(k * step, step)],
             send_sem=send_sem.at[k], recv_sem=recv_sem.at[k],

time: 121 us -> 120 us (level)
  no operation moved by 1% of the time
where the time goes in v14:
time: 120 us
  Pallas kernels  99 us (82%)
  between operations  14.9 us (12%)
  local copies, waits for them, and re-layouts  3.51 us (3%)
  other arithmetic  2.2 us (2%)
    pallas_call x1, Pallas kernels, _reduce(): pl.pallas_call(functools.partial(_reduce_kernel, n_red), out_shape=jax.Sh...  54 us
    pallas_call x1, Pallas kernels, _gather(): pl.pallas_call(functools.partial(_gather_kernel, n_red), out_shape=jax.Sh...  31.3 us
    pallas_call x1, Pallas kernels, _core_reduce(): pl.pallas_call(_core_reduce_kernel, out_shape=jax.ShapeDtypeStruct((n_z,...  13.6 us
  transfers between devices with their start and end apart: 2, of which 0 were waited for; matrix products, arithmetic and copies ran while one was open for 1% of the time, Pallas kernels for 83%

profile of v14, /device:TPU:1, one launch (start us, length us, event | category | flops | bytes accessed | tf_op | source)
XLA Modules:
  0.0 119.7 jit_solution(4159682073951482645)
XLA Ops:
  7.4 0.0 all-gather.2.cloned.1.call-start
  7.4 1.7 %all_gather_reshape.3 = bf16[1,96,1024]{2,1,0:T(8,128)(2,1)} reshape(bf16[8,12,8,128]{3,2,1,0:T(8,128)(2,1)} %param.6) | data formatting | bytes 393216 | tf_op jit(solution)/shard_map/all_gather;reshape | solution.py:422
  9.1 0.0 all-gather.2.cloned.1.call-update
  9.1 0.0 reduce-scatter.2.cloned.1.call-start
  9.1 31.3 %shard_map.65 = bf16[4,4,64,1536]{3,2,1,0:T(8,128)(2,1)} custom-call(bf16[64,1536]{1,0:T(8,128)(2,1)} %bitcast.18), custom_call_target="tpu_custom_call" | custom-call | bytes 6291456 | tf_op jit(solution)/shard_map/pallas_call | solution.py:173
  40.5 13.6 %shard_map.66 = f32[8,64,1536]{2,1,0:T(8,128)} custom-call(bf16[8,2,64,1536]{3,2,1,0:T(8,128)(2,1)} %bitcast.16, bf16[1536,1536]{1,0:T(8,128)(2,1)} %ints_ref.3), custom_call_target="tpu_custom_call" | custom-call | flops 4831838208 | bytes 11010048 | tf_op jit(solution)/shard_map/pallas_call | solution.py:350
  54.1 0.0 copy-start.1
  54.1 0.0 copy-start
  54.1 0.0 copy-start.2
  54.1 0.0 reduce-scatter.2.cloned.1.call-update
  54.2 0.6 copy-done.1
  54.8 0.1 dynamic_slice.6
  54.8 0.0 copy-done
  54.8 0.1 dynamic_slice.7
  54.9 0.0 copy-done.2
  54.9 0.2 select_reduce_fusion
  55.1 0.1 broadcast_add_fusion
  55.2 0.1 broadcast_subtract_fusion
  55.2 0.0 all-gather.2.cloned.1.call-done
  55.2 54.0 %shard_map.64 = f32[96,1024]{1,0:T(8,128)} custom-call(bf16[4,4,96,1024]{3,2,1,0:T(8,128)(2,1)} %bitcast.20, bf16[1024,1024]{1,0:T(8,128)(2,1)} %ints_ref.2), custom_call_target="tpu_custom_call" | custom-call | flops 3221225472 | bytes 5636096 | tf_op jit(solution)/shard_map/pallas_call | solution.py:280
  109.3 1.1 copy.7
  110.3 0.0 reduce-scatter.2.cloned.1.call-done
  110.4 1.9 %fusion = f32[8,12,8,128]{3,2,1,0:T(8,128)} fusion(f32[8,12,8,128]{3,2,1,0:T(8,128)S(1)} %bitcast.17, f32[1,64,1536]{2,1,0:T(8,128)} %reduce-scatter.2.cloned.1.call-done, f32[12]{0:T(128)S(1)} %dynamic_slice.7, f32[8,8,128]{2,1,0:T(8,128)S(1)} %broadcast_subtract_fusion), kind=kLoop, calls=%fused_computation.1 | loop fusion | flops 294912 | bytes 1212464 | tf_op jit(solution)/shard_map/div | solution.py:440
Async XLA Ops:
  7.4 47.9 %all-gather.2.cloned.1.call-start = ((), (), s32[]{:S(2)}) async-start(), calls=%async_computation.1 | async-start | bytes 3342336 | tf_op jit(solution)/shard_map/all_gather | solution.py:422
  9.1 101.3 %reduce-scatter.2.cloned.1.call-start = ((), (), s32[]{:S(2)}) async-start(), calls=%async_computation.2 | async-start | bytes 3538944 | tf_op jit(solution)/shard_map/reduce_scatter | solution.py:415
  54.1 0.7 copy-start.1
  54.1 0.7 copy-start
  54.1 0.8 copy-start.2
Sparse Core Ops, SparseCore 0:
  10.0 44.7 all-gather.1
Sparse Core Ops, SparseCore 1:
  54.2 43.8 reduce-scatter.1

commit v15 on v14

--- a/solution.py
+++ b/solution.py
@@ -8,7 +8,6 @@
 from jax.sharding import Mesh, PartitionSpec as P
 
 MESH = pl.DeviceIdType.MESH
-PIECES = 1
 
 
 NY = 4
@@ -27,57 +26,6 @@
     if kind == "x":
         return x, n_red // NY, lambda pos: pos * NY + y
     return r, n_red, lambda pos: pos
-
-
-def _exchange_kernel(jobs, n_in, n_out, n_red, *refs):
-    ins, outs = refs[:n_in], refs[n_in:n_in + n_out]
-    send_sem, recv_sem, local_sem = refs[n_in + n_out:]
-    row = _row()
-
-    barrier = pltpu.get_barrier_semaphore()
-    count = 0
-    for kind in sorted(set(job[0] for job in jobs)):
-        me, n, red_of = _group(kind, n_red)
-        for o in range(1, n):
-            pl.semaphore_signal(
-                barrier, inc=1, device_id=(*row, red_of(lax.rem(me + o, n))), device_id_type=MESH
-            )
-            count += 1
-    pl.semaphore_wait(barrier, count)
-
-    def remote(j, pos, slot, piece=None):
-        kind, si, src_view, di, dst_view = jobs[j]
-        _, _, red_of = _group(kind, n_red)
-        src, dst = src_view(ins[si], pos), dst_view(outs[di], slot)
-        if piece is not None:
-            size = src.shape[0] // PIECES
-            src, dst = src.at[pl.ds(piece * size, size)], dst.at[pl.ds(piece * size, size)]
-        return pltpu.make_async_remote_copy(
-            src_ref=src,
-            dst_ref=dst,
-            send_sem=send_sem.at[j, pos],
-            recv_sem=recv_sem.at[j, slot],
-            device_id=(*row, red_of(pos)),
-            device_id_type=MESH,
-        )
-
-    for piece in range(PIECES):
-        for j, job in enumerate(jobs):
-            me, n, _ = _group(job[0], n_red)
-            for o in range(1, n):
-                remote(j, lax.rem(me + o, n), me, piece).start()
-    for j, (kind, si, src_view, di, dst_view) in enumerate(jobs):
-        me, n, _ = _group(kind, n_red)
-        local = pltpu.make_async_copy(
-            src_view(ins[si], me), dst_view(outs[di], me), local_sem.at[j]
-        )
-        local.start()
-        local.wait()
-    for j, job in enumerate(jobs):
-        me, n, _ = _group(job[0], n_red)
-        for o in range(1, n):
-            g = lax.rem(me + o, n)
-            remote(j, g, g).wait()
 
 
 def _gather_kernel(n_red, src_ref, out_ref, send_sem, recv_sem, local_sem):
@@ -368,36 +316,6 @@
     )(amp, ints)
 
 
-def _exchange(jobs, srcs, out_shapes, n_red, collective_id):
-    nbytes = sum(s.size * s.dtype.itemsize for s in srcs)
-    nmax = max(_group_size(job[0], n_red) for job in jobs)
-    return pl.pallas_call(
-        functools.partial(_exchange_kernel, tuple(jobs), len(srcs), len(out_shapes), n_red),
-        out_shape=tuple(jax.ShapeDtypeStruct(s, d) for s, d in out_shapes),
-        in_specs=[pl.BlockSpec(memory_space=pl.ANY)] * len(srcs),
-        out_specs=tuple(pl.BlockSpec(memory_space=pl.ANY) for _ in out_shapes),
-        scratch_shapes=[
-            pltpu.SemaphoreType.DMA((len(jobs), nmax)),
-            pltpu.SemaphoreType.DMA((len(jobs), nmax)),
-            pltpu.SemaphoreType.DMA((len(jobs),)),
-        ],
-        compiler_params=pltpu.CompilerParams(collective_id=collective_id, has_side_effects=True),
-        cost_estimate=pl.CostEstimate(flops=0, bytes_accessed=4 * nbytes, transcendentals=0),
-    )(*srcs)
-
-
-def _group_size(kind, n_red):
-    return {"y": NY, "x": n_red // NY}.get(kind, n_red)
-
-
-def _whole(ref, pos):
-    return ref
-
-
-def _slot(ref, pos):
-    return ref.at[pos]
-
-
 def shards(amplitudes, ladder_ints, cycle_ints, occ_energy, vir_energy, slab_index):
     slab_rows, occ_local, vir_local, virt_width = amplitudes.shape
     n_red = lax.axis_size("red")

time: 120 us -> 120 us (level)
  no operation moved by 1% of the time
where the time goes in v15:
time: 120 us
  Pallas kernels  99 us (82%)
  between operations  14.9 us (12%)
  local copies, waits for them, and re-layouts  3.51 us (3%)
  other arithmetic  2.2 us (2%)
    pallas_call x1, Pallas kernels, _reduce(): pl.pallas_call(functools.partial(_reduce_kernel, n_red), out_shape=jax.Sh...  54 us
    pallas_call x1, Pallas kernels, _gather(): pl.pallas_call(functools.partial(_gather_kernel, n_red), out_shape=jax.Sh...  31.3 us
    pallas_call x1, Pallas kernels, _core_reduce(): pl.pallas_call(_core_reduce_kernel, out_shape=jax.ShapeDtypeStruct((n_z,...  13.6 us
  transfers between devices with their start and end apart: 2, of which 0 were waited for; matrix products, arithmetic and copies ran while one was open for 1% of the time, Pallas kernels for 83%

profile of v15, /device:TPU:1, one launch (start us, length us, event | category | flops | bytes accessed | tf_op | source)
XLA Modules:
  0.0 119.7 jit_solution(4159682073951482645)
XLA Ops:
  7.4 0.0 all-gather.2.cloned.1.call-start
  7.4 1.7 %all_gather_reshape.3 = bf16[1,96,1024]{2,1,0:T(8,128)(2,1)} reshape(bf16[8,12,8,128]{3,2,1,0:T(8,128)(2,1)} %param.6) | data formatting | bytes 393216 | tf_op jit(solution)/shard_map/all_gather;reshape | solution.py:340
  9.1 0.0 all-gather.2.cloned.1.call-update
  9.1 0.0 reduce-scatter.2.cloned.1.call-start
  9.1 31.3 %shard_map.65 = bf16[4,4,64,1536]{3,2,1,0:T(8,128)(2,1)} custom-call(bf16[64,1536]{1,0:T(8,128)(2,1)} %bitcast.18), custom_call_target="tpu_custom_call" | custom-call | bytes 6291456 | tf_op jit(solution)/shard_map/pallas_call | solution.py:121
  40.5 13.6 %shard_map.66 = f32[8,64,1536]{2,1,0:T(8,128)} custom-call(bf16[8,2,64,1536]{3,2,1,0:T(8,128)(2,1)} %bitcast.16, bf16[1536,1536]{1,0:T(8,128)(2,1)} %ints_ref.3), custom_call_target="tpu_custom_call" | custom-call | flops 4831838208 | bytes 11010048 | tf_op jit(solution)/shard_map/pallas_call | solution.py:298
  54.1 0.0 copy-start.1
  54.1 0.0 copy-start
  54.1 0.0 copy-start.2
  54.1 0.0 reduce-scatter.2.cloned.1.call-update
  54.2 0.6 copy-done.1
  54.8 0.1 dynamic_slice.6
  54.8 0.0 copy-done
  54.8 0.1 dynamic_slice.7
  54.9 0.0 copy-done.2
  54.9 0.2 select_reduce_fusion
  55.1 0.1 broadcast_add_fusion
  55.2 0.1 broadcast_subtract_fusion
  55.2 0.0 all-gather.2.cloned.1.call-done
  55.2 54.0 %shard_map.64 = f32[96,1024]{1,0:T(8,128)} custom-call(bf16[4,4,96,1024]{3,2,1,0:T(8,128)(2,1)} %bitcast.20, bf16[1024,1024]{1,0:T(8,128)(2,1)} %ints_ref.2), custom_call_target="tpu_custom_call" | custom-call | flops 3221225472 | bytes 5636096 | tf_op jit(solution)/shard_map/pallas_call | solution.py:228
  109.3 1.1 copy.7
  110.3 0.0 reduce-scatter.2.cloned.1.call-done
  110.4 1.9 %fusion = f32[8,12,8,128]{3,2,1,0:T(8,128)} fusion(f32[8,12,8,128]{3,2,1,0:T(8,128)S(1)} %bitcast.17, f32[1,64,1536]{2,1,0:T(8,128)} %reduce-scatter.2.cloned.1.call-done, f32[12]{0:T(128)S(1)} %dynamic_slice.7, f32[8,8,128]{2,1,0:T(8,128)S(1)} %broadcast_subtract_fusion), kind=kLoop, calls=%fused_computation.1 | loop fusion | flops 294912 | bytes 1212464 | tf_op jit(solution)/shard_map/div | solution.py:358
Async XLA Ops:
  7.4 47.9 %all-gather.2.cloned.1.call-start = ((), (), s32[]{:S(2)}) async-start(), calls=%async_computation.1 | async-start | bytes 3342336 | tf_op jit(solution)/shard_map/all_gather | solution.py:340
  9.1 101.3 %reduce-scatter.2.cloned.1.call-start = ((), (), s32[]{:S(2)}) async-start(), calls=%async_computation.2 | async-start | bytes 3538944 | tf_op jit(solution)/shard_map/reduce_scatter | solution.py:333
  54.1 0.7 copy-start.1
  54.1 0.7 copy-start
  54.1 0.8 copy-start.2
Sparse Core Ops, SparseCore 0:
  10.0 44.7 all-gather.1
Sparse Core Ops, SparseCore 1:
  54.2 43.8 reduce-scatter.1

commit v16 on v15

--- a/solution.py
+++ b/solution.py
@@ -12,6 +12,7 @@
 
 NY = 4
 CORES = 2
+LANES = 128
 
 
 def _row():
@@ -216,8 +217,9 @@
         g = lax.rem(ym + o, ny)
         copy(sb.at[g], qb.at[g], send2.at[1, g], recv2.at[1, g], red_y(g)).wait_recv()
         total_b = total_b + qb[g]
-    out_ref[first] = total_a
-    out_ref[second] = total_b
+    lanes = out_ref.shape[2]
+    out_ref[first] = total_a.reshape(half, width // lanes, lanes)
+    out_ref[second] = total_b.reshape(half, width // lanes, lanes)
 
 
 def _reduce(amp, ints, n_red, collective_id):
@@ -227,7 +229,7 @@
     f32 = jnp.float32
     return pl.pallas_call(
         functools.partial(_reduce_kernel, n_red),
-        out_shape=jax.ShapeDtypeStruct((rows, cols), f32),
+        out_shape=jax.ShapeDtypeStruct((rows, cols // LANES, LANES), f32),
         in_specs=[pl.BlockSpec(memory_space=pltpu.VMEM)] * 2,
         out_specs=pl.BlockSpec(memory_space=pltpu.VMEM),
         scratch_shapes=[

time: 120 us -> 119 us (level)
  transfers between devices with their start and end apart: 2 -> 2, of which waited for: 0 -> 0; matrix products, arithmetic and copies ran while one was open for 1% -> 0% of each run, Pallas kernels for 83% -> 83%
where the time goes in v16:
time: 119 us
  Pallas kernels  99 us (83%)
  between operations  14.9 us (13%)
  local copies, waits for them, and re-layouts  2.44 us (2%)
  other arithmetic  2.32 us (2%)
    pallas_call x1, Pallas kernels, _reduce(): pl.pallas_call(functools.partial(_reduce_kernel, n_red), out_shape=jax.Sh...  54.1 us
    pallas_call x1, Pallas kernels, _gather(): pl.pallas_call(functools.partial(_gather_kernel, n_red), out_shape=jax.Sh...  31.3 us
    pallas_call x1, Pallas kernels, _core_reduce(): pl.pallas_call(_core_reduce_kernel, out_shape=jax.ShapeDtypeStruct((n_z,...  13.6 us
  transfers between devices with their start and end apart: 2, of which 0 were waited for; matrix products, arithmetic and copies ran while one was open for 0% of the time, Pallas kernels for 83%

profile of v16, /device:TPU:1, one launch (start us, length us, event | category | flops | bytes accessed | tf_op | source)
XLA Modules:
  0.0 118.8 jit_solution(1478480200522324194)
XLA Ops:
  7.4 0.0 all-gather.2.cloned.1.call-start
  7.4 1.7 %all_gather_reshape.3 = bf16[1,96,1024]{2,1,0:T(8,128)(2,1)} reshape(bf16[8,12,8,128]{3,2,1,0:T(8,128)(2,1)} %param.6) | data formatting | bytes 393216 | tf_op jit(solution)/shard_map/all_gather;reshape | solution.py:342
  9.1 0.0 all-gather.2.cloned.1.call-update
  9.1 0.0 reduce-scatter.2.cloned.1.call-start
  9.1 31.3 %shard_map.65 = bf16[4,4,64,1536]{3,2,1,0:T(8,128)(2,1)} custom-call(bf16[64,1536]{1,0:T(8,128)(2,1)} %bitcast.15), custom_call_target="tpu_custom_call" | custom-call | bytes 6291456 | tf_op jit(solution)/shard_map/pallas_call | solution.py:122
  40.5 13.6 %shard_map.66 = f32[8,64,1536]{2,1,0:T(8,128)} custom-call(bf16[8,2,64,1536]{3,2,1,0:T(8,128)(2,1)} %bitcast.14, bf16[1536,1536]{1,0:T(8,128)(2,1)} %ints_ref.3), custom_call_target="tpu_custom_call" | custom-call | flops 4831838208 | bytes 11010048 | tf_op jit(solution)/shard_map/pallas_call | solution.py:300
  54.1 0.0 copy-start.1
  54.1 0.0 copy-start
  54.1 0.0 copy-start.2
  54.1 0.0 reduce-scatter.2.cloned.1.call-update
  54.2 0.6 copy-done.1
  54.8 0.1 dynamic_slice.6
  54.8 0.0 copy-done
  54.8 0.1 dynamic_slice.7
  54.9 0.0 copy-done.2
  54.9 0.2 select_reduce_fusion
  55.1 0.1 broadcast_add_fusion
  55.2 0.1 broadcast_subtract_fusion
  55.2 0.0 all-gather.2.cloned.1.call-done
  55.2 54.1 %shard_map.64 = f32[96,8,128]{2,1,0:T(8,128)} custom-call(bf16[4,4,96,1024]{3,2,1,0:T(8,128)(2,1)} %bitcast.17, bf16[1024,1024]{1,0:T(8,128)(2,1)} %ints_ref.2), custom_call_target="tpu_custom_call" | custom-call | flops 3221225472 | bytes 5636096 | tf_op jit(solution)/shard_map/pallas_call | solution.py:230
  109.3 0.0 reduce-scatter.2.cloned.1.call-done
  109.3 2.0 %fusion = f32[8,12,8,128]{3,2,1,0:T(8,128)} fusion(f32[8,12,8,128]{3,2,1,0:T(8,128)} %bitcast.16, f32[1,64,1536]{2,1,0:T(8,128)} %reduce-scatter.2.cloned.1.call-done, f32[12]{0:T(128)S(1)} %dynamic_slice.7, f32[8,8,128]{2,1,0:T(8,128)S(1)} %broadcast_subtract_fusion), kind=kLoop, calls=%fused_computation.1 | loop fusion | flops 294912 | bytes 1212464 | tf_op jit(solution)/shard_map/div | solution.py:360
Async XLA Ops:
  7.4 47.9 %all-gather.2.cloned.1.call-start = ((), (), s32[]{:S(2)}) async-start(), calls=%async_computation.1 | async-start | bytes 3342336 | tf_op jit(solution)/shard_map/all_gather | solution.py:342
  9.1 100.3 %reduce-scatter.2.cloned.1.call-start = ((), (), s32[]{:S(2)}) async-start(), calls=%async_computation.2 | async-start | bytes 3538944 | tf_op jit(solution)/shard_map/reduce_scatter | solution.py:335
  54.1 0.7 copy-start.1
  54.1 0.7 copy-start
  54.1 0.8 copy-start.2
Sparse Core Ops, SparseCore 0:
  10.0 44.7 all-gather.1
Sparse Core Ops, SparseCore 1:
  54.2 43.8 reduce-scatter.1

commit v17 on v16

--- a/solution.py
+++ b/solution.py
@@ -285,12 +285,9 @@
         )
         c.start()
         sends.append(c)
-    for k in range(2):
-        out_ref[pl.ds(k * step, step)] = block(k, core)
     for k, c in enumerate(sends):
         c.wait()
-        for i in range(k * step, (k + 1) * step):
-            out_ref[i] = out_ref[i] + theirs[i]
+        out_ref[pl.ds(k * step, step)] = block(k, core) + theirs[pl.ds(k * step, step)]
 
 
 def _core_reduce(amp, ints, collective_id):

time: 119 us -> 119 us (level)
    pallas_call x1, Pallas kernels: 54.1 us -> 52.7 us  [_reduce(): pl.pallas_call(functools.partial(_reduce_kernel, n_red), out_shape=jax.Sh...]
    pallas_call x1, Pallas kernels: 13.6 us -> 14.8 us  [_core_reduce(): pl.pallas_call(_core_reduce_kernel, out_shape=jax.ShapeDtypeStruct((n_z,...]
where the time goes in v17:
time: 119 us
  Pallas kernels  98.9 us (83%)
  between operations  14.9 us (13%)
  local copies, waits for them, and re-layouts  2.44 us (2%)
  other arithmetic  2.32 us (2%)
    pallas_call x1, Pallas kernels, _reduce(): pl.pallas_call(functools.partial(_reduce_kernel, n_red), out_shape=jax.Sh...  52.7 us
    pallas_call x1, Pallas kernels, _gather(): pl.pallas_call(functools.partial(_gather_kernel, n_red), out_shape=jax.Sh...  31.3 us
    pallas_call x1, Pallas kernels, _core_reduce(): pl.pallas_call(_core_reduce_kernel, out_shape=jax.ShapeDtypeStruct((n_z,...  14.8 us
  transfers between devices with their start and end apart: 2, of which 0 were waited for; matrix products, arithmetic and copies ran while one was open for 0% of the time, Pallas kernels for 83%

profile of v17, /device:TPU:1, one launch (start us, length us, event | category | flops | bytes accessed | tf_op | source)
XLA Modules:
  0.0 118.6 jit_solution(1746050493456781074)
XLA Ops:
  7.4 0.0 all-gather.2.cloned.1.call-start
  7.4 1.7 %all_gather_reshape.3 = bf16[1,96,1024]{2,1,0:T(8,128)(2,1)} reshape(bf16[8,12,8,128]{3,2,1,0:T(8,128)(2,1)} %param.6) | data formatting | bytes 393216 | tf_op jit(solution)/shard_map/all_gather;reshape | solution.py:339
  9.1 0.0 all-gather.2.cloned.1.call-update
  9.1 0.0 reduce-scatter.2.cloned.1.call-start
  9.1 31.3 %shard_map.65 = bf16[4,4,64,1536]{3,2,1,0:T(8,128)(2,1)} custom-call(bf16[64,1536]{1,0:T(8,128)(2,1)} %bitcast.15), custom_call_target="tpu_custom_call" | custom-call | bytes 6291456 | tf_op jit(solution)/shard_map/pallas_call | solution.py:122
  40.5 14.8 %shard_map.66 = f32[8,64,1536]{2,1,0:T(8,128)} custom-call(bf16[8,2,64,1536]{3,2,1,0:T(8,128)(2,1)} %bitcast.14, bf16[1536,1536]{1,0:T(8,128)(2,1)} %ints_ref.3), custom_call_target="tpu_custom_call" | custom-call | flops 4831838208 | bytes 11010048 | tf_op jit(solution)/shard_map/pallas_call | solution.py:297
  55.3 0.0 copy-start.1
  55.3 0.0 copy-start
  55.3 0.0 copy-start.2
  55.4 0.0 reduce-scatter.2.cloned.1.call-update
  55.4 0.6 copy-done.1
  56.0 0.1 dynamic_slice.6
  56.1 0.0 copy-done
  56.1 0.1 dynamic_slice.7
  56.1 0.0 copy-done.2
  56.1 0.2 select_reduce_fusion
  56.3 0.1 broadcast_add_fusion
  56.4 0.1 broadcast_subtract_fusion
  56.5 0.0 all-gather.2.cloned.1.call-done
  56.5 52.7 %shard_map.64 = f32[96,8,128]{2,1,0:T(8,128)} custom-call(bf16[4,4,96,1024]{3,2,1,0:T(8,128)(2,1)} %bitcast.17, bf16[1024,1024]{1,0:T(8,128)(2,1)} %ints_ref.2), custom_call_target="tpu_custom_call" | custom-call | flops 3221225472 | bytes 5636096 | tf_op jit(solution)/shard_map/pallas_call | solution.py:230
  109.2 0.0 reduce-scatter.2.cloned.1.call-done
  109.2 2.0 %fusion = f32[8,12,8,128]{3,2,1,0:T(8,128)} fusion(f32[8,12,8,128]{3,2,1,0:T(8,128)} %bitcast.16, f32[1,64,1536]{2,1,0:T(8,128)} %reduce-scatter.2.cloned.1.call-done, f32[12]{0:T(128)S(1)} %dynamic_slice.7, f32[8,8,128]{2,1,0:T(8,128)S(1)} %broadcast_subtract_fusion), kind=kLoop, calls=%fused_computation.1 | loop fusion | flops 294912 | bytes 1212464 | tf_op jit(solution)/shard_map/div | solution.py:357
Async XLA Ops:
  7.4 49.1 %all-gather.2.cloned.1.call-start = ((), (), s32[]{:S(2)}) async-start(), calls=%async_computation.1 | async-start | bytes 3342336 | tf_op jit(solution)/shard_map/all_gather | solution.py:339
  9.1 100.1 %reduce-scatter.2.cloned.1.call-start = ((), (), s32[]{:S(2)}) async-start(), calls=%async_computation.2 | async-start | bytes 3538944 | tf_op jit(solution)/shard_map/reduce_scatter | solution.py:332
  55.3 0.7 copy-start.1
  55.3 0.7 copy-start
  55.3 0.8 copy-start.2
Sparse Core Ops, SparseCore 0:
  10.0 44.8 all-gather.1
Sparse Core Ops, SparseCore 1:
  55.5 43.8 reduce-scatter.1

commit v18 on v16

--- a/solution.py
+++ b/solution.py
@@ -262,20 +262,21 @@
     other = CORES - 1 - core
     n_z, _, rows, _ = amp_ref.shape
     width = ints_ref.shape[1]
-    step = n_z // 2
+    pieces = send_sem.shape[0]
     barrier = pltpu.get_barrier_semaphore()
     pl.semaphore_signal(barrier, inc=1, device_id=(z, other, red), device_id_type=MESH)
 
-    def block(k, which):
-        lhs = amp_ref[pl.ds(k * step, step), which]
+    def block(start, size, which):
+        lhs = amp_ref[pl.ds(start, size), which]
         product = jnp.dot(
-            lhs.reshape(step * rows, lhs.shape[2]), ints_ref[...], preferred_element_type=jnp.float32
-        )
-        return product.reshape(step, rows, width)
-
+            lhs.reshape(size * rows, lhs.shape[2]), ints_ref[...], preferred_element_type=jnp.float32
+        )
+        return product.reshape(size, rows, width)
+
+    step = n_z // pieces
     sends = []
-    for k in range(2):
-        mine_sent[pl.ds(k * step, step)] = block(k, other)
+    for k in range(pieces):
+        mine_sent[pl.ds(k * step, step)] = block(k * step, step, other)
         if k == 0:
             pl.semaphore_wait(barrier, 1)
         c = pltpu.make_async_remote_copy(
@@ -286,7 +287,7 @@
         c.start()
         sends.append(c)
     for k in range(2):
-        out_ref[pl.ds(k * step, step)] = block(k, core)
+        out_ref[pl.ds(k * (n_z // 2), n_z // 2)] = block(k * (n_z // 2), n_z // 2, core)
     for k, c in enumerate(sends):
         c.wait()
         for i in range(k * step, (k + 1) * step):
@@ -305,8 +306,8 @@
         scratch_shapes=[
             pltpu.VMEM((n_z, rows, cols), f32),
             pltpu.VMEM((n_z, rows, cols), f32),
-            pltpu.SemaphoreType.DMA((2,)),
-            pltpu.SemaphoreType.DMA((2,)),
+            pltpu.SemaphoreType.DMA((4,)),
+            pltpu.SemaphoreType.DMA((4,)),
         ],
         compiler_params=pltpu.CompilerParams(
             collective_id=collective_id, has_side_effects=True, vmem_limit_bytes=60 * 1024 * 1024

time: 119 us -> 119 us (level)
  transfers between devices with their start and end apart: 2 -> 2, of which waited for: 0 -> 1; matrix products, arithmetic and copies ran while one was open for 0% -> 0% of each run, Pallas kernels for 83% -> 83%
where the time goes in v18:
time: 119 us
  Pallas kernels  98.6 us (83%)
  between operations  14.9 us (13%)
  local copies, waits for them, and re-layouts  2.44 us (2%)
  other arithmetic  2.32 us (2%)
    pallas_call x1, Pallas kernels, _reduce(): pl.pallas_call(functools.partial(_reduce_kernel, n_red), out_shape=jax.Sh...  54.3 us
    pallas_call x1, Pallas kernels, _gather(): pl.pallas_call(functools.partial(_gather_kernel, n_red), out_shape=jax.Sh...  31.3 us
    pallas_call x1, Pallas kernels, _core_reduce(): pl.pallas_call(_core_reduce_kernel, out_shape=jax.ShapeDtypeStruct((n_z,...  13 us
  transfers between devices with their start and end apart: 2, of which 1 were waited for; matrix products, arithmetic and copies ran while one was open for 0% of the time, Pallas kernels for 83%

profile of v18, /device:TPU:1, one launch (start us, length us, event | category | flops | bytes accessed | tf_op | source)
XLA Modules:
  0.0 118.6 jit_solution(7141689478576531991)
XLA Ops:
  7.4 0.0 all-gather.2.cloned.1.call-start
  7.4 1.7 %all_gather_reshape.3 = bf16[1,96,1024]{2,1,0:T(8,128)(2,1)} reshape(bf16[8,12,8,128]{3,2,1,0:T(8,128)(2,1)} %param.6) | data formatting | bytes 393216 | tf_op jit(solution)/shard_map/all_gather;reshape | solution.py:343
  9.1 0.0 all-gather.2.cloned.1.call-update
  9.1 0.0 reduce-scatter.2.cloned.1.call-start
  9.1 31.3 %shard_map.65 = bf16[4,4,64,1536]{3,2,1,0:T(8,128)(2,1)} custom-call(bf16[64,1536]{1,0:T(8,128)(2,1)} %bitcast.15), custom_call_target="tpu_custom_call" | custom-call | bytes 6291456 | tf_op jit(solution)/shard_map/pallas_call | solution.py:122
  40.5 13.0 %shard_map.66 = f32[8,64,1536]{2,1,0:T(8,128)} custom-call(bf16[8,2,64,1536]{3,2,1,0:T(8,128)(2,1)} %bitcast.14, bf16[1536,1536]{1,0:T(8,128)(2,1)} %ints_ref.3), custom_call_target="tpu_custom_call" | custom-call | flops 4831838208 | bytes 11010048 | tf_op jit(solution)/shard_map/pallas_call | solution.py:301
  53.5 0.0 copy-start.1
  53.5 0.0 copy-start
  53.5 0.0 copy-start.2
  53.5 0.0 reduce-scatter.2.cloned.1.call-update
  53.5 0.6 copy-done.1
  54.1 0.1 dynamic_slice.6
  54.2 0.0 copy-done
  54.2 0.1 dynamic_slice.7
  54.3 0.0 copy-done.2
  54.3 0.2 select_reduce_fusion
  54.5 0.1 broadcast_add_fusion
  54.5 0.1 broadcast_subtract_fusion
  54.6 0.2 all-gather.2.cloned.1.call-done
  54.8 54.3 %shard_map.64 = f32[96,8,128]{2,1,0:T(8,128)} custom-call(bf16[4,4,96,1024]{3,2,1,0:T(8,128)(2,1)} %bitcast.17, bf16[1024,1024]{1,0:T(8,128)(2,1)} %ints_ref.2), custom_call_target="tpu_custom_call" | custom-call | flops 3221225472 | bytes 5636096 | tf_op jit(solution)/shard_map/pallas_call | solution.py:230
  109.2 0.0 reduce-scatter.2.cloned.1.call-done
  109.2 2.0 %fusion = f32[8,12,8,128]{3,2,1,0:T(8,128)} fusion(f32[8,12,8,128]{3,2,1,0:T(8,128)} %bitcast.16, f32[1,64,1536]{2,1,0:T(8,128)} %reduce-scatter.2.cloned.1.call-done, f32[12]{0:T(128)S(1)} %dynamic_slice.7, f32[8,8,128]{2,1,0:T(8,128)S(1)} %broadcast_subtract_fusion), kind=kLoop, calls=%fused_computation.1 | loop fusion | flops 294912 | bytes 1212464 | tf_op jit(solution)/shard_map/div | solution.py:361
Async XLA Ops:
  7.4 47.5 %all-gather.2.cloned.1.call-start = ((), (), s32[]{:S(2)}) async-start(), calls=%async_computation.1 | async-start | bytes 3342336 | tf_op jit(solution)/shard_map/all_gather | solution.py:343
  9.1 100.1 %reduce-scatter.2.cloned.1.call-start = ((), (), s32[]{:S(2)}) async-start(), calls=%async_computation.2 | async-start | bytes 3538944 | tf_op jit(solution)/shard_map/reduce_scatter | solution.py:336
  53.5 0.7 copy-start.1
  53.5 0.7 copy-start
  53.5 0.8 copy-start.2
Sparse Core Ops, SparseCore 0:
  10.0 44.7 all-gather.1
Sparse Core Ops, SparseCore 1:
  53.6 43.8 reduce-scatter.1

commit v19 on v18

--- a/solution.py
+++ b/solution.py
@@ -358,6 +358,7 @@
         - slab_energy[:, None, None, None]
         - pair_energy[None, :, None, None]
     )
+    denominator = lax.optimization_barrier(denominator)
     return (ladder_own + cycle_own) / denominator
 
 

time: 119 us -> 119 us (level)
  no operation moved by 1% of the time
where the time goes in v19:
time: 119 us
  Pallas kernels  98.6 us (83%)
  between operations  14.9 us (13%)
  local copies, waits for them, and re-layouts  2.44 us (2%)
  other arithmetic  2.35 us (2%)
    pallas_call x1, Pallas kernels, _reduce(): pl.pallas_call(functools.partial(_reduce_kernel, n_red), out_shape=jax.Sh...  54.3 us
    pallas_call x1, Pallas kernels, _gather(): pl.pallas_call(functools.partial(_gather_kernel, n_red), out_shape=jax.Sh...  31.3 us
    pallas_call x1, Pallas kernels, _core_reduce(): pl.pallas_call(_core_reduce_kernel, out_shape=jax.ShapeDtypeStruct((n_z,...  13 us
  transfers between devices with their start and end apart: 2, of which 1 were waited for; matrix products, arithmetic and copies ran while one was open for 0% of the time, Pallas kernels for 83%

profile of v19, /device:TPU:1, one launch (start us, length us, event | category | flops | bytes accessed | tf_op | source)
XLA Modules:
  0.0 118.6 jit_solution(10374264522635464838)
XLA Ops:
  7.4 0.0 all-gather.2.cloned.1.call-start
  7.4 1.7 %all_gather_reshape.3 = bf16[1,96,1024]{2,1,0:T(8,128)(2,1)} reshape(bf16[8,12,8,128]{3,2,1,0:T(8,128)(2,1)} %param.6) | data formatting | bytes 393216 | tf_op jit(solution)/shard_map/all_gather;reshape | solution.py:343
  9.1 0.0 all-gather.2.cloned.1.call-update
  9.1 0.0 reduce-scatter.2.cloned.1.call-start
  9.1 31.3 %shard_map.65 = bf16[4,4,64,1536]{3,2,1,0:T(8,128)(2,1)} custom-call(bf16[64,1536]{1,0:T(8,128)(2,1)} %bitcast.15), custom_call_target="tpu_custom_call" | custom-call | bytes 6291456 | tf_op jit(solution)/shard_map/pallas_call | solution.py:122
  40.5 13.0 %shard_map.66 = f32[8,64,1536]{2,1,0:T(8,128)} custom-call(bf16[8,2,64,1536]{3,2,1,0:T(8,128)(2,1)} %bitcast.14, bf16[1536,1536]{1,0:T(8,128)(2,1)} %ints_ref.3), custom_call_target="tpu_custom_call" | custom-call | flops 4831838208 | bytes 11010048 | tf_op jit(solution)/shard_map/pallas_call | solution.py:301
  53.5 0.0 copy-start.1
  53.5 0.0 copy-start
  53.5 0.0 copy-start.2
  53.5 0.0 reduce-scatter.2.cloned.1.call-update
  53.5 0.6 copy-done.1
  54.1 0.1 dynamic_slice.6
  54.2 0.0 copy-done
  54.2 0.1 dynamic_slice.7
  54.3 0.0 copy-done.2
  54.3 0.2 select_reduce_fusion
  54.5 0.1 broadcast_add_fusion
  54.5 0.1 broadcast_subtract_fusion.1
  54.6 0.1 broadcast_subtract_fusion
  54.7 0.2 all-gather.2.cloned.1.call-done
  54.9 54.3 %shard_map.64 = f32[96,8,128]{2,1,0:T(8,128)} custom-call(bf16[4,4,96,1024]{3,2,1,0:T(8,128)(2,1)} %bitcast.17, bf16[1024,1024]{1,0:T(8,128)(2,1)} %ints_ref.2), custom_call_target="tpu_custom_call" | custom-call | flops 3221225472 | bytes 5636096 | tf_op jit(solution)/shard_map/pallas_call | solution.py:230
  109.2 0.0 reduce-scatter.2.cloned.1.call-done
  109.2 1.9 %fusion = f32[8,12,8,128]{3,2,1,0:T(8,128)} fusion(f32[8,12,8,128]{3,2,1,0:T(8,128)S(1)} %broadcast_subtract_fusion, f32[8,12,8,128]{3,2,1,0:T(8,128)} %bitcast.16, f32[1,64,1536]{2,1,0:T(8,128)} %reduce-scatter.2.cloned.1.call-done), kind=kLoop, calls=%fused_computation.1 | loop fusion | flops 196608 | bytes 1572864 | tf_op jit(solution)/shard_map/div | solution.py:362
Async XLA Ops:
  7.4 47.5 %all-gather.2.cloned.1.call-start = ((), (), s32[]{:S(2)}) async-start(), calls=%async_computation.1 | async-start | bytes 3342336 | tf_op jit(solution)/shard_map/all_gather | solution.py:343
  9.1 100.1 %reduce-scatter.2.cloned.1.call-start = ((), (), s32[]{:S(2)}) async-start(), calls=%async_computation.2 | async-start | bytes 3538944 | tf_op jit(solution)/shard_map/reduce_scatter | solution.py:336
  53.5 0.7 copy-start.1
  53.5 0.7 copy-start
  53.5 0.8 copy-start.2
Sparse Core Ops, SparseCore 0:
  10.0 44.8 all-gather.1
Sparse Core Ops, SparseCore 1:
  53.6 43.9 reduce-scatter.1

commit v20 on v18

--- a/solution.py
+++ b/solution.py
@@ -340,7 +340,7 @@
 
     rows = slab_rows * occ_local
     flat = amplitudes.reshape(rows, vir_local * virt_width)
-    shard_piece = lax.all_gather(flat, ("z", "core"), axis=0, tiled=False)
+    shard_piece = lax.all_gather(flat, ("z", "core"), axis=0, tiled=True)
     ladder_own = _reduce(shard_piece.reshape(n_x, NY, rows, -1), ladder_ints, n_red, 1)
     ladder_own = ladder_own.reshape(slab_rows, occ_red, -1, virt_width)
 

time: 119 us -> 119 us (level)
    another operation x1 -> x0, local copies, waits for them, and re-layouts: 1.69 us -> none  [shards(): shard_piece = lax.all_gather(flat, ('z', 'core'), axis=0, tiled=False)]
    unnamed x6 -> x7, local copies, waits for them, and re-layouts: 0.61 us -> 2.24 us
where the time goes in v20:
time: 119 us
  Pallas kernels  98.7 us (83%)
  between operations  14.9 us (13%)
  local copies, waits for them, and re-layouts  2.39 us (2%)
  other arithmetic  2.32 us (2%)
    pallas_call x1, Pallas kernels, _reduce(): pl.pallas_call(functools.partial(_reduce_kernel, n_red), out_shape=jax.Sh...  54.4 us
    pallas_call x1, Pallas kernels, _gather(): pl.pallas_call(functools.partial(_gather_kernel, n_red), out_shape=jax.Sh...  31.3 us
    pallas_call x1, Pallas kernels, _core_reduce(): pl.pallas_call(_core_reduce_kernel, out_shape=jax.ShapeDtypeStruct((n_z,...  13 us
  transfers between devices with their start and end apart: 2, of which 1 were waited for; matrix products, arithmetic and copies ran while one was open for 0% of the time, Pallas kernels for 83%

profile of v20, /device:TPU:1, one launch (start us, length us, event | category | flops | bytes accessed | tf_op | source)
XLA Modules:
  0.0 118.7 jit_solution(7862405980256308526)
XLA Ops:
  7.4 0.0 all-gather.2.cloned.1.call-start
  7.4 1.6 %copy.9 = bf16[12,8,8,128]{3,1,2,0:T(8,128)(2,1)} copy(bf16[12,8,8,128]{3,2,1,0:T(8,128)(2,1)} %bitcast.18) | data formatting | bytes 393216
  9.0 0.0 all-gather.2.cloned.1.call-update
  9.0 0.0 reduce-scatter.2.cloned.1.call-start
  9.1 31.3 %shard_map.65 = bf16[4,4,64,1536]{3,2,1,0:T(8,128)(2,1)} custom-call(bf16[64,1536]{1,0:T(8,128)(2,1)} %bitcast.19), custom_call_target="tpu_custom_call" | custom-call | bytes 6291456 | tf_op jit(solution)/shard_map/pallas_call | solution.py:122
  40.4 13.0 %shard_map.66 = f32[8,64,1536]{2,1,0:T(8,128)} custom-call(bf16[8,2,64,1536]{3,2,1,0:T(8,128)(2,1)} %bitcast.17, bf16[1536,1536]{1,0:T(8,128)(2,1)} %ints_ref.3), custom_call_target="tpu_custom_call" | custom-call | flops 4831838208 | bytes 11010048 | tf_op jit(solution)/shard_map/pallas_call | solution.py:301
  53.4 0.0 copy-start.1
  53.5 0.0 copy-start
  53.5 0.0 copy-start.2
  53.5 0.0 reduce-scatter.2.cloned.1.call-update
  53.5 0.6 copy-done.1
  54.1 0.1 dynamic_slice.6
  54.2 0.0 copy-done
  54.2 0.1 dynamic_slice.7
  54.3 0.0 copy-done.2
  54.3 0.2 select_reduce_fusion
  54.4 0.1 broadcast_add_fusion
  54.5 0.1 broadcast_subtract_fusion
  54.6 0.3 all-gather.2.cloned.1.call-done
  54.8 54.4 %shard_map.64 = f32[96,8,128]{2,1,0:T(8,128)} custom-call(bf16[4,4,96,1024]{3,2,1,0:T(8,128)(2,1)} %bitcast.22, bf16[1024,1024]{1,0:T(8,128)(2,1)} %ints_ref.2), custom_call_target="tpu_custom_call" | custom-call | flops 3221225472 | bytes 5636096 | tf_op jit(solution)/shard_map/pallas_call | solution.py:230
  109.2 0.0 reduce-scatter.2.cloned.1.call-done
  109.3 2.0 %fusion = f32[8,12,8,128]{3,2,1,0:T(8,128)} fusion(f32[8,12,8,128]{3,2,1,0:T(8,128)} %bitcast.21, f32[1,64,1536]{2,1,0:T(8,128)} %reduce-scatter.2.cloned.1.call-done, f32[12]{0:T(128)S(1)} %dynamic_slice.7, f32[8,8,128]{2,1,0:T(8,128)S(1)} %broadcast_subtract_fusion), kind=kLoop, calls=%fused_computation.1 | loop fusion | flops 294912 | bytes 1212464 | tf_op jit(solution)/shard_map/div | solution.py:361
Async XLA Ops:
  7.4 47.5 %all-gather.2.cloned.1.call-start = ((), (), s32[]{:S(2)}) async-start(), calls=%async_computation.1 | async-start | bytes 3342336 | tf_op jit(solution)/shard_map/all_gather | solution.py:343
  9.0 100.2 %reduce-scatter.2.cloned.1.call-start = ((), (), s32[]{:S(2)}) async-start(), calls=%async_computation.2 | async-start | bytes 3538944 | tf_op jit(solution)/shard_map/reduce_scatter | solution.py:336
  53.4 0.7 copy-start.1
  53.5 0.7 copy-start
  53.5 0.8 copy-start.2
Sparse Core Ops, SparseCore 0:
  10.0 44.7 all-gather.1
Sparse Core Ops, SparseCore 1:
  53.6 43.7 reduce-scatter.1
